TPU v7x, 32 devices: a whole 2x2x4 slice. The times are simulated.
32 devices in a mesh: groups: 2 (over y), tm: 4 (over z), dp: 2 (over x), width: 2 (over core).
Axes of the slice: x: 2, y: 2, z: 4, core: 2. Of those that a mesh axis runs over, the one named last changes fastest.
Arguments:
- clips: bfloat16 [4, 16, 8, 64, 128], P(('groups', 'dp'), 'tm', 'width'), parts along dimension 0, may hold values from -16.5 to 16.5
- gain: float32 [128], replicated, may hold values from 0.5 to 1.5
- bias: float32 [128], replicated, may hold values from -3 to 3
- weight: bfloat16 [3456, 256], replicated, may hold values from -0.109375 to 0.109375
- cotangent: bfloat16 [4, 16, 8, 64, 256], P(('groups', 'dp'), 'tm', 'width'), parts along dimension 0, may hold values from -6 to 6
Outputs:
- output: bfloat16 [4, 16, 8, 64, 256], P(('groups', 'dp'), 'tm', 'width'), parts along dimension 0
- grad_weight: float32 [6912, 256], P(('groups', 'tm', 'dp'), 'width'), parts along dimension 0
- grad_gain: float32 [256], P('groups'), parts along dimension 0
- grad_bias: float32 [256], P('groups'), parts along dimension 0
There are 2 independent parts, one for each index of `groups`. A program takes and returns all parts, laid end to end along the dimension named above; an argument that names none is the same for every part. Nothing has to cross between parts.
All inputs are finite; a program needn't handle non-finite values.
Results may differ from a plain program's by a relative error of at most 0.0049.
Values may be sent and summed in bfloat16 or wider, within the bound.
No kernel may reach another device: no remote copies, remote signals or barrier semaphores. Data moves between devices by JAX's collectives and lax.ppermute only.
A program may use at most 64 MiB of HBM per device.

v0:
```python
import jax
import jax.numpy as jnp
from jax import lax
from jax.sharding import PartitionSpec as P

GROUPS = 32


def prefix(value, axis, join, neutral):
    count, mine = (lax.axis_size(axis), lax.axis_index(axis))
    pieces = jax.tree.map(lambda part: lax.all_gather(part, axis), value)
    total = jax.tree.map(
        lambda part, zero: jnp.full_like(part, 0) + jnp.asarray(zero, part.dtype), value, neutral
    )

    def lap(position, total):
        longer = join(total, jax.tree.map(lambda part: part[position], pieces))
        return jax.tree.map(lambda new, old: jnp.where(position < mine, new, old), longer, total)

    return lax.fori_loop(0, count - 1, lap, total)


def with_halo(value, sides, width):
    for axis, dim in sides:
        devices, length = (lax.axis_size(axis), value.shape[dim])
        up = [(i, (i + 1) % devices) for i in range(devices - 1)]
        down = [(j, i) for i, j in up]
        last = lax.slice_in_dim(value, length - width, length, axis=dim)
        first = lax.slice_in_dim(value, 0, width, axis=dim)
        before = lax.ppermute(last, axis, up)
        after = lax.ppermute(first, axis, down)
        value = jnp.concatenate([before, value, after], axis=dim)
    return value


def from_behind(value, axis, steps):
    count = lax.axis_size(axis)
    first, last = (max(0, -steps), min(count, count - steps))
    return lax.ppermute(value, axis, [(source, source + steps) for source in range(first, last)])


def add_pair(earlier, later):
    return (earlier[0] + later[0], earlier[1] + later[1])


def body(clips, gain, bias, weight, cotangent):
    frames_in = clips[0]
    frame_count, row_count, col_count, chan_in = frames_in.shape
    chan_out = weight.shape[1]
    per_group = chan_in // GROUPS
    values = frames_in.astype(jnp.float32)
    grouped = values.reshape(frame_count, row_count, col_count, GROUPS, per_group)
    local_first = jnp.sum(grouped, axis=(1, 2, 4))
    local_square = jnp.sum(grouped * grouped, axis=(1, 2, 4))
    total_first, total_square = lax.psum((local_first, local_square), "width")
    zero_row = jnp.zeros((GROUPS,), jnp.float32)
    before_first, before_square = prefix(
        (jnp.sum(total_first, axis=0), jnp.sum(total_square, axis=0)),
        "tm",
        add_pair,
        (zero_row, zero_row),
    )
    first_sum = before_first + jnp.cumsum(total_first, axis=0)
    square_sum = before_square + jnp.cumsum(total_square, axis=0)
    frame_start = (lax.axis_index("tm") * frame_count).astype(jnp.float32)
    count = (frame_start + jnp.arange(frame_count, dtype=jnp.float32) + 1.0) * float(
        row_count * lax.axis_size("width") * col_count * per_group
    )
    mean = first_sum / count[:, None]
    variance = square_sum / count[:, None] - mean * mean
    inverse = lax.rsqrt(variance + 1e-05)
    normed = ((grouped - mean[:, None, None, :, None]) * inverse[:, None, None, :, None]).reshape(
        frame_count, row_count, col_count, chan_in
    )
    act = normed * gain + bias
    sigma = jax.nn.sigmoid(act)
    hidden = (act * sigma).astype(jnp.bfloat16)
    hidden_rows = with_halo(hidden, (("width", 1),), 1)
    earlier = from_behind(hidden_rows[frame_count - 2 :], "tm", 1)
    padded = jnp.pad(
        jnp.concatenate([earlier, hidden_rows], axis=0), ((0, 0), (0, 0), (1, 1), (0, 0))
    )
    pieces = []
    for lag_t in range(3):
        for row_off in range(3):
            for col_off in range(3):
                pieces.append(
                    padded[
                        lag_t : lag_t + frame_count,
                        row_off : row_off + row_count,
                        col_off : col_off + col_count,
                    ].reshape(-1, chan_in)
                )
    patches = jnp.concatenate(pieces, axis=1)
    output = jnp.dot(patches, weight, preferred_element_type=jnp.float32).astype(jnp.bfloat16)
    output = output.reshape(1, frame_count, row_count, col_count, chan_out)
    cot_local = cotangent[0]
    cot_rows = with_halo(cot_local, (("width", 1),), 1)
    later = from_behind(cot_rows[:2], "tm", -1)
    cot_padded = jnp.pad(
        jnp.concatenate([cot_rows, later], axis=0), ((0, 0), (0, 0), (1, 1), (0, 0))
    )
    kernel_taps = weight.reshape(27, chan_in, chan_out)
    grad_hidden = jnp.zeros((frame_count * row_count * col_count, chan_in), jnp.float32)
    for lag_t in range(3):
        for row_off in range(3):
            for col_off in range(3):
                tap_index = (lag_t * 3 + row_off) * 3 + col_off
                window = cot_padded[
                    2 - lag_t : 2 - lag_t + frame_count,
                    2 - row_off : 2 - row_off + row_count,
                    2 - col_off : 2 - col_off + col_count,
                ].reshape(-1, chan_out)
                grad_hidden = grad_hidden + lax.dot_general(
                    window,
                    kernel_taps[tap_index],
                    (((1,), (1,)), ((), ())),
                    preferred_element_type=jnp.float32,
                )
    grad_hidden = grad_hidden.reshape(frame_count, row_count, col_count, chan_in)
    grad_act = grad_hidden * sigma * (1.0 + act * (1.0 - sigma))
    grad_gain, grad_bias = lax.psum(
        (jnp.sum(grad_act * normed, axis=(0, 1, 2)), jnp.sum(grad_act, axis=(0, 1, 2))),
        ("tm", "dp", "width"),
    )
    cot_flat = cot_local.reshape(-1, chan_out)
    partial_rows = lax.psum_scatter(
        lax.dot_general(
            patches, cot_flat, (((0,), (0,)), ((), ())), preferred_element_type=jnp.float32
        ),
        ("tm", "dp"),
        scatter_dimension=0,
        tiled=True,
    )
    grad_weight = lax.psum_scatter(partial_rows, "width", scatter_dimension=1, tiled=True)
    return (output, grad_weight, grad_gain, grad_bias)


def solution(mesh):
    return jax.shard_map(
        body,
        mesh=mesh,
        in_specs=(
            P(("groups", "dp"), "tm", "width", None, None),
            P(),
            P(),
            P(),
            P(("groups", "dp"), "tm", "width", None, None),
        ),
        out_specs=(
            P(("groups", "dp"), "tm", "width", None, None),
            P(("groups", "tm", "dp"), "width"),
            P("groups"),
            P("groups"),
        ),
        check_vma=False,
    )
```

profile of v0, /device:TPU:0, one launch (start us, length us, event | category | flops | bytes accessed | tf_op | source)
XLA Modules:
  0.0 179.6 jit_solution(5625925412675377033)
XLA Ops:
  7.2 1.1 multiply_reduce_fusion.1
  8.3 0.1 reduce_sum.69
  8.4 0.1 reduce_sum.73
  8.6 0.1 reduce_sum.70
  8.7 0.1 reduce_sum.74
  8.8 2.6 %all-reduce.6 = (f32[4,32]{1,0:T(4,128)S(1)}, f32[4,32]{1,0:T(4,128)S(1)}) all-reduce(f32[4,32]{1,0:T(4,128)S(1)} %reduce_sum.70, f32[4,32]{1,0:T(4,128)S(1)} %reduce_sum.74), channel_id=1, replica_groups=mesh['groups'=2,'tm'=4,'dp'=2,'width'=2] {'width'}, use_global_device_ids=true, to_apply=%region_2.0 | all-reduce | flops 256 | bytes 2048 | tf_op jit(solution)/shard_map/psum | solution.py:55
  11.4 1.2 dynamic-slice
  13.3 0.2 dynamic-update-slice
  13.6 0.2 dynamic-update-slice.1
  13.8 13.3 %all-reduce.5 = (f32[128]{0:T(128)S(1)}, f32[128]{0:T(128)S(1)}) all-reduce(f32[128]{0:T(128)S(1)} %dynamic-update-slice, f32[128]{0:T(128)S(1)} %dynamic-update-slice.1), channel_id=2, replica_groups=mesh['groups'=2,'tm'=4,'dp'=2,'width'=2] {'tm'}, use_global_device_ids=true, to_apply=%add.2 | all-reduce | flops 256 | bytes 2048
  27.0 0.1 reshape.401
  27.2 0.1 while.16
  27.5 0.1 mul.86
  27.7 0.1 sub.33
  27.8 1.2 multiply_convert_fusion.1
  29.0 1.3 collective-permute-start.1
  30.3 3.0 %collective-permute-start = (bf16[4,1,64,128]{3,2,1,0:T(8,128)(2,1)S(1)}, bf16[4,1,64,128]{3,2,1,0:T(8,128)(2,1)S(1)}, u32[]{:S(2)}, u32[]{:S(2)}) collective-permute-start(bf16[4,1,64,128]{3,2,1,0:T(8,128)(2,1)S(1)} %get-tuple-element.217), channel_id=1, source_target_pairs={{0,1},{2,3},{4,5},{6,7},{8,9},{10,11},{12,13},{14,15},{16,17},{18,... | collective-permute-start | bytes 196616 | tf_op jit(solution)/shard_map/ppermute | solution.py:30
  33.4 1.0 fusion.41
  34.4 1.3 collective-permute-start.4
  35.7 3.0 %collective-permute-start.3 = (bf16[4,1,64,256]{3,2,1,0:T(8,128)(2,1)S(1)}, bf16[4,1,64,256]{3,2,1,0:T(8,128)(2,1)S(1)}, u32[]{:S(2)}, u32[]{:S(2)}) collective-permute-start(bf16[4,1,64,256]{3,2,1,0:T(8,128)(2,1)S(1)} %get-tuple-element.213), channel_id=1, source_target_pairs={{0,1},{2,3},{4,5},{6,7},{8,9},{10,11},{12,13},{14,15},{16,17},{18,... | collective-permute-start | bytes 393224 | tf_op jit(solution)/shard_map/ppermute | solution.py:30
  38.8 1.3 collective-permute-start.2
  40.2 1.3 collective-permute-start.5
  41.6 2.4 %collective-permute-done.2 = bf16[2,6,64,128]{3,2,1,0:T(8,128)(2,1)S(1)} collective-permute-done((bf16[2,6,64,128]{3,2,1,0:T(8,128)(2,1)S(1)}, bf16[2,6,64,128]{3,2,1,0:T(8,128)(2,1)S(1)}, u32[]{:S(2)}, u32[]{:S(2)}) %collective-permute-start.2) | collective-permute-done | bytes 196640 | tf_op jit(solution)/shard_map/ppermute | solution.py:39
  44.1 0.2 fusion.40
  44.3 0.7 pad_slice_fusion
  45.1 0.7 pad_slice_fusion.1
  47.4 1.0 fusion.7
  48.7 2.9 %copy-done.5 = bf16[1024,3456]{1,0:T(8,128)(2,1)} copy-done((bf16[1024,3456]{1,0:T(8,128)(2,1)}, bf16[1024,3456]{1,0:T(8,128)(2,1)S(1)}, u32[]{:S(2)}) %copy-start.5) | copy-done | bytes 7077912
  51.6 3.9 %fusion.43 = f32[3456,256]{1,0:T(8,128)} fusion(bf16[1024,3456]{1,0:T(8,128)(2,1)S(1)} %constant_dynamic-update-slice_fusion, bf16[1024,256]{1,0:T(8,128)(2,1)S(1)} %bitcast.120), kind=kOutput, calls=%fused_computation.158 | convolution fusion | flops 1811939328 | bytes 11141120 | tf_op jit(solution)/shard_map/dot_general | solution.py:128
  55.6 0.2 reduce-scatter.5.cloned.1.call-start
  55.8 6.3 %convolution_convert_fusion = bf16[1024,256]{1,0:T(8,128)(2,1)} fusion(bf16[1024,3456]{1,0:T(8,128)(2,1)} %copy-done.5, bf16[3456,256]{1,0:T(8,128)(2,1)} %param.10), kind=kOutput, calls=%fused_computation.4 | convolution fusion | flops 1812201472 | bytes 9371648 | tf_op jit(solution)/shard_map/dot_general | solution.py:95
  62.1 0.2 pad_maximum_fusion
  62.3 2.6 %pad_slice_fusion.20 = (bf16[4,4,64,256]{3,2,1,0:T(8,128)(2,1)S(1)}, bf16[4,4,64,256]{3,2,1,0:T(8,128)(2,1)S(1)}, bf16[4,4,64,256]{3,2,1,0:T(8,128)(2,1)S(1)}, b...) fusion(bf16[6,6,64,256]{3,2,1,0:T(8,128)(2,1)S(1)} %pad_maximum, ...), kind=kLoop, calls=%fused_computation.137 | loop fusion | bytes 8519680 | tf_op jit(solution)/shard_map/slice | solution.py:109
  65.0 0.3 fusion.15
  65.2 0.3 fusion.39
  65.5 0.3 fusion.36
  65.8 0.3 convolution_add_fusion.23
  66.1 2.1 %pad_slice_fusion.19 = (bf16[4,4,64,256]{3,2,1,0:T(8,128)(2,1)}, bf16[4,4,64,256]{3,2,1,0:T(8,128)(2,1)S(1)}, bf16[4,4,64,256]{3,2,1,0:T(8,128)(2,1)S(1)}, bf16[...) fusion(bf16[6,6,64,256]{3,2,1,0:T(8,128)(2,1)S(1)} %pad_maximum, ...), kind=kLoop, calls=%fused_computation.136 | loop fusion | bytes 6946816 | tf_op jit(solution)/shard_map/slice | solution.py:109
  68.2 0.3 convolution_add_fusion.22
  68.5 0.3 convolution_add_fusion.21
  68.8 0.3 convolution_add_fusion.20
  69.1 0.3 convolution_add_fusion.19
  69.4 0.3 convolution_add_fusion.18
  69.7 0.3 convolution_add_fusion.17
  70.0 0.3 convolution_add_fusion.16
  70.3 0.3 convolution_add_fusion.15
  70.6 0.3 convolution_add_fusion.14
  71.0 0.3 convolution_add_fusion.13
  71.3 0.3 convolution_add_fusion.12
  71.6 0.3 convolution_add_fusion.11
  71.9 0.3 convolution_add_fusion.10
  72.2 0.3 convolution_add_fusion.9
  72.5 0.3 convolution_add_fusion.8
  72.8 0.3 convolution_add_fusion.7
  73.1 0.3 convolution_add_fusion.6
  73.4 0.3 fusion.3
  73.7 0.3 convolution_add_fusion.4
  74.0 60.9 %reduce-scatter.3.cloned.1.call-done = f32[432,256]{1,0:T(8,128)} async-done(((f32[3456,256]{1,0:T(8,128)}), f32[432,256]{1,0:T(8,128)}) %reduce-scatter.3.cloned.1.call-update) | async-done | bytes 442384 | tf_op jit(solution)/shard_map/reduce_scatter | solution.py:127
  134.9 1.2 fusion.8
  136.1 1.1 convolution_add_fusion.3
  137.2 1.1 convolution_add_fusion.2
  138.4 1.1 convolution_add_fusion.1
  139.5 1.3 fusion.38
  140.8 31.9 %all-reduce.4 = (f32[128]{0:T(128)}, f32[128]{0:T(128)}) all-reduce(f32[128]{0:T(128)S(1)} %get-tuple-element.138, f32[128]{0:T(128)S(1)} %get-tuple-element.137), channel_id=1, replica_groups=mesh['groups'=2,'tm'=4,'dp'=2,'width'=2] {'tm','dp','width'}, use_global_device_ids=true, to_apply=%region_15.16 | all-reduce | flops 256 | bytes 2048 | tf_op jit(solution)/shard_map/psum | solution.py:122
  (72 shorter events, 2.6 us)
Async XLA Ops:
  7.2 33.0 %copy-start = (bf16[1,4,4,64,256]{4,3,2,1,0:T(8,128)(2,1)S(1)}, bf16[1,4,4,64,256]{4,3,2,1,0:T(8,128)(2,1)}, u32[]{:S(2)}) copy-start(bf16[1,4,4,64,256]{4,3,2,1,0:T(8,128)(2,1)} %param.11) | copy-start | bytes 1572868
  7.2 127.7 %reduce-scatter.3.cloned.1.call-start = ((), (), s32[]{:S(2)}) async-start(), calls=%async_computation.2 | async-start | bytes 3981312 | tf_op jit(solution)/shard_map/reduce_scatter | solution.py:127
  29.0 9.7 %collective-permute-start.1 = (bf16[4,1,64,128]{3,2,1,0:T(8,128)(2,1)S(1)}, bf16[4,1,64,128]{3,2,1,0:T(8,128)(2,1)S(1)}, u32[]{:S(2)}, u32[]{:S(2)}) collective-permute-start(bf16[4,1,64,128]{3,2,1,0:T(8,128)(2,1)S(1)} %get-tuple-element.218), channel_id=1, source_target_pairs={{1,0},{3,2},{5,4},{7,6},{9,8},{11,10},{13,12},{15,14},{17,16},{19,... | collective-permute-start | bytes 196616 | tf_op jit(solution)/shard_map/ppermute | solution.py:31
  30.3 8.4 %collective-permute-start = (bf16[4,1,64,128]{3,2,1,0:T(8,128)(2,1)S(1)}, bf16[4,1,64,128]{3,2,1,0:T(8,128)(2,1)S(1)}, u32[]{:S(2)}, u32[]{:S(2)}) collective-permute-start(bf16[4,1,64,128]{3,2,1,0:T(8,128)(2,1)S(1)} %get-tuple-element.217), channel_id=1, source_target_pairs={{0,1},{2,3},{4,5},{6,7},{8,9},{10,11},{12,13},{14,15},{16,17},{18,... | collective-permute-start | bytes 196616 | tf_op jit(solution)/shard_map/ppermute | solution.py:30
  34.4 5.8 %collective-permute-start.4 = (bf16[4,1,64,256]{3,2,1,0:T(8,128)(2,1)S(1)}, bf16[4,1,64,256]{3,2,1,0:T(8,128)(2,1)S(1)}, u32[]{:S(2)}, u32[]{:S(2)}) collective-permute-start(bf16[4,1,64,256]{3,2,1,0:T(8,128)(2,1)S(1)} %get-tuple-element.214), channel_id=1, source_target_pairs={{1,0},{3,2},{5,4},{7,6},{9,8},{11,10},{13,12},{15,14},{17,16},{19,... | collective-permute-start | bytes 393224 | tf_op jit(solution)/shard_map/ppermute | solution.py:31
  35.7 4.5 %collective-permute-start.3 = (bf16[4,1,64,256]{3,2,1,0:T(8,128)(2,1)S(1)}, bf16[4,1,64,256]{3,2,1,0:T(8,128)(2,1)S(1)}, u32[]{:S(2)}, u32[]{:S(2)}) collective-permute-start(bf16[4,1,64,256]{3,2,1,0:T(8,128)(2,1)S(1)} %get-tuple-element.213), channel_id=1, source_target_pairs={{0,1},{2,3},{4,5},{6,7},{8,9},{10,11},{12,13},{14,15},{16,17},{18,... | collective-permute-start | bytes 393224 | tf_op jit(solution)/shard_map/ppermute | solution.py:30
  38.8 5.3 %collective-permute-start.2 = (bf16[2,6,64,128]{3,2,1,0:T(8,128)(2,1)S(1)}, bf16[2,6,64,128]{3,2,1,0:T(8,128)(2,1)S(1)}, u32[]{:S(2)}, u32[]{:S(2)}) collective-permute-start(bf16[2,6,64,128]{3,2,1,0:T(8,128)(2,1)S(1)} %pad_maximum_fusion.7), channel_id=1, source_target_pairs={{0,4},{4,8},{8,12},{1,5},{5,9},{9,13},{2,6},{6,10},{10,14},{3,7},{... | collective-permute-start | bytes 589832 | tf_op jit(solution)/shard_map/ppermute | solution.py:39
  40.2 21.9 %collective-permute-start.5 = (bf16[2,6,64,256]{3,2,1,0:T(8,128)(2,1)S(1)}, bf16[2,6,64,256]{3,2,1,0:T(8,128)(2,1)S(1)}, u32[]{:S(2)}, u32[]{:S(2)}) collective-permute-start(bf16[2,6,64,256]{3,2,1,0:T(8,128)(2,1)S(1)} %pad_maximum_fusion.3), channel_id=1, source_target_pairs={{4,0},{8,4},{12,8},{5,1},{9,5},{13,9},{6,2},{10,6},{14,10},{7,3},{... | collective-permute-start | bytes 1179656 | tf_op jit(solution)/shard_map/ppermute | solution.py:39
  46.4 1.0 copy-start.1
  46.4 1.0 copy-start.6
  46.4 1.0 copy-start.7
  48.7 2.9 %copy-start.5 = (bf16[1024,3456]{1,0:T(8,128)(2,1)}, bf16[1024,3456]{1,0:T(8,128)(2,1)S(1)}, u32[]{:S(2)}) copy-start(bf16[1024,3456]{1,0:T(8,128)(2,1)S(1)} %constant_dynamic-update-slice_fusion) | copy-start | bytes 21233668
  55.6 117.2 %reduce-scatter.5.cloned.1.call-start = ((), (), s32[]{:S(2)}) async-start(), calls=%async_computation.3 | async-start | bytes 663552 | tf_op jit(solution)/shard_map/reduce_scatter | solution.py:135
  62.3 2.7 %copy-start.4 = (bf16[3456,256]{1,0:T(8,128)(2,1)S(1)}, bf16[3456,256]{1,0:T(8,128)(2,1)}, u32[]{:S(2)}) copy-start(bf16[3456,256]{1,0:T(8,128)(2,1)} %param.10) | copy-start | bytes 5308420
  74.0 65.5 %copy-start.2 = (f32[1024,128]{1,0:T(8,128)S(1)}, f32[1024,128]{1,0:T(8,128)}, u32[]{:S(2)}) copy-start(f32[1024,128]{1,0:T(8,128)} %get-tuple-element.220) | copy-start | bytes 1572868
  134.9 3.5 %copy-start.3 = (bf16[4,4,64,256]{3,2,1,0:T(8,128)(2,1)S(1)}, bf16[4,4,64,256]{3,2,1,0:T(8,128)(2,1)}, u32[]{:S(2)}) copy-start(bf16[4,4,64,256]{3,2,1,0:T(8,128)(2,1)} %get-tuple-element.163) | copy-start | bytes 1572868
Sparse Core Ops, SparseCore 0:
  55.7 79.1 reduce-scatter.2
  137.7 7.3 reduce-scatter.4
where the time goes:
time: 180 us
  waiting for transfers between devices  63.3 us (35%)
  blocking collectives  47.8 us (27%)
  matrix products  22.7 us (13%)
  between operations  15.4 us (9%)
  local copies, waits for them, and re-layouts  14.7 us (8%)
  starting transfers between devices  11.5 us (6%)
  other arithmetic  4.15 us (2%)
    reduce_scatter x1, waiting for transfers between devices, body(): lax.psum_scatter(lax.dot_general(patches, cot_flat, (((0,), (0,)), ((), (...  60.9 us
    psum x1, blocking collectives, body(): lax.psum((jnp.sum(grad_act * normed, axis=(0, 1, 2)), jnp.sum(grad_act, a...  31.9 us
    unnamed x1, blocking collectives  13.3 us
    dot_general x27, matrix products, body(): lax.dot_general(window, kernel_taps[tap_index], (((1,), (1,)), ((), ())),...  12.5 us
    dot_general x1, matrix products, body(): jnp.dot(patches, weight, preferred_element_type=jnp.float32)  6.34 us
    unnamed x46, local copies, waits for them, and re-layouts  6.22 us
    ppermute x2, starting transfers between devices, with_halo(): before = lax.ppermute(last, axis, up)  6.07 us
    slice x3, local copies, waits for them, and re-layouts, body(): cot_padded[2 - lag_t:2 - lag_t + frame_count, 2 - row_off:2 - row_off + r...  5.01 us
  transfers between devices with their start and end apart: 8, of which 2 were waited for; matrix products, arithmetic and copies ran while one was open for 19% of the time, Pallas kernels for 0%

commit v1 on v0

v1 whole, which is shorter than its diff:
```python
import functools

import jax
import jax.numpy as jnp
from jax import lax
from jax.experimental import pallas as pl
from jax.experimental.pallas import tpu as pltpu
from jax.sharding import PartitionSpec as P

GROUPS = 32
F32, BF16 = jnp.float32, jnp.bfloat16
VMEM = pl.BlockSpec(memory_space=pltpu.VMEM)
SMEM = pl.BlockSpec(memory_space=pltpu.SMEM)


def call(kernel, out_shape, inputs, scratch=(), flops=0, scalars=0, trans=0):
    outs = jax.tree.leaves(out_shape)
    moved = sum(v.size * v.dtype.itemsize for v in list(inputs) + list(outs))
    return pl.pallas_call(
        kernel,
        out_shape=out_shape,
        in_specs=[SMEM] * scalars + [VMEM] * (len(inputs) - scalars),
        out_specs=jax.tree.map(lambda _: VMEM, out_shape),
        scratch_shapes=list(scratch),
        cost_estimate=pl.CostEstimate(flops=flops, bytes_accessed=moved, transcendentals=trans),
        compiler_params=pltpu.CompilerParams(vmem_limit_bytes=40 << 20),
    )(*inputs)


def group_sum(rows, per_group):
    lane = lax.broadcasted_iota(jnp.int32, rows.shape, 1)
    lanes = rows.shape[1]
    step = 1
    while step < per_group:
        up = pltpu.roll(rows, lanes - step, 1)
        down = pltpu.roll(rows, step, 1)
        rows = rows + jnp.where((lane // step) % 2 == 0, up, down)
        step *= 2
    return rows


def sums_kernel(per_group, x_ref, o_ref):
    frames = x_ref.shape[0]
    firsts, squares = [], []
    for t in range(frames):
        v = x_ref[t].astype(F32)
        firsts.append(jnp.sum(v, axis=0, keepdims=True))
        squares.append(jnp.sum(v * v, axis=0, keepdims=True))
    o_ref[...] = group_sum(jnp.concatenate(firsts + squares, axis=0), per_group)


def frame_stats(place, stats_ref, frames, per_frame):
    devices = stats_ref.shape[0]
    mine = place[0]
    own = stats_ref[0]
    before = jnp.zeros_like(own)
    behind = jnp.zeros_like(own)
    for x in range(1, devices):
        other = jnp.bitwise_xor(mine, x)
        rows = stats_ref[x]
        before = before + jnp.where(other < mine - 1, rows, 0.0)
        behind = behind + jnp.where(other == mine - 1, rows, 0.0)

    def total(rows, at):
        return jnp.sum(rows[at : at + frames], axis=0, keepdims=True)

    first, square = total(before, 0), total(before, frames)
    means, inverses = [], []
    for k in range(2 * frames):
        rows, t = (behind, k) if k < frames else (own, k - frames)
        first = first + rows[t : t + 1]
        square = square + rows[frames + t : frames + t + 1]
        if k < frames - 2:
            continue
        shown = jnp.maximum(mine * frames + k - frames + 1, 1).astype(F32) * per_frame
        mean = first / shown
        variance = square / shown - mean * mean
        means.append(mean)
        inverses.append(lax.rsqrt(variance + 1e-05))
    return means, inverses


def grad_hidden_kernel(place, g_ref, next_ref, edge_ref, w_ref, gp_ref, o_ref, z_ref):
    frames, rows, cols, chan_out = g_ref.shape
    chan_in = o_ref.shape[1]
    core = place[1]
    edge = edge_ref[...]
    zero = jnp.zeros_like(edge)
    gp_ref[:, 0] = jnp.where(core == 0, zero, edge)
    gp_ref[:, rows + 1] = jnp.where(core == 0, edge, zero)
    gp_ref[:frames, 1 : rows + 1] = g_ref[...]
    gp_ref[frames:, 1 : rows + 1] = next_ref[...]
    cells = frames * rows * cols
    for a in range(3):
        for b in range(3):
            tap = a * 3 + b
            window = gp_ref[2 - a : 2 - a + frames, 2 - b : 2 - b + rows].reshape(cells, chan_out)
            part = lax.dot_general(
                window,
                w_ref[tap * 3 * chan_in : (tap + 1) * 3 * chan_in],
                (((1,), (1,)), ((), ())),
                preferred_element_type=F32,
            )
            if tap == 0:
                z_ref[...] = part
            else:
                z_ref[...] += part
    col = lax.broadcasted_iota(jnp.int32, (cells, chan_in), 0) % cols
    left = jnp.where(col == cols - 1, 0.0, pltpu.roll(z_ref[:, :chan_in], cells - 1, 0))
    right = jnp.where(col == 0, 0.0, pltpu.roll(z_ref[:, 2 * chan_in :], 1, 0))
    o_ref[...] = left + z_ref[:, chan_in : 2 * chan_in] + right


def kernel_grad_kernel(per_frame, place, stats_ref, gain_ref, bias_ref, x_ref, gp_ref, keep_ref, send_ref, ht_ref):
    frames, cells, chan_in = x_ref.shape
    rows = gp_ref.shape[1] - 2
    cols = gp_ref.shape[2]
    chan_out = gp_ref.shape[3]
    core = place[1]
    means, inverses = frame_stats(place, stats_ref, frames, per_frame)
    gain, bias = gain_ref[...], bias_ref[...]
    block = 2 * cols
    lane = lax.broadcasted_iota(jnp.int32, (chan_in, block), 1) % cols
    for t in range(frames):
        for half in range(cells // block):
            v = x_ref[t, half * block : (half + 1) * block].astype(F32)
            act = (v - means[2 + t]) * inverses[2 + t] * gain + bias
            hidden = (act * lax.logistic(act)).astype(BF16).astype(F32)
            turned = hidden.T
            at = t * cells + half * block
            earlier = jnp.where(lane == 0, 0.0, pltpu.roll(turned, 1, 1))
            later = jnp.where(lane == cols - 1, 0.0, pltpu.roll(turned, block - 1, 1))
            ht_ref[:chan_in, at : at + block] = earlier.astype(BF16)
            ht_ref[chan_in : 2 * chan_in, at : at + block] = turned.astype(BF16)
            ht_ref[2 * chan_in :, at : at + block] = later.astype(BF16)
    mine = chan_out // 2
    for a in range(3):
        for b in range(3):
            tap = a * 3 + b
            window = gp_ref[2 - a : 2 - a + frames, 2 - b : 2 - b + rows].reshape(frames * cells, chan_out)
            part = jnp.dot(ht_ref[...], window, preferred_element_type=F32)
            at = tap * 3 * chan_in
            low, high = part[:, :mine], part[:, mine:]
            keep_ref[at : at + 3 * chan_in] = jnp.where(core == 0, low, high)
            send_ref[at : at + 3 * chan_in] = jnp.where(core == 0, high, low).astype(BF16)


def gain_kernel(per_frame, place, stats_ref, gain_ref, bias_ref, x_ref, gh_ref, o_ref):
    frames, cells, chan_in = x_ref.shape
    means, inverses = frame_stats(place, stats_ref, frames, per_frame)
    gain, bias = gain_ref[...], bias_ref[...]
    by_gain = jnp.zeros((1, chan_in), F32)
    by_bias = jnp.zeros((1, chan_in), F32)
    for t in range(frames):
        normed = (x_ref[t].astype(F32) - means[2 + t]) * inverses[2 + t]
        act = normed * gain + bias
        sigma = lax.logistic(act)
        grad_act = gh_ref[t * cells : (t + 1) * cells] * sigma * (1.0 + act * (1.0 - sigma))
        by_gain = by_gain + jnp.sum(grad_act * normed, axis=0, keepdims=True)
        by_bias = by_bias + jnp.sum(grad_act, axis=0, keepdims=True)
    o_ref[...] = jnp.concatenate([by_gain, by_bias], axis=0)


def output_kernel(
    per_frame, place, stats_ref, gain_ref, bias_ref, x_ref, prev_ref, edge_ref, w_ref, o_ref, h_ref, acc_ref
):
    frames, rows, cols, chan_in = x_ref.shape
    chan_out = o_ref.shape[1]
    mine, core = place[0], place[1]
    means, inverses = frame_stats(place, stats_ref, frames, per_frame)
    gain, bias = gain_ref[...], bias_ref[...]

    def put(f, r0, count, value, keep):
        act = (value.astype(F32) - means[f]) * inverses[f] * gain + bias
        hidden = act * lax.logistic(act)
        if keep is not None:
            hidden = jnp.where(keep, hidden, 0.0)
        n = count * cols
        col = lax.broadcasted_iota(jnp.int32, (n, chan_in), 0) % cols
        earlier = jnp.where(col == 0, 0.0, pltpu.roll(hidden, 1, 0))
        later = jnp.where(col == cols - 1, 0.0, pltpu.roll(hidden, n - 1, 0))
        for d, piece in enumerate((earlier, hidden, later)):
            h_ref[f, r0 : r0 + count, :, d * chan_in : (d + 1) * chan_in] = piece.astype(BF16).reshape(
                count, cols, chan_in
            )

    for f in range(frames + 2):
        inside = (mine > 0) if f < 2 else None
        value = prev_ref[f] if f < 2 else x_ref[f - 2]
        put(f, 1, rows, value.reshape(rows * cols, chan_in), inside)
        for r0, here in ((0, core == 1), (rows + 1, core == 0)):
            put(f, r0, 1, edge_ref[f], here if inside is None else jnp.logical_and(here, inside))
    cells = frames * rows * cols
    for a in range(3):
        for b in range(3):
            tap = a * 3 + b
            window = h_ref[a : a + frames, b : b + rows].reshape(cells, 3 * chan_in)
            part = jnp.dot(window, w_ref[tap * 3 * chan_in : (tap + 1) * 3 * chan_in], preferred_element_type=F32)
            if tap == 0:
                acc_ref[...] = part
            elif tap < 8:
                acc_ref[...] += part
            else:
                o_ref[...] = (acc_ref[...] + part).astype(BF16)


def bits_of(axis):
    return [1 << k for k in range((lax.axis_size(axis) - 1).bit_length())]


def swap(value, axis, step):
    return lax.ppermute(value, axis, [(i, i ^ step) for i in range(lax.axis_size(axis))])


def gather_xor(value, axis):
    value = value[None]
    for step in bits_of(axis):
        value = jnp.concatenate([value, swap(value, axis, step)], axis=0)
    return value


def all_sum(value, axes):
    for axis in axes:
        for step in bits_of(axis):
            value = value + swap(value, axis, step)
    return value


def halve(value, axis, dims):
    value = jnp.moveaxis(value, dims, 0) if dims else value
    rest = value.shape[1:]
    me = lax.axis_index(axis)
    for step in bits_of(axis):
        value = value.reshape((value.shape[0] // 2, 2) + rest)
        bit = (me // step) % 2
        keep = lax.dynamic_index_in_dim(value, bit, 1, keepdims=False)
        send = lax.dynamic_index_in_dim(value, 1 - bit, 1, keepdims=False)
        value = keep + swap(send.astype(BF16), axis, step).astype(F32)
    return value[0]


def body(clips, gain, bias, weight, cotangent):
    x, g = clips[0], cotangent[0]
    frames, rows, cols, chan_in = x.shape
    chan_out = g.shape[-1]
    per_group = chan_in // GROUPS
    tm, dp, width = (lax.axis_size(name) for name in ("tm", "dp", "width"))
    per_frame = float(rows * width * cols * per_group)
    z, core = lax.axis_index("tm"), lax.axis_index("width")
    place = jnp.stack([z, core]).astype(jnp.int32)
    cells = rows * cols
    shape = jax.ShapeDtypeStruct
    flat = x.reshape(frames, cells, chan_in)
    conv_flops = 2 * frames * cells * 27 * chan_in * chan_out

    sums = call(functools.partial(sums_kernel, per_group), shape((2 * frames, chan_in), F32), [flat])
    sums = sums + swap(sums, "width", 1)
    stats = gather_xor(sums, "tm")

    up = [(i, i + 1) for i in range(tm - 1)]
    down = [(i + 1, i) for i in range(tm - 1)]
    g_next = lax.ppermute(g[:2], "tm", down)
    x_prev = lax.ppermute(x[frames - 2 :], "tm", up)

    def edge_row(value):
        return jnp.where(core == 0, value[:, rows - 1], value[:, 0])

    g_edge = swap(jnp.concatenate([edge_row(g), edge_row(g_next)], axis=0), "width", 1)
    x_edge = swap(jnp.concatenate([edge_row(x_prev), edge_row(x)], axis=0), "width", 1)

    gp, grad_hidden = call(
        grad_hidden_kernel,
        (shape((frames + 2, rows + 2, cols, chan_out), BF16), shape((frames * cells, chan_in), F32)),
        [place, g, g_next, g_edge, weight],
        [pltpu.VMEM((frames * cells, 3 * chan_in), F32)],
        conv_flops,
        1,
    )
    gain_row, bias_row = gain[None], bias[None]
    norm = [place, stats, gain_row, bias_row]
    keep, send = call(
        functools.partial(kernel_grad_kernel, per_frame),
        (shape((27 * chan_in, chan_out // 2), F32), shape((27 * chan_in, chan_out // 2), BF16)),
        norm + [flat, gp],
        [pltpu.VMEM((3 * chan_in, frames * cells), BF16)],
        conv_flops,
        1,
    )
    total = keep + swap(send, "width", 1).astype(F32)
    local = call(
        functools.partial(gain_kernel, per_frame),
        shape((2, chan_in), F32),
        norm + [flat, grad_hidden],
        scalars=1,
    )
    output = call(
        functools.partial(output_kernel, per_frame),
        shape((frames * cells, chan_out), BF16),
        norm + [x, x_prev, x_edge, weight],
        [
            pltpu.VMEM((frames + 2, rows + 2, cols, 3 * chan_in), BF16),
            pltpu.VMEM((frames * cells, chan_out), F32),
        ],
        conv_flops,
        1,
    )
    share = 27 * chan_in // (tm * dp)
    cut = max(share * 11 // 16 // 16 * 16, 1)
    total = total.reshape(tm, dp, share, chan_out // 2)
    one = halve(halve(total[:, :, :cut], "dp", 1), "tm", 0)
    two = halve(halve(total[:, :, cut:], "tm", 0), "dp", 0)
    grad_weight = jnp.concatenate([one, two], axis=0)
    grads = all_sum(local, ("width", "dp", "tm"))
    return (output.reshape(1, frames, rows, cols, chan_out), grad_weight, grads[0], grads[1])


def solution(mesh):
    return jax.shard_map(
        body,
        mesh=mesh,
        in_specs=(
            P(("groups", "dp"), "tm", "width", None, None),
            P(),
            P(),
            P(),
            P(("groups", "dp"), "tm", "width", None, None),
        ),
        out_specs=(
            P(("groups", "dp"), "tm", "width", None, None),
            P(("groups", "tm", "dp"), "width"),
            P("groups"),
            P("groups"),
        ),
        check_vma=False,
    )
```

time: 180 us -> 77.1 us (0.43)
  blocking collectives: 47.8 us -> 0 us
  waiting for transfers between devices: 63.3 us -> 28.7 us
  matrix products: 22.7 us -> 0 us
  between operations: 15.4 us -> 0.93 us
  starting transfers between devices: 11.5 us -> 25 us
  Pallas kernels: 0 us -> 11.6 us
  local copies, waits for them, and re-layouts: 14.7 us -> 7.41 us
    reduce_scatter x2 -> x0, waiting for transfers between devices: 60.9 us -> none  [the longest x1 60.9 us: body(): lax.psum_scatter(lax.dot_general(patches, cot_flat, (((0,), (0,)), ((), (...]
    psum x2 -> x0, blocking collectives: 34.5 us -> none  [the longest x1 31.9 us: body(): lax.psum((jnp.sum(grad_act * normed, axis=(0, 1, 2)), jnp.sum(grad_act, a...]
    ppermute x6 -> x18, waiting for transfers between devices: 2.44 us -> 28.7 us  [the longest x16 25.2 us: swap(): lax.ppermute(value, axis, [(i, i ^ step) for i in range(lax.axis_size(axi...]
    dot_general x29 -> x0, matrix products: 22.7 us -> none  [the longest x27 12.5 us: body(): lax.dot_general(window, kernel_taps[tap_index], (((1,), (1,)), ((), ())),...]
    ppermute x6 -> x18, starting transfers between devices: 11.3 us -> 25 us  [the longest x16 22.3 us: swap(): lax.ppermute(value, axis, [(i, i ^ step) for i in range(lax.axis_size(axi...]
    unnamed x1 -> x0, blocking collectives: 13.3 us -> none
    pallas_call x0 -> x5, Pallas kernels: none -> 11.6 us  [call(): pl.pallas_call(kernel, out_shape=out_shape, in_specs=[SMEM] * scalars + [...]
    slice x8 -> x4, local copies, waits for them, and re-layouts: 7.62 us -> 0.15 us  [the longest x1 0.08 us: body(): one = halve(halve(total[:, :, :cut], 'dp', 1), 'tm', 0)]
  transfers between devices with their start and end apart: 8 -> 18, of which waited for: 2 -> 12; matrix products, arithmetic and copies ran while one was open for 19% -> 5% of each run, Pallas kernels for 0% -> 7%
where the time goes in v1:
time: 77.1 us; the launch traced here: 76.7 us
  waiting for transfers between devices  28.7 us (37%)
  starting transfers between devices  25 us (32%)
  Pallas kernels  11.6 us (15%)
  local copies, waits for them, and re-layouts  7.41 us (10%)
  other arithmetic  3.07 us (4%)
  between operations  0.93 us (1%)
    ppermute x16, waiting for transfers between devices, swap(): lax.ppermute(value, axis, [(i, i ^ step) for i in range(lax.axis_size(axi...  25.2 us
    ppermute x16, starting transfers between devices, swap(): lax.ppermute(value, axis, [(i, i ^ step) for i in range(lax.axis_size(axi...  22.3 us
    pallas_call x5, Pallas kernels, call(): pl.pallas_call(kernel, out_shape=out_shape, in_specs=[SMEM] * scalars + [...  11.6 us
    unnamed x18, local copies, waits for them, and re-layouts  5.66 us
    ppermute x1, waiting for transfers between devices, body(): x_prev = lax.ppermute(x[frames - 2:], 'tm', up)  3.48 us
  transfers between devices with their start and end apart: 18, of which 12 were waited for; matrix products, arithmetic and copies ran while one was open for 5% of the time, Pallas kernels for 7%

profile of v1, /device:TPU:0, one launch (start us, length us, event | category | flops | bytes accessed | tf_op | source)
XLA Modules:
  0.0 76.7 jit_solution(17301948851842386897)
XLA Ops:
  0.6 0.0 copy-start
  0.6 0.9 %copy-done = bf16[1,4,4,64,128]{4,3,2,1,0:T(8,128)(2,1)S(1)} copy-done((bf16[1,4,4,64,128]{4,3,2,1,0:T(8,128)(2,1)S(1)}, bf16[1,4,4,64,128]{4,3,2,1,0:T(8,128)(2,1)}, u32[]{:S(2)}) %copy-start) | copy-done | bytes 262168
  1.6 0.0 copy-start.1
  1.6 0.2 shard_map.84
  1.8 0.0 copy-start.2
  1.8 0.5 collective-permute-start
  2.3 1.1 %copy.38 = bf16[1,4,4,64,256]{4,3,1,2,0:T(8,128)(2,1)S(1)} copy(bf16[1,4,4,64,256]{4,3,2,1,0:T(8,128)(2,1)} %param.9) | data formatting | bytes 1048576 | tf_op args[4]
  3.4 1.3 %collective-permute-start.5 = (bf16[2,4,64,256]{3,2,0,1:T(8,128)(2,1)S(1)}, bf16[2,4,64,256]{3,2,0,1:T(8,128)(2,1)S(1)}, u32[]{:S(2)}, u32[]{:S(2)}) collective-permute-start(bf16[2,4,64,256]{3,2,0,1:T(8,128)(2,1)S(1)} %slice_bitcast_fusion), channel_id=1, source_target_pairs={{4,0},{8,4},{12,8},{5,1},{9,5},{13,9},{6,2},{10,6},{14,10},{7,3},{... | collective-permute-start | bytes 786440 | tf_op jit(solution)/shard_map/ppermute | solution.py:262
  4.7 0.0 collective-permute-done
  4.7 3.3 %collective-permute-start.1 = (f32[1,8,128]{2,1,0:T(8,128)S(1)}, f32[1,8,128]{2,1,0:T(8,128)S(1)}, u32[]{:S(2)}, u32[]{:S(2)}) collective-permute-start(f32[1,8,128]{2,1,0:T(8,128)S(1)} %add_bitcast_fusion.1), channel_id=1, source_target_pairs={{0,4},{4,0},{8,12},{12,8},{1,5},{5,1},{9,13},{13,9},{2,6},{6,2},{1... | collective-permute-start | bytes 12296 | tf_op jit(solution)/shard_map/ppermute | solution.py:212
  8.1 6.9 %collective-permute-done.1 = f32[1,8,128]{2,1,0:T(8,128)S(1)} collective-permute-done((f32[1,8,128]{2,1,0:T(8,128)S(1)}, f32[1,8,128]{2,1,0:T(8,128)S(1)}, u32[]{:S(2)}, u32[]{:S(2)}) %collective-permute-start.1) | collective-permute-done | bytes 4128 | tf_op jit(solution)/shard_map/ppermute | solution.py:212
  14.9 2.7 %collective-permute-start.2 = (f32[2,8,128]{2,1,0:T(8,128)S(1)}, f32[2,8,128]{2,1,0:T(8,128)S(1)}, u32[]{:S(2)}, u32[]{:S(2)}) collective-permute-start(f32[2,8,128]{2,1,0:T(8,128)S(1)} %pad_maximum_fusion.4), channel_id=1, source_target_pairs={{0,8},{4,12},{8,0},{12,4},{1,9},{5,13},{9,1},{13,5},{2,10},{6,14},... | collective-permute-start | bytes 24584 | tf_op jit(solution)/shard_map/ppermute | solution.py:212
  17.7 0.0 collective-permute-done.5
  17.7 0.1 collective-permute-start.6
  17.8 0.1 pad_add_fusion.place
  17.9 0.0 copy-done.1
  17.9 1.6 %collective-permute-done.2 = f32[2,8,128]{2,1,0:T(8,128)S(1)} collective-permute-done((f32[2,8,128]{2,1,0:T(8,128)S(1)}, f32[2,8,128]{2,1,0:T(8,128)S(1)}, u32[]{:S(2)}, u32[]{:S(2)}) %collective-permute-start.2) | collective-permute-done | bytes 8224 | tf_op jit(solution)/shard_map/ppermute | solution.py:212
  19.5 0.0 collective-permute-done.6.edge_ref
  19.5 0.0 copy-done.2
  19.5 0.0 copy-start.5
  19.5 1.5 %copy-done.5 = bf16[3456,256]{1,0:T(8,128)(2,1)S(1)} copy-done((bf16[3456,256]{1,0:T(8,128)(2,1)S(1)}, bf16[3456,256]{1,0:T(8,128)(2,1)}, u32[]{:S(2)}) %copy-start.5) | copy-done | bytes 1769496
  21.0 0.0 copy-start.3
  21.0 0.0 copy-start.4
  21.0 3.2 %shard_map.86 = (bf16[6,6,64,256]{3,2,1,0:T(8,128)(2,1)S(1)}, f32[1024,128]{1,0:T(8,128)S(1)}) custom-call(s32[2]{0:T(128)S(1)} %pad_add_fusion.place, bf16[4,4,64,256]{3,2,1,0:T(8,128)(2,1)S(1)} %bitcast.71, bf16[2,4,64,256]{3,2,1,0:T(8,128)(2,1)S(1)} %copy.24.next_ref, bf16[6,64,256]{2,1,0:T(8,128)(2,1)S(1)} %collective-permute-done.6.edge_ref, ...), custom_call_target="tpu_custom_call" | custom-call | flops 1811939328 | bytes 4456456 | tf_op jit(solution)/shard_map/pallas_call | solution.py:19
  24.2 0.0 copy-done.3
  24.2 0.0 copy-done.4
  24.2 2.8 %shard_map.87 = (f32[3456,128]{1,0:T(8,128)S(1)}, bf16[3456,128]{1,0:T(8,128)(2,1)S(1)}) custom-call(s32[2]{0:T(128)S(1)} %pad_add_fusion.place, f32[4,8,128]{2,1,0:T(8,128)S(1)} %pad_maximum_fusion.3.stats_ref, f32[1,128]{1,0:T(1,128)S(1)} %bitcast.72, f32[1,128]{1,0:T(1,128)S(1)} %bitcast.75, bf16[4,256,128]{2,1,0:T(8,128)(2,1)S(1)} %bitcast.68, ...), custom_call_target="tpu_custom_call" | custom-call | flops 1811939328 | bytes 4113416 | tf_op jit(solution)/shard_map/pallas_call | solution.py:19
  27.0 0.1 collective-permute-start.7
  27.1 1.5 %collective-permute-start.3 = (bf16[2,4,64,128]{3,2,0,1:T(8,128)(2,1)S(1)}, bf16[2,4,64,128]{3,2,0,1:T(8,128)(2,1)S(1)}, u32[]{:S(2)}, u32[]{:S(2)}) collective-permute-start(bf16[2,4,64,128]{3,2,0,1:T(8,128)(2,1)S(1)} %slice_bitcast_fusion.1), channel_id=1, source_target_pairs={{0,4},{4,8},{8,12},{1,5},{5,9},{9,13},{2,6},{6,10},{10,14},{3,7},{... | collective-permute-start | bytes 393224 | tf_op jit(solution)/shard_map/ppermute | solution.py:263
  28.6 3.5 %collective-permute-done.3 = bf16[2,4,64,128]{3,2,0,1:T(8,128)(2,1)S(1)} collective-permute-done((bf16[2,4,64,128]{3,2,0,1:T(8,128)(2,1)S(1)}, bf16[2,4,64,128]{3,2,0,1:T(8,128)(2,1)S(1)}, u32[]{:S(2)}, u32[]{:S(2)}) %collective-permute-start.3) | collective-permute-done | bytes 131104 | tf_op jit(solution)/shard_map/ppermute | solution.py:263
  32.1 0.7 copy-done.7
  32.8 0.7 pad_maximum_fusion.2
  33.4 0.0 collective-permute-start.4
  33.4 0.9 %shard_map.88 = f32[2,128]{1,0:T(2,128)S(1)} custom-call(s32[2]{0:T(128)S(1)} %pad_add_fusion.place, f32[4,8,128]{2,1,0:T(8,128)S(1)} %pad_maximum_fusion.3.stats_ref, f32[1,128]{1,0:T(1,128)S(1)} %bitcast.73, f32[1,128]{1,0:T(1,128)S(1)} %bitcast.76, bf16[4,256,128]{2,1,0:T(8,128)(2,1)S(1)} %bitcast.69, f32[1024,128]{1,0:T(8,128)S(1)} %get-tuple-element.11.gh_ref), custom_call_target="tpu_custom_call" | custom-call | bytes 804872 | tf_op jit(solution)/shard_map/pallas_call | solution.py:19
  34.3 0.6 collective-permute-start.14
  34.9 0.8 %collective-permute-done.14 = f32[2,128]{1,0:T(2,128)S(1)} collective-permute-done((f32[2,128]{1,0:T(2,128)S(1)}, f32[2,128]{1,0:T(2,128)S(1)}, u32[]{:S(2)}, u32[]{:S(2)}) %collective-permute-start.14) | collective-permute-done | bytes 1056 | tf_op jit(solution)/shard_map/ppermute | solution.py:212
  35.7 1.6 %collective-permute-start.15 = (f32[2,128]{1,0:T(2,128)S(1)}, f32[2,128]{1,0:T(2,128)S(1)}, u32[]{:S(2)}, u32[]{:S(2)}) collective-permute-start(f32[2,128]{1,0:T(2,128)S(1)} %add.102), channel_id=1, source_target_pairs={{0,2},{2,0},{1,3},{3,1},{4,6},{6,4},{5,7},{7,5},{8,10},{10,8},{9,1... | collective-permute-start | bytes 3080 | tf_op jit(solution)/shard_map/ppermute | solution.py:212
  37.3 1.9 %collective-permute-done.15 = f32[2,128]{1,0:T(2,128)S(1)} collective-permute-done((f32[2,128]{1,0:T(2,128)S(1)}, f32[2,128]{1,0:T(2,128)S(1)}, u32[]{:S(2)}, u32[]{:S(2)}) %collective-permute-start.15) | collective-permute-done | bytes 1056 | tf_op jit(solution)/shard_map/ppermute | solution.py:212
  39.2 3.6 %collective-permute-start.16 = (f32[2,128]{1,0:T(2,128)S(1)}, f32[2,128]{1,0:T(2,128)S(1)}, u32[]{:S(2)}, u32[]{:S(2)}) collective-permute-start(f32[2,128]{1,0:T(2,128)S(1)} %add.103), channel_id=1, source_target_pairs={{0,4},{4,0},{8,12},{12,8},{1,5},{5,1},{9,13},{13,9},{2,6},{6,2},{1... | collective-permute-start | bytes 3080 | tf_op jit(solution)/shard_map/ppermute | solution.py:212
  42.9 0.9 %copy.20.prev_ref = bf16[2,4,64,128]{3,2,1,0:T(8,128)(2,1)S(1)} copy(bf16[2,4,64,128]{3,2,0,1:T(8,128)(2,1)} %copy-done.7) | data formatting | bytes 262144 | tf_op jit(solution)/shard_map/ppermute | solution.py:263
  43.8 0.6 collective-permute-done.16
  44.4 3.9 %collective-permute-start.17 = (f32[2,128]{1,0:T(2,128)S(1)}, f32[2,128]{1,0:T(2,128)S(1)}, u32[]{:S(2)}, u32[]{:S(2)}) collective-permute-start(f32[2,128]{1,0:T(2,128)S(1)} %add.104), channel_id=1, source_target_pairs={{0,8},{4,12},{8,0},{12,4},{1,9},{5,13},{9,1},{13,5},{2,10},{6,14},... | collective-permute-start | bytes 3080 | tf_op jit(solution)/shard_map/ppermute | solution.py:212
  48.4 0.0 collective-permute-done.4.edge_ref
  48.4 1.5 %copy-done.6 = bf16[3456,256]{1,0:T(8,128)(2,1)S(1)} copy-done((bf16[3456,256]{1,0:T(8,128)(2,1)S(1)}, bf16[3456,256]{1,0:T(8,128)(2,1)}, u32[]{:S(2)}) %copy-start.6) | copy-done | bytes 1769496
  49.9 4.5 %shard_map.85 = bf16[1024,256]{1,0:T(8,128)(2,1)} custom-call(s32[2]{0:T(128)S(1)} %pad_add_fusion.place, f32[4,8,128]{2,1,0:T(8,128)S(1)} %pad_maximum_fusion.3.stats_ref, f32[1,128]{1,0:T(1,128)S(1)} %bitcast.74, f32[1,128]{1,0:T(1,128)S(1)} %bitcast.77, bf16[4,4,64,128]{3,2,1,0:T(8,128)(2,1)S(1)} %bitcast.70, bf16[2,4,64,128]{3,2,1,0:T(8,128)(2,1)S(1)} %copy.20.prev_ref, ...), custom_call_target="tpu_custom_call" | custom-call | flops 1811939328 | bytes 2802696 | tf_op jit(solution)/shard_map/pallas_call | solution.py:19
  54.4 0.0 collective-permute-done.17
  54.4 0.0 collective-permute-done.7
  54.4 1.4 %convert_add_fusion = f32[3456,128]{1,0:T(8,128)S(1)} fusion(f32[3456,128]{1,0:T(8,128)S(1)} %get-tuple-element.9, bf16[3456,128]{1,0:T(8,128)(2,1)} %collective-permute-done.7), kind=kLoop, calls=%fused_computation | loop fusion | flops 884736 | bytes 4423680 | tf_op jit(solution)/shard_map/add | solution.py:289
  55.9 0.4 collective-permute-start.11
  56.2 0.5 slice_bitcast_fusion.2
  56.8 0.1 slice.74
  56.9 1.6 %collective-permute-start.8 = (bf16[1,4,288,128]{3,2,1,0:T(8,128)(2,1)S(1)}, bf16[1,4,288,128]{3,2,1,0:T(8,128)(2,1)S(1)}, u32[]{:S(2)}, u32[]{:S(2)}) collective-permute-start(bf16[1,4,288,128]{3,2,1,0:T(8,128)(2,1)S(1)} %fusion), channel_id=1, source_target_pairs={{0,2},{2,0},{1,3},{3,1},{4,6},{6,4},{5,7},{7,5},{8,10},{10,8},{9,1... | collective-permute-start | bytes 884744 | tf_op jit(solution)/shard_map/ppermute | solution.py:212
  58.4 2.6 %collective-permute-done.11 = bf16[2,2,144,128]{3,2,1,0:T(8,128)(2,1)S(1)} collective-permute-done((bf16[2,2,144,128]{3,2,1,0:T(8,128)(2,1)S(1)}, bf16[2,2,144,128]{3,2,1,0:T(8,128)(2,1)S(1)}, u32[]{:S(2)}, u32[]{:S(2)}) %collective-permute-start.11) | collective-permute-done | bytes 147488 | tf_op jit(solution)/shard_map/ppermute | solution.py:212
  61.1 0.1 collective-permute-start.12
  61.2 2.5 %collective-permute-done.8 = bf16[1,4,288,128]{3,2,1,0:T(8,128)(2,1)S(1)} collective-permute-done((bf16[1,4,288,128]{3,2,1,0:T(8,128)(2,1)S(1)}, bf16[1,4,288,128]{3,2,1,0:T(8,128)(2,1)S(1)}, u32[]{:S(2)}, u32[]{:S(2)}) %collective-permute-start.8) | collective-permute-done | bytes 294944 | tf_op jit(solution)/shard_map/ppermute | solution.py:212
  63.7 0.1 bitcast_add_fusion
  63.8 2.2 %collective-permute-start.9 = (bf16[2,288,128]{2,1,0:T(8,128)(2,1)S(1)}, bf16[2,288,128]{2,1,0:T(8,128)(2,1)S(1)}, u32[]{:S(2)}, u32[]{:S(2)}) collective-permute-start(bf16[2,288,128]{2,1,0:T(8,128)(2,1)S(1)} %fusion.1), channel_id=1, source_target_pairs={{0,4},{4,0},{8,12},{12,8},{1,5},{5,1},{9,13},{13,9},{2,6},{6,2},{1... | collective-permute-start | bytes 442376 | tf_op jit(solution)/shard_map/ppermute | solution.py:212
  65.9 1.3 %collective-permute-done.12 = bf16[1,2,144,128]{3,2,1,0:T(8,128)(2,1)S(1)} collective-permute-done((bf16[1,2,144,128]{3,2,1,0:T(8,128)(2,1)S(1)}, bf16[1,2,144,128]{3,2,1,0:T(8,128)(2,1)S(1)}, u32[]{:S(2)}, u32[]{:S(2)}) %collective-permute-start.12) | collective-permute-done | bytes 73760 | tf_op jit(solution)/shard_map/ppermute | solution.py:212
  67.3 1.6 %collective-permute-start.13 = (bf16[1,144,128]{2,1,0:T(8,128)(2,1)S(1)}, bf16[1,144,128]{2,1,0:T(8,128)(2,1)S(1)}, u32[]{:S(2)}, u32[]{:S(2)}) collective-permute-start(bf16[1,144,128]{2,1,0:T(8,128)(2,1)S(1)} %fusion.7), channel_id=1, source_target_pairs={{0,2},{2,0},{1,3},{3,1},{4,6},{6,4},{5,7},{7,5},{8,10},{10,8},{9,1... | collective-permute-start | bytes 110600 | tf_op jit(solution)/shard_map/ppermute | solution.py:212
  68.9 1.0 %collective-permute-done.9 = bf16[2,288,128]{2,1,0:T(8,128)(2,1)S(1)} collective-permute-done((bf16[2,288,128]{2,1,0:T(8,128)(2,1)S(1)}, bf16[2,288,128]{2,1,0:T(8,128)(2,1)S(1)}, u32[]{:S(2)}, u32[]{:S(2)}) %collective-permute-start.9) | collective-permute-done | bytes 147488 | tf_op jit(solution)/shard_map/ppermute | solution.py:212
  69.9 0.1 collective-permute-start.10
  70.0 1.3 %collective-permute-done.13 = bf16[1,144,128]{2,1,0:T(8,128)(2,1)S(1)} collective-permute-done((bf16[1,144,128]{2,1,0:T(8,128)(2,1)S(1)}, bf16[1,144,128]{2,1,0:T(8,128)(2,1)S(1)}, u32[]{:S(2)}, u32[]{:S(2)}) %collective-permute-start.13) | collective-permute-done | bytes 36896 | tf_op jit(solution)/shard_map/ppermute | solution.py:212
  71.3 4.7 %collective-permute-done.10 = bf16[1,288,128]{2,1,0:T(8,128)(2,1)S(1)} collective-permute-done((bf16[1,288,128]{2,1,0:T(8,128)(2,1)S(1)}, bf16[1,288,128]{2,1,0:T(8,128)(2,1)S(1)}, u32[]{:S(2)}, u32[]{:S(2)}) %collective-permute-start.10) | collective-permute-done | bytes 73760 | tf_op jit(solution)/shard_map/ppermute | solution.py:212
  76.0 0.7 pad_maximum_fusion
  (30 shorter events, 0.5 us)
Async XLA Ops:
  0.6 1.0 %copy-start = (bf16[1,4,4,64,128]{4,3,2,1,0:T(8,128)(2,1)S(1)}, bf16[1,4,4,64,128]{4,3,2,1,0:T(8,128)(2,1)}, u32[]{:S(2)}) copy-start(bf16[1,4,4,64,128]{4,3,2,1,0:T(8,128)(2,1)} %param.5) | copy-start | bytes 786436
  1.6 16.3 %copy-start.1 = (bf16[1,4,4,64,128]{4,3,2,1,0:T(8,128)(2,1)S(1)}, bf16[1,4,4,64,128]{4,3,2,1,0:T(8,128)(2,1)}, u32[]{:S(2)}) copy-start(bf16[1,4,4,64,128]{4,3,2,1,0:T(8,128)(2,1)} %param.5) | copy-start | bytes 786436
  1.8 17.7 %copy-start.2 = (bf16[1,4,4,64,256]{4,3,2,1,0:T(8,128)(2,1)S(1)}, bf16[1,4,4,64,256]{4,3,2,1,0:T(8,128)(2,1)}, u32[]{:S(2)}) copy-start(bf16[1,4,4,64,256]{4,3,2,1,0:T(8,128)(2,1)} %param.9) | copy-start | bytes 1572868
  1.8 2.9 %collective-permute-start = (f32[8,128]{1,0:T(8,128)S(1)}, f32[8,128]{1,0:T(8,128)S(1)}, u32[]{:S(2)}, u32[]{:S(2)}) collective-permute-start(f32[8,128]{1,0:T(8,128)S(1)} %shard_map.84), channel_id=1, source_target_pairs={{0,1},{1,0},{2,3},{3,2},{4,5},{5,4},{6,7},{7,6},{8,9},{9,8},{10,11... | collective-permute-start | bytes 12296 | tf_op jit(solution)/shard_map/ppermute | solution.py:212
  3.4 14.3 %collective-permute-start.5 = (bf16[2,4,64,256]{3,2,0,1:T(8,128)(2,1)S(1)}, bf16[2,4,64,256]{3,2,0,1:T(8,128)(2,1)S(1)}, u32[]{:S(2)}, u32[]{:S(2)}) collective-permute-start(bf16[2,4,64,256]{3,2,0,1:T(8,128)(2,1)S(1)} %slice_bitcast_fusion), channel_id=1, source_target_pairs={{4,0},{8,4},{12,8},{5,1},{9,5},{13,9},{6,2},{10,6},{14,10},{7,3},{... | collective-permute-start | bytes 786440 | tf_op jit(solution)/shard_map/ppermute | solution.py:262
  4.7 10.2 %collective-permute-start.1 = (f32[1,8,128]{2,1,0:T(8,128)S(1)}, f32[1,8,128]{2,1,0:T(8,128)S(1)}, u32[]{:S(2)}, u32[]{:S(2)}) collective-permute-start(f32[1,8,128]{2,1,0:T(8,128)S(1)} %add_bitcast_fusion.1), channel_id=1, source_target_pairs={{0,4},{4,0},{8,12},{12,8},{1,5},{5,1},{9,13},{13,9},{2,6},{6,2},{1... | collective-permute-start | bytes 12296 | tf_op jit(solution)/shard_map/ppermute | solution.py:212
  14.9 4.5 %collective-permute-start.2 = (f32[2,8,128]{2,1,0:T(8,128)S(1)}, f32[2,8,128]{2,1,0:T(8,128)S(1)}, u32[]{:S(2)}, u32[]{:S(2)}) collective-permute-start(f32[2,8,128]{2,1,0:T(8,128)S(1)} %pad_maximum_fusion.4), channel_id=1, source_target_pairs={{0,8},{4,12},{8,0},{12,4},{1,9},{5,13},{9,1},{13,5},{2,10},{6,14},... | collective-permute-start | bytes 24584 | tf_op jit(solution)/shard_map/ppermute | solution.py:212
  17.7 1.8 %collective-permute-start.6 = (bf16[6,64,256]{2,1,0:T(8,128)(2,1)S(1)}, bf16[6,64,256]{2,1,0:T(8,128)(2,1)S(1)}, u32[]{:S(2)}, u32[]{:S(2)}) collective-permute-start(bf16[6,64,256]{2,1,0:T(8,128)(2,1)S(1)} %pad_maximum_fusion.1), channel_id=1, source_target_pairs={{0,1},{1,0},{2,3},{3,2},{4,5},{5,4},{6,7},{7,6},{8,9},{9,8},{10,11... | collective-permute-start | bytes 589832 | tf_op jit(solution)/shard_map/ppermute | solution.py:212
  19.5 1.5 %copy-start.5 = (bf16[3456,256]{1,0:T(8,128)(2,1)S(1)}, bf16[3456,256]{1,0:T(8,128)(2,1)}, u32[]{:S(2)}) copy-start(bf16[3456,256]{1,0:T(8,128)(2,1)} %w_ref.3) | copy-start | bytes 5308420
  21.0 3.2 %copy-start.3 = (f32[128]{0:T(128)S(1)}, f32[128]{0:T(128)}, u32[]{:S(2)}) copy-start(f32[128]{0:T(128)} %param.6) | copy-start | bytes 1540
  21.0 3.2 %copy-start.4 = (f32[128]{0:T(128)S(1)}, f32[128]{0:T(128)}, u32[]{:S(2)}) copy-start(f32[128]{0:T(128)} %param.7) | copy-start | bytes 1540
  27.0 27.4 %collective-permute-start.7 = (bf16[3456,128]{1,0:T(8,128)(2,1)S(1)}, bf16[3456,128]{1,0:T(8,128)(2,1)}, u32[]{:S(2)}, u32[]{:S(2)}) collective-permute-start(bf16[3456,128]{1,0:T(8,128)(2,1)S(1)} %get-tuple-element.10), channel_id=1, source_target_pairs={{0,1},{1,0},{2,3},{3,2},{4,5},{5,4},{6,7},{7,6},{8,9},{9,8},{10,11... | collective-permute-start | bytes 2654216 | tf_op jit(solution)/shard_map/ppermute | solution.py:212
  27.1 5.0 %collective-permute-start.3 = (bf16[2,4,64,128]{3,2,0,1:T(8,128)(2,1)S(1)}, bf16[2,4,64,128]{3,2,0,1:T(8,128)(2,1)S(1)}, u32[]{:S(2)}, u32[]{:S(2)}) collective-permute-start(bf16[2,4,64,128]{3,2,0,1:T(8,128)(2,1)S(1)} %slice_bitcast_fusion.1), channel_id=1, source_target_pairs={{0,4},{4,8},{8,12},{1,5},{5,9},{9,13},{2,6},{6,10},{10,14},{3,7},{... | collective-permute-start | bytes 393224 | tf_op jit(solution)/shard_map/ppermute | solution.py:263
  32.1 0.7 copy-start.7
  33.4 15.0 %collective-permute-start.4 = (bf16[6,64,128]{2,1,0:T(8,128)(2,1)}, bf16[6,64,128]{2,1,0:T(8,128)(2,1)}, u32[]{:S(2)}, u32[]{:S(2)}) collective-permute-start(bf16[6,64,128]{2,1,0:T(8,128)(2,1)} %pad_maximum_fusion.2), channel_id=1, source_target_pairs={{0,1},{1,0},{2,3},{3,2},{4,5},{5,4},{6,7},{7,6},{8,9},{9,8},{10,11... | collective-permute-start | bytes 294920 | tf_op jit(solution)/shard_map/ppermute | solution.py:212
  34.3 1.4 %collective-permute-start.14 = (f32[2,128]{1,0:T(2,128)S(1)}, f32[2,128]{1,0:T(2,128)S(1)}, u32[]{:S(2)}, u32[]{:S(2)}) collective-permute-start(f32[2,128]{1,0:T(2,128)S(1)} %shard_map.88), channel_id=1, source_target_pairs={{0,1},{1,0},{2,3},{3,2},{4,5},{5,4},{6,7},{7,6},{8,9},{9,8},{10,11... | collective-permute-start | bytes 3080 | tf_op jit(solution)/shard_map/ppermute | solution.py:212
  35.7 3.6 %collective-permute-start.15 = (f32[2,128]{1,0:T(2,128)S(1)}, f32[2,128]{1,0:T(2,128)S(1)}, u32[]{:S(2)}, u32[]{:S(2)}) collective-permute-start(f32[2,128]{1,0:T(2,128)S(1)} %add.102), channel_id=1, source_target_pairs={{0,2},{2,0},{1,3},{3,1},{4,6},{6,4},{5,7},{7,5},{8,10},{10,8},{9,1... | collective-permute-start | bytes 3080 | tf_op jit(solution)/shard_map/ppermute | solution.py:212
  39.2 5.2 %collective-permute-start.16 = (f32[2,128]{1,0:T(2,128)S(1)}, f32[2,128]{1,0:T(2,128)S(1)}, u32[]{:S(2)}, u32[]{:S(2)}) collective-permute-start(f32[2,128]{1,0:T(2,128)S(1)} %add.103), channel_id=1, source_target_pairs={{0,4},{4,0},{8,12},{12,8},{1,5},{5,1},{9,13},{13,9},{2,6},{6,2},{1... | collective-permute-start | bytes 3080 | tf_op jit(solution)/shard_map/ppermute | solution.py:212
  44.4 9.9 %collective-permute-start.17 = (f32[2,128]{1,0:T(2,128)S(1)}, f32[2,128]{1,0:T(2,128)S(1)}, u32[]{:S(2)}, u32[]{:S(2)}) collective-permute-start(f32[2,128]{1,0:T(2,128)S(1)} %add.104), channel_id=1, source_target_pairs={{0,8},{4,12},{8,0},{12,4},{1,9},{5,13},{9,1},{13,5},{2,10},{6,14},... | collective-permute-start | bytes 3080 | tf_op jit(solution)/shard_map/ppermute | solution.py:212
  48.4 1.5 %copy-start.6 = (bf16[3456,256]{1,0:T(8,128)(2,1)S(1)}, bf16[3456,256]{1,0:T(8,128)(2,1)}, u32[]{:S(2)}) copy-start(bf16[3456,256]{1,0:T(8,128)(2,1)} %w_ref.3) | copy-start | bytes 5308420
  55.9 5.2 %collective-permute-start.11 = (bf16[2,2,144,128]{3,2,1,0:T(8,128)(2,1)S(1)}, bf16[2,2,144,128]{3,2,1,0:T(8,128)(2,1)S(1)}, u32[]{:S(2)}, u32[]{:S(2)}) collective-permute-start(bf16[2,2,144,128]{3,2,1,0:T(8,128)(2,1)S(1)} %fusion.2), channel_id=1, source_target_pairs={{0,4},{4,0},{8,12},{12,8},{1,5},{5,1},{9,13},{13,9},{2,6},{6,2},{1... | collective-permute-start | bytes 442376 | tf_op jit(solution)/shard_map/ppermute | solution.py:212
  56.9 6.8 %collective-permute-start.8 = (bf16[1,4,288,128]{3,2,1,0:T(8,128)(2,1)S(1)}, bf16[1,4,288,128]{3,2,1,0:T(8,128)(2,1)S(1)}, u32[]{:S(2)}, u32[]{:S(2)}) collective-permute-start(bf16[1,4,288,128]{3,2,1,0:T(8,128)(2,1)S(1)} %fusion), channel_id=1, source_target_pairs={{0,2},{2,0},{1,3},{3,1},{4,6},{6,4},{5,7},{7,5},{8,10},{10,8},{9,1... | collective-permute-start | bytes 884744 | tf_op jit(solution)/shard_map/ppermute | solution.py:212
  61.1 6.1 %collective-permute-start.12 = (bf16[1,2,144,128]{3,2,1,0:T(8,128)(2,1)S(1)}, bf16[1,2,144,128]{3,2,1,0:T(8,128)(2,1)S(1)}, u32[]{:S(2)}, u32[]{:S(2)}) collective-permute-start(bf16[1,2,144,128]{3,2,1,0:T(8,128)(2,1)S(1)} %dynamic-slice_convert_fusion.1), channel_id=1, source_target_pairs={{0,8},{4,12},{8,0},{12,4},{1,9},{5,13},{9,1},{13,5},{2,10},{6,14},... | collective-permute-start | bytes 221192 | tf_op jit(solution)/shard_map/ppermute | solution.py:212
  63.8 6.1 %collective-permute-start.9 = (bf16[2,288,128]{2,1,0:T(8,128)(2,1)S(1)}, bf16[2,288,128]{2,1,0:T(8,128)(2,1)S(1)}, u32[]{:S(2)}, u32[]{:S(2)}) collective-permute-start(bf16[2,288,128]{2,1,0:T(8,128)(2,1)S(1)} %fusion.1), channel_id=1, source_target_pairs={{0,4},{4,0},{8,12},{12,8},{1,5},{5,1},{9,13},{13,9},{2,6},{6,2},{1... | collective-permute-start | bytes 442376 | tf_op jit(solution)/shard_map/ppermute | solution.py:212
  67.3 4.0 %collective-permute-start.13 = (bf16[1,144,128]{2,1,0:T(8,128)(2,1)S(1)}, bf16[1,144,128]{2,1,0:T(8,128)(2,1)S(1)}, u32[]{:S(2)}, u32[]{:S(2)}) collective-permute-start(bf16[1,144,128]{2,1,0:T(8,128)(2,1)S(1)} %fusion.7), channel_id=1, source_target_pairs={{0,2},{2,0},{1,3},{3,1},{4,6},{6,4},{5,7},{7,5},{8,10},{10,8},{9,1... | collective-permute-start | bytes 110600 | tf_op jit(solution)/shard_map/ppermute | solution.py:212
  69.9 6.1 %collective-permute-start.10 = (bf16[1,288,128]{2,1,0:T(8,128)(2,1)S(1)}, bf16[1,288,128]{2,1,0:T(8,128)(2,1)S(1)}, u32[]{:S(2)}, u32[]{:S(2)}) collective-permute-start(bf16[1,288,128]{2,1,0:T(8,128)(2,1)S(1)} %dynamic-slice_convert_fusion.2), channel_id=1, source_target_pairs={{0,8},{4,12},{8,0},{12,4},{1,9},{5,13},{9,1},{13,5},{2,10},{6,14},... | collective-permute-start | bytes 221192 | tf_op jit(solution)/shard_map/ppermute | solution.py:212

commit v2 on v1

--- a/solution.py
+++ b/solution.py
@@ -11,19 +11,20 @@
 F32, BF16 = jnp.float32, jnp.bfloat16
 VMEM = pl.BlockSpec(memory_space=pltpu.VMEM)
 SMEM = pl.BlockSpec(memory_space=pltpu.SMEM)
-
-
-def call(kernel, out_shape, inputs, scratch=(), flops=0, scalars=0, trans=0):
+ANY = pl.BlockSpec(memory_space=pl.ANY)
+
+
+def call(kernel, out_shape, inputs, scratch=(), flops=0, scalars=0, far=0):
     outs = jax.tree.leaves(out_shape)
     moved = sum(v.size * v.dtype.itemsize for v in list(inputs) + list(outs))
     return pl.pallas_call(
         kernel,
         out_shape=out_shape,
-        in_specs=[SMEM] * scalars + [VMEM] * (len(inputs) - scalars),
+        in_specs=[SMEM] * scalars + [VMEM] * (len(inputs) - scalars - far) + [ANY] * far,
         out_specs=jax.tree.map(lambda _: VMEM, out_shape),
         scratch_shapes=list(scratch),
-        cost_estimate=pl.CostEstimate(flops=flops, bytes_accessed=moved, transcendentals=trans),
-        compiler_params=pltpu.CompilerParams(vmem_limit_bytes=40 << 20),
+        cost_estimate=pl.CostEstimate(flops=flops, bytes_accessed=moved, transcendentals=0),
+        compiler_params=pltpu.CompilerParams(vmem_limit_bytes=16 << 20),
     )(*inputs)
 
 
@@ -80,21 +81,37 @@
     return means, inverses
 
 
-def grad_hidden_kernel(place, g_ref, next_ref, edge_ref, w_ref, gp_ref, o_ref, z_ref):
-    frames, rows, cols, chan_out = g_ref.shape
-    chan_in = o_ref.shape[1]
-    core = place[1]
+def pad_cotangent(core, g_ref, next_ref, edge_ref, gp_ref):
+    frames, rows = g_ref.shape[:2]
     edge = edge_ref[...]
     zero = jnp.zeros_like(edge)
     gp_ref[:, 0] = jnp.where(core == 0, zero, edge)
     gp_ref[:, rows + 1] = jnp.where(core == 0, edge, zero)
     gp_ref[:frames, 1 : rows + 1] = g_ref[...]
     gp_ref[frames:, 1 : rows + 1] = next_ref[...]
+
+
+def tap_copies(w_hbm, w_ref, sems):
+    each = w_hbm.shape[0] // 9
+    return [
+        pltpu.make_async_copy(w_hbm.at[pl.ds(k * each, each)], w_ref.at[pl.ds(k * each, each)], sems.at[k])
+        for k in range(9)
+    ]
+
+
+def grad_hidden_kernel(place, g_ref, next_ref, edge_ref, w_hbm, o_ref, gp_ref, z_ref, w_ref, sems):
+    frames, rows, cols, chan_out = g_ref.shape
+    chan_in = o_ref.shape[1]
+    copies = tap_copies(w_hbm, w_ref, sems)
+    for copy in copies:
+        copy.start()
+    pad_cotangent(place[1], g_ref, next_ref, edge_ref, gp_ref)
     cells = frames * rows * cols
     for a in range(3):
         for b in range(3):
             tap = a * 3 + b
             window = gp_ref[2 - a : 2 - a + frames, 2 - b : 2 - b + rows].reshape(cells, chan_out)
+            copies[tap].wait()
             part = lax.dot_general(
                 window,
                 w_ref[tap * 3 * chan_in : (tap + 1) * 3 * chan_in],
@@ -111,12 +128,11 @@
     o_ref[...] = left + z_ref[:, chan_in : 2 * chan_in] + right
 
 
-def kernel_grad_kernel(per_frame, place, stats_ref, gain_ref, bias_ref, x_ref, gp_ref, keep_ref, send_ref, ht_ref):
+def kernel_grad_kernel(per_frame, place, stats_ref, gain_ref, bias_ref, x_ref, g_ref, next_ref, edge_ref, keep_ref, send_ref, gp_ref, ht_ref):
     frames, cells, chan_in = x_ref.shape
-    rows = gp_ref.shape[1] - 2
-    cols = gp_ref.shape[2]
-    chan_out = gp_ref.shape[3]
+    rows, cols, chan_out = g_ref.shape[1:]
     core = place[1]
+    pad_cotangent(core, g_ref, next_ref, edge_ref, gp_ref)
     means, inverses = frame_stats(place, stats_ref, frames, per_frame)
     gain, bias = gain_ref[...], bias_ref[...]
     block = 2 * cols
@@ -162,10 +178,13 @@
 
 
 def output_kernel(
-    per_frame, place, stats_ref, gain_ref, bias_ref, x_ref, prev_ref, edge_ref, w_ref, o_ref, h_ref, acc_ref
+    per_frame, place, stats_ref, gain_ref, bias_ref, x_ref, prev_ref, edge_ref, w_hbm, o_ref, h_ref, acc_ref, w_ref, sems
 ):
     frames, rows, cols, chan_in = x_ref.shape
     chan_out = o_ref.shape[1]
+    copies = tap_copies(w_hbm, w_ref, sems)
+    for copy in copies:
+        copy.start()
     mine, core = place[0], place[1]
     means, inverses = frame_stats(place, stats_ref, frames, per_frame)
     gain, bias = gain_ref[...], bias_ref[...]
@@ -195,6 +214,7 @@
         for b in range(3):
             tap = a * 3 + b
             window = h_ref[a : a + frames, b : b + rows].reshape(cells, 3 * chan_in)
+            copies[tap].wait()
             part = jnp.dot(window, w_ref[tap * 3 * chan_in : (tap + 1) * 3 * chan_in], preferred_element_type=F32)
             if tap == 0:
                 acc_ref[...] = part
@@ -204,12 +224,31 @@
                 o_ref[...] = (acc_ref[...] + part).astype(BF16)
 
 
+def split_kernel(cut, place, keep_ref, recv_ref, keep1, send1, keep2, send2):
+    tm, dp = keep_ref.shape[:2]
+    z, x = jnp.bitwise_and(place[0], 1), jnp.bitwise_and(place[2], 1)
+    for t in range(tm):
+        for j in range(dp // 2):
+            mine, other = 2 * j + x, 2 * j + 1 - x
+            keep1[t, j] = keep_ref[t, mine, :cut] + recv_ref[t, mine, :cut].astype(F32)
+            send1[t, j] = (keep_ref[t, other, :cut] + recv_ref[t, other, :cut].astype(F32)).astype(BF16)
+    for j in range(tm // 2):
+        for d in range(dp):
+            mine, other = 2 * j + z, 2 * j + 1 - z
+            keep2[j, d] = keep_ref[mine, d, cut:] + recv_ref[mine, d, cut:].astype(F32)
+            send2[j, d] = (keep_ref[other, d, cut:] + recv_ref[other, d, cut:].astype(F32)).astype(BF16)
+
+
 def bits_of(axis):
     return [1 << k for k in range((lax.axis_size(axis) - 1).bit_length())]
 
 
 def swap(value, axis, step):
     return lax.ppermute(value, axis, [(i, i ^ step) for i in range(lax.axis_size(axis))])
+
+
+def after(value, *others):
+    return lax.optimization_barrier((value,) + others)[0]
 
 
 def gather_xor(value, axis):
@@ -219,24 +258,32 @@
     return value
 
 
-def all_sum(value, axes):
-    for axis in axes:
-        for step in bits_of(axis):
-            value = value + swap(value, axis, step)
-    return value
-
-
-def halve(value, axis, dims):
-    value = jnp.moveaxis(value, dims, 0) if dims else value
-    rest = value.shape[1:]
-    me = lax.axis_index(axis)
-    for step in bits_of(axis):
-        value = value.reshape((value.shape[0] // 2, 2) + rest)
-        bit = (me // step) % 2
-        keep = lax.dynamic_index_in_dim(value, bit, 1, keepdims=False)
-        send = lax.dynamic_index_in_dim(value, 1 - bit, 1, keepdims=False)
-        value = keep + swap(send.astype(BF16), axis, step).astype(F32)
-    return value[0]
+def parts_of(value):
+    parts = []
+    for _ in range(2):
+        part = lax.reduce_precision(value, 8, 7)
+        parts.append(part.astype(BF16))
+        value = value - part
+    return parts + [value.astype(BF16)]
+
+
+def with_rider(send, rider, axis, step):
+    lanes = send.shape[-1]
+    load = send.reshape(-1, lanes)
+    extra = jnp.concatenate(parts_of(rider), axis=0)
+    extra = jnp.pad(extra, ((0, -extra.shape[0] % 16), (0, 0)))
+    got = swap(jnp.concatenate([load, extra], axis=0), axis, step)
+    n, k = load.shape[0], rider.shape[0]
+    parts = [got[n + i * k : n + (i + 1) * k].astype(F32) for i in range(3)]
+    return got[:n].reshape(send.shape), rider + ((parts[0] + parts[1]) + parts[2])
+
+
+def parted(value, axis, step):
+    value = value.reshape((value.shape[0] // 2, 2) + value.shape[1:])
+    bit = jnp.minimum(jnp.bitwise_and(lax.axis_index(axis), step), 1)
+    keep = lax.dynamic_index_in_dim(value, bit, 1, keepdims=False)
+    send = lax.dynamic_index_in_dim(value, 1 - bit, 1, keepdims=False)
+    return keep, send.astype(BF16)
 
 
 def body(clips, gain, bias, weight, cotangent):
@@ -247,71 +294,116 @@
     tm, dp, width = (lax.axis_size(name) for name in ("tm", "dp", "width"))
     per_frame = float(rows * width * cols * per_group)
     z, core = lax.axis_index("tm"), lax.axis_index("width")
-    place = jnp.stack([z, core]).astype(jnp.int32)
+    place = jnp.stack([z, core, lax.axis_index("dp")]).astype(jnp.int32)
     cells = rows * cols
     shape = jax.ShapeDtypeStruct
     flat = x.reshape(frames, cells, chan_in)
     conv_flops = 2 * frames * cells * 27 * chan_in * chan_out
 
+    up = [(i, i + 1) for i in range(tm - 1)]
+    down = [(i + 1, i) for i in range(tm - 1)]
+    flat_g = g.reshape(frames, cells, chan_out)
+    g_next = lax.ppermute(flat_g[:2], "tm", down)
+    x_prev = lax.ppermute(flat[frames - 2 :], "tm", up)
     sums = call(functools.partial(sums_kernel, per_group), shape((2 * frames, chan_in), F32), [flat])
     sums = sums + swap(sums, "width", 1)
     stats = gather_xor(sums, "tm")
 
-    up = [(i, i + 1) for i in range(tm - 1)]
-    down = [(i + 1, i) for i in range(tm - 1)]
-    g_next = lax.ppermute(g[:2], "tm", down)
-    x_prev = lax.ppermute(x[frames - 2 :], "tm", up)
-
     def edge_row(value):
-        return jnp.where(core == 0, value[:, rows - 1], value[:, 0])
-
-    g_edge = swap(jnp.concatenate([edge_row(g), edge_row(g_next)], axis=0), "width", 1)
-    x_edge = swap(jnp.concatenate([edge_row(x_prev), edge_row(x)], axis=0), "width", 1)
-
-    gp, grad_hidden = call(
-        grad_hidden_kernel,
-        (shape((frames + 2, rows + 2, cols, chan_out), BF16), shape((frames * cells, chan_in), F32)),
-        [place, g, g_next, g_edge, weight],
-        [pltpu.VMEM((frames * cells, 3 * chan_in), F32)],
+        return jnp.where(core == 0, value[:, cells - cols :], value[:, :cols])
+
+    g_edge = swap(jnp.concatenate([edge_row(flat_g), edge_row(g_next)], axis=0), "width", 1)
+    x_edge = swap(jnp.concatenate([edge_row(x_prev), edge_row(flat)], axis=0), "width", 1)
+    stats, x_prev, x_edge = lax.optimization_barrier((stats, x_prev, x_edge))
+    g_next = g_next.reshape(2, rows, cols, chan_out)
+    x_prev = x_prev.reshape(2, rows, cols, chan_in)
+
+    norm = [place, stats, gain[None], bias[None]]
+    padded = pltpu.VMEM((frames + 2, rows + 2, cols, chan_out), BF16)
+    copied = [pltpu.VMEM(weight.shape, BF16), pltpu.SemaphoreType.DMA((9,))]
+    half = chan_out // 2
+    keep, send = call(
+        functools.partial(kernel_grad_kernel, per_frame),
+        (shape((27 * chan_in, half), F32), shape((27 * chan_in, half), BF16)),
+        norm + [flat, g, g_next, g_edge],
+        [padded, pltpu.VMEM((3 * chan_in, frames * cells), BF16)],
         conv_flops,
         1,
     )
-    gain_row, bias_row = gain[None], bias[None]
-    norm = [place, stats, gain_row, bias_row]
-    keep, send = call(
-        functools.partial(kernel_grad_kernel, per_frame),
-        (shape((27 * chan_in, chan_out // 2), F32), shape((27 * chan_in, chan_out // 2), BF16)),
-        norm + [flat, gp],
-        [pltpu.VMEM((3 * chan_in, frames * cells), BF16)],
+    grad_hidden = call(
+        grad_hidden_kernel,
+        shape((frames * cells, chan_in), F32),
+        [place, g, g_next, after(g_edge, send), weight],
+        [padded, pltpu.VMEM((frames * cells, 3 * chan_in), F32), *copied],
         conv_flops,
         1,
-    )
-    total = keep + swap(send, "width", 1).astype(F32)
+        1,
+    )
+    recv = after(swap(send, "width", 1), grad_hidden)
+    share = 27 * chan_in // (tm * dp)
+    cut = max(share * 11 // 16 // 16 * 16, 1)
+    rest = share - cut
+    whole = (tm, dp, share, half)
+    keep1, send1, keep2, send2 = call(
+        functools.partial(split_kernel, cut),
+        (
+            shape((tm, dp // 2, cut, half), F32),
+            shape((tm, dp // 2, cut, half), BF16),
+            shape((tm // 2, dp, rest, half), F32),
+            shape((tm // 2, dp, rest, half), BF16),
+        ),
+        [place, keep.reshape(whole), recv.reshape(whole)],
+        scalars=1,
+    )
+    recv2 = swap(send2, "tm", 1)
+    recv1 = swap(send1, "dp", 1)
     local = call(
         functools.partial(gain_kernel, per_frame),
         shape((2, chan_in), F32),
-        norm + [flat, grad_hidden],
+        norm + [flat, after(grad_hidden, send1, send2)],
         scalars=1,
     )
+    rider = local + swap(local, "width", 1)
+    two = keep2 + after(recv2, rider).astype(F32)
+    hold = stats
+    for step in bits_of("tm")[1:]:
+        two, send = parted(two, "tm", step)
+        hold = after(hold, send)
+        got, rider = with_rider(send, rider, "tm", step)
+        two = two + got.astype(F32)
     output = call(
         functools.partial(output_kernel, per_frame),
         shape((frames * cells, chan_out), BF16),
-        norm + [x, x_prev, x_edge, weight],
+        [place, hold, gain[None], bias[None], x, x_prev, x_edge, weight],
         [
             pltpu.VMEM((frames + 2, rows + 2, cols, 3 * chan_in), BF16),
             pltpu.VMEM((frames * cells, chan_out), F32),
+            *copied,
         ],
         conv_flops,
         1,
-    )
-    share = 27 * chan_in // (tm * dp)
-    cut = max(share * 11 // 16 // 16 * 16, 1)
-    total = total.reshape(tm, dp, share, chan_out // 2)
-    one = halve(halve(total[:, :, :cut], "dp", 1), "tm", 0)
-    two = halve(halve(total[:, :, cut:], "tm", 0), "dp", 0)
-    grad_weight = jnp.concatenate([one, two], axis=0)
-    grads = all_sum(local, ("width", "dp", "tm"))
-    return (output.reshape(1, frames, rows, cols, chan_out), grad_weight, grads[0], grads[1])
+        1,
+    )
+    two, rider, recv1, output = lax.optimization_barrier((two, rider, recv1, output))
+    one = jnp.moveaxis(keep1 + recv1.astype(F32), 1, 0)
+    for step in bits_of("dp")[1:]:
+        one, send = parted(one, "dp", step)
+        one = one + swap(send, "dp", step).astype(F32)
+    one = one[0]
+    for step in bits_of("tm"):
+        one, send = parted(one, "tm", step)
+        if step == 1:
+            got, rider = with_rider(send, rider, "tm", step)
+        else:
+            got = swap(send, "tm", step)
+        one = one + got.astype(F32)
+    two = two[0]
+    for step in bits_of("dp"):
+        two, send = parted(two, "dp", step)
+        got, rider = with_rider(send, rider, "dp", step)
+        two = two + got.astype(F32)
+    grad_weight = jnp.concatenate([one[0], two[0]], axis=0)
+    return (output.reshape(1, frames, rows, cols, chan_out), grad_weight, rider[0], rider[1])
 
 
 def solution(mesh):

time: 77.1 us -> 67.3 us (0.87)
  waiting for transfers between devices: 28.7 us -> 19.8 us
  Pallas kernels: 11.6 us -> 20.4 us
  starting transfers between devices: 25 us -> 19.3 us
  local copies, waits for them, and re-layouts: 7.41 us -> 3.47 us
    pallas_call x5 -> x6, Pallas kernels: 11.6 us -> 20.4 us  [call(): pl.pallas_call(kernel, out_shape=out_shape, in_specs=[SMEM] * scalars + [...]
    ppermute x16 -> x13, starting transfers between devices: 22.3 us -> 13.6 us  [swap(): lax.ppermute(value, axis, [(i, i ^ step) for i in range(lax.axis_size(axi...]
    ppermute x16 -> x13, waiting for transfers between devices: 25.2 us -> 19.8 us  [swap(): lax.ppermute(value, axis, [(i, i ^ step) for i in range(lax.axis_size(axi...]
    unnamed x18 -> x16, local copies, waits for them, and re-layouts: 5.66 us -> 1.87 us
    ppermute x2, waiting for transfers between devices: 3.49 us -> 0.01 us  [the longest x1 0.01 us: body(): x_prev = lax.ppermute(flat[frames - 2:], 'tm', up)]
    ppermute x2, starting transfers between devices: 2.75 us -> 5.78 us  [the longest x1 4.49 us: body(): x_prev = lax.ppermute(flat[frames - 2:], 'tm', up)]
    select_n x4, other arithmetic: 0.04 us -> 1.9 us  [edge_row(): return jnp.where(core == 0, value[:, cells - cols:], value[:, :cols])]
    add x9 -> x7, other arithmetic: 1.53 us -> 0.16 us  [the longest x1 0.05 us: body(): one = jnp.moveaxis(keep1 + recv1.astype(F32), 1, 0)]
  transfers between devices with their start and end apart: 18 -> 15, of which waited for: 12 -> 6; matrix products, arithmetic and copies ran while one was open for 5% -> 6% of each run, Pallas kernels for 7% -> 24%
where the time goes in v2:
time: 67.3 us; the launch traced here: 67 us
  Pallas kernels  20.4 us (30%)
  waiting for transfers between devices  19.8 us (29%)
  starting transfers between devices  19.3 us (29%)
  local copies, waits for them, and re-layouts  3.47 us (5%)
  other arithmetic  3 us (4%)
  between operations  0.99 us (1%)
    pallas_call x6, Pallas kernels, call(): pl.pallas_call(kernel, out_shape=out_shape, in_specs=[SMEM] * scalars + [...  20.4 us
    ppermute x13, waiting for transfers between devices, swap(): lax.ppermute(value, axis, [(i, i ^ step) for i in range(lax.axis_size(axi...  19.8 us
    ppermute x13, starting transfers between devices, swap(): lax.ppermute(value, axis, [(i, i ^ step) for i in range(lax.axis_size(axi...  13.6 us
    ppermute x1, starting transfers between devices, body(): x_prev = lax.ppermute(flat[frames - 2:], 'tm', up)  4.49 us
    select_n x4, other arithmetic, edge_row(): return jnp.where(core == 0, value[:, cells - cols:], value[:, :cols])  1.9 us
    unnamed x16, local copies, waits for them, and re-layouts  1.87 us
  transfers between devices with their start and end apart: 15, of which 6 were waited for; matrix products, arithmetic and copies ran while one was open for 6% of the time, Pallas kernels for 24%

profile of v2, /device:TPU:0, one launch (start us, length us, event | category | flops | bytes accessed | tf_op | source)
XLA Modules:
  0.0 67.0 jit_solution(17727216886129704999)
XLA Ops:
  0.6 0.0 copy-start.3
  0.6 0.0 copy-start.4
  0.7 0.0 copy-start
  0.7 1.0 %copy-done = bf16[1,4,4,64,128]{4,3,2,1,0:T(8,128)(2,1)S(1)} copy-done((bf16[1,4,4,64,128]{4,3,2,1,0:T(8,128)(2,1)S(1)}, bf16[1,4,4,64,128]{4,3,2,1,0:T(8,128)(2,1)}, u32[]{:S(2)}) %copy-start) | copy-done | bytes 262168
  1.6 0.0 copy-start.1
  1.6 0.0 copy-start.2
  1.6 0.2 shard_map.84
  1.8 0.5 collective-permute-start
  2.3 4.5 %collective-permute-start.3 = (bf16[2,256,128]{2,1,0:T(8,128)(2,1)S(1)}, bf16[2,256,128]{2,1,0:T(8,128)(2,1)S(1)}, u32[]{:S(2)}, u32[]{:S(2)}) collective-permute-start(bf16[2,256,128]{2,1,0:T(8,128)(2,1)S(1)} %bitcast.65), channel_id=1, source_target_pairs={{0,4},{4,8},{8,12},{1,5},{5,9},{9,13},{2,6},{6,10},{10,14},{3,7},{... | collective-permute-start | bytes 393224 | tf_op jit(solution)/shard_map/ppermute | solution.py:307
  6.8 1.0 %slice.84 = bf16[1,2,4,64,256]{4,3,2,1,0:T(8,128)(2,1)S(1)} slice(bf16[1,4,4,64,256]{4,3,2,1,0:T(8,128)(2,1)} %param.9), slice={[0:1], [0:2], [0:4], [0:64], [0:256]} | slice | bytes 524288 | tf_op jit(solution)/shard_map/slice | solution.py:306
  7.8 1.3 %collective-permute-start.5 = (bf16[2,256,256]{2,1,0:T(8,128)(2,1)S(1)}, bf16[2,256,256]{2,1,0:T(8,128)(2,1)S(1)}, u32[]{:S(2)}, u32[]{:S(2)}) collective-permute-start(bf16[2,256,256]{2,1,0:T(8,128)(2,1)S(1)} %bitcast.64), channel_id=1, source_target_pairs={{4,0},{8,4},{12,8},{5,1},{9,5},{13,9},{6,2},{10,6},{14,10},{7,3},{... | collective-permute-start | bytes 786440 | tf_op jit(solution)/shard_map/ppermute | solution.py:306
  9.1 1.0 %slice_select_fusion = bf16[4,64,256]{2,1,0:T(8,128)(2,1)S(1)} fusion(bf16[4,256,256]{2,1,0:T(8,128)(2,1)} %bitcast.46, pred[]{:T(512)S(6)} %eq.2), kind=kLoop, calls=%fused_computation.11 | loop fusion | flops 65536 | bytes 393217 | tf_op jit(solution)/shard_map/jit(_where)/select_n | solution.py:313
  10.1 0.9 %slice_select_fusion.2 = bf16[4,64,128]{2,1,0:T(8,128)(2,1)S(1)} fusion(bf16[4,256,128]{2,1,0:T(8,128)(2,1)} %bitcast.39, pred[]{:T(512)S(6)} %eq.2), kind=kLoop, calls=%fused_computation.17 | loop fusion | flops 32768 | bytes 196609 | tf_op jit(solution)/shard_map/jit(_where)/select_n | solution.py:313
  11.0 0.0 collective-permute-done
  11.0 2.7 %collective-permute-start.1 = (f32[1,8,128]{2,1,0:T(8,128)S(1)}, f32[1,8,128]{2,1,0:T(8,128)S(1)}, u32[]{:S(2)}, u32[]{:S(2)}) collective-permute-start(f32[1,8,128]{2,1,0:T(8,128)S(1)} %add_bitcast_fusion.1), channel_id=1, source_target_pairs={{0,4},{4,0},{8,12},{12,8},{1,5},{5,1},{9,13},{13,9},{2,6},{6,2},{1... | collective-permute-start | bytes 12296 | tf_op jit(solution)/shard_map/ppermute | solution.py:247
  13.7 0.1 pad_add_fusion.place
  13.8 4.4 %collective-permute-done.1 = f32[1,8,128]{2,1,0:T(8,128)S(1)} collective-permute-done((f32[1,8,128]{2,1,0:T(8,128)S(1)}, f32[1,8,128]{2,1,0:T(8,128)S(1)}, u32[]{:S(2)}, u32[]{:S(2)}) %collective-permute-start.1) | collective-permute-done | bytes 4128 | tf_op jit(solution)/shard_map/ppermute | solution.py:247
  18.2 2.7 %collective-permute-start.2 = (f32[2,8,128]{2,1,0:T(8,128)S(1)}, f32[2,8,128]{2,1,0:T(8,128)S(1)}, u32[]{:S(2)}, u32[]{:S(2)}) collective-permute-start(f32[2,8,128]{2,1,0:T(8,128)S(1)} %pad_maximum_fusion.7), channel_id=1, source_target_pairs={{0,8},{4,12},{8,0},{12,4},{1,9},{5,13},{9,1},{13,5},{2,10},{6,14},... | collective-permute-start | bytes 24584 | tf_op jit(solution)/shard_map/ppermute | solution.py:247
  20.9 0.0 collective-permute-done.3
  20.9 0.0 collective-permute-done.5
  20.9 0.1 collective-permute-start.6
  21.0 0.6 collective-permute-start.4
  21.6 1.2 %collective-permute-done.2 = f32[2,8,128]{2,1,0:T(8,128)S(1)} collective-permute-done((f32[2,8,128]{2,1,0:T(8,128)S(1)}, f32[2,8,128]{2,1,0:T(8,128)S(1)}, u32[]{:S(2)}, u32[]{:S(2)}) %collective-permute-start.2) | collective-permute-done | bytes 8224 | tf_op jit(solution)/shard_map/ppermute | solution.py:247
  22.8 0.0 collective-permute-done.4.edge_ref
  22.8 0.0 copy-start.6
  22.8 0.0 collective-permute-done.6.edge_ref
  22.8 0.0 copy-done.3
  22.8 0.0 copy-done.4
  22.8 0.0 copy-done.1
  22.8 0.0 copy-done.2
  22.8 0.0 copy-start.5
  22.8 2.8 %shard_map.85 = (f32[3456,128]{1,0:T(8,128)S(1)}, bf16[3456,128]{1,0:T(8,128)(2,1)S(1)}) custom-call(s32[3]{0:T(128)S(1)} %pad_add_fusion.place, f32[4,8,128]{2,1,0:T(8,128)S(1)} %pad_maximum_fusion.6.stats_ref, f32[1,128]{1,0:T(1,128)S(1)} %bitcast.52, f32[1,128]{1,0:T(1,128)S(1)} %bitcast.55, bf16[4,256,128]{2,1,0:T(8,128)(2,1)S(1)} %bitcast.41, ...), custom_call_target="tpu_custom_call" | custom-call | flops 1811939328 | bytes 3916812 | tf_op jit(solution)/shard_map/pallas_call | solution.py:20
  25.7 0.0 copy-done.6
  25.7 0.2 collective-permute-start.7
  25.8 0.0 copy-done.5
  25.8 6.1 %shard_map.86.gh_ref = f32[1024,128]{1,0:T(8,128)S(1)} custom-call(s32[3]{0:T(128)S(1)} %pad_add_fusion.place, bf16[4,4,64,256]{3,2,1,0:T(8,128)(2,1)S(1)} %bitcast.48, bf16[2,4,64,256]{3,2,1,0:T(8,128)(2,1)S(1)} %bitcast.50, bf16[6,64,256]{2,1,0:T(8,128)(2,1)S(1)} %collective-permute-done.6.edge_ref, bf16[3456,256]{1,0:T(8,128)(2,1)S(1)} %copy-done.5), custom_call_target="tpu_custom_call" | custom-call | flops 1811939328 | bytes 3276812 | tf_op jit(solution)/shard_map/pallas_call | solution.py:20
  32.0 0.0 collective-permute-done.7
  32.0 0.7 %shard_map.87 = (f32[4,1,288,128]{3,2,1,0:T(8,128)S(1)}, bf16[4,1,288,128]{3,2,1,0:T(8,128)(2,1)S(1)}, f32[2,2,144,128]{3,2,1,0:T(8,128)S(1)}, bf16[2,2,144,128]{3,2,1,0:T(8,128)(2,1)S(1)}) custom-call(s32[3]{0:T(128)S(1)} %pad_add_fusion.place, f32[4,2,432,128]{3,2,1,0:T(8,128)S(1)} %bitcast.44, bf16[4,2,432,128]{3,2,1,0:T(8,128)(2,1)S(1)} %bitcast.45), custom_call_target="tpu_custom_call" | custom-call | bytes 3981324 | tf_op jit(solution)/shard_map/pallas_call | solution.py:20
  32.7 0.8 %shard_map.88 = f32[2,128]{1,0:T(2,128)S(1)} custom-call(s32[3]{0:T(128)S(1)} %pad_add_fusion.place, f32[4,8,128]{2,1,0:T(8,128)S(1)} %pad_maximum_fusion.6.stats_ref, f32[1,128]{1,0:T(1,128)S(1)} %bitcast.53, f32[1,128]{1,0:T(1,128)S(1)} %bitcast.56, bf16[4,256,128]{2,1,0:T(8,128)(2,1)S(1)} %bitcast.42, f32[1024,128]{1,0:T(8,128)S(1)} %shard_map.86.gh_ref), custom_call_target="tpu_custom_call" | custom-call | bytes 804876 | tf_op jit(solution)/shard_map/pallas_call | solution.py:20
  33.6 0.5 collective-permute-start.9
  34.0 0.0 collective-permute-start.8
  34.0 1.5 %collective-permute-start.11 = (bf16[4,1,288,128]{3,2,1,0:T(8,128)(2,1)S(1)}, bf16[4,1,288,128]{3,2,1,0:T(8,128)(2,1)S(1)}, u32[]{:S(2)}, u32[]{:S(2)}) collective-permute-start(bf16[4,1,288,128]{3,2,1,0:T(8,128)(2,1)S(1)} %get-tuple-element.29), channel_id=1, source_target_pairs={{0,2},{2,0},{1,3},{3,1},{4,6},{6,4},{5,7},{7,5},{8,10},{10,8},{9,1... | collective-permute-start | bytes 884744 | tf_op jit(solution)/shard_map/ppermute | solution.py:247
  35.5 0.0 collective-permute-done.9
  35.6 4.3 %collective-permute-done.8 = bf16[2,2,144,128]{3,2,1,0:T(8,128)(2,1)S(1)} collective-permute-done((bf16[2,2,144,128]{3,2,1,0:T(8,128)(2,1)S(1)}, bf16[2,2,144,128]{3,2,1,0:T(8,128)(2,1)S(1)}, u32[]{:S(2)}, u32[]{:S(2)}) %collective-permute-start.8) | collective-permute-done | bytes 147488 | tf_op jit(solution)/shard_map/ppermute | solution.py:247
  40.0 2.7 %collective-permute-start.10 = (bf16[304,128]{1,0:T(8,128)(2,1)S(1)}, bf16[304,128]{1,0:T(8,128)(2,1)S(1)}, u32[]{:S(2)}, u32[]{:S(2)}) collective-permute-start(bf16[304,128]{1,0:T(8,128)(2,1)S(1)} %pad_maximum_fusion.4), channel_id=1, source_target_pairs={{0,8},{4,12},{8,0},{12,4},{1,9},{5,13},{9,1},{13,5},{2,10},{6,14},... | collective-permute-start | bytes 233480 | tf_op jit(solution)/shard_map/ppermute | solution.py:247
  42.7 0.0 copy-start.7
  42.7 0.9 %copy-done.7 = bf16[6,64,128]{2,1,0:T(8,128)(2,1)S(1)} copy-done((bf16[6,64,128]{2,1,0:T(8,128)(2,1)S(1)}, bf16[6,64,128]{2,1,0:T(8,128)(2,1)}, u32[]{:S(2)}) %copy-start.7) | copy-done | bytes 98328
  43.6 9.7 %shard_map.89 = bf16[1024,256]{1,0:T(8,128)(2,1)} custom-call(s32[3]{0:T(128)S(1)} %pad_add_fusion.place, f32[4,8,128]{2,1,0:T(8,128)S(1)} %pad_maximum_fusion.6.stats_ref, f32[1,128]{1,0:T(1,128)S(1)} %bitcast.54, f32[1,128]{1,0:T(1,128)S(1)} %bitcast.57, bf16[4,4,64,128]{3,2,1,0:T(8,128)(2,1)S(1)} %bitcast.43, bf16[2,4,64,128]{3,2,1,0:T(8,128)(2,1)S(1)} %bitcast.51, ...), custom_call_target="tpu_custom_call" | custom-call | flops 1811939328 | bytes 2802700 | tf_op jit(solution)/shard_map/pallas_call | solution.py:20
  53.2 0.0 collective-permute-done.10
  53.3 0.0 collective-permute-done.11
  53.3 0.1 convert_add_fusion
  53.5 0.3 collective-permute-start.12
  53.8 4.9 %collective-permute-done.12 = bf16[592,128]{1,0:T(8,128)(2,1)S(1)} collective-permute-done((bf16[592,128]{1,0:T(8,128)(2,1)S(1)}, bf16[592,128]{1,0:T(8,128)(2,1)S(1)}, u32[]{:S(2)}, u32[]{:S(2)}) %collective-permute-start.12) | collective-permute-done | bytes 151584 | tf_op jit(solution)/shard_map/ppermute | solution.py:247
  58.8 1.6 %collective-permute-start.14 = (bf16[160,128]{1,0:T(8,128)(2,1)S(1)}, bf16[160,128]{1,0:T(8,128)(2,1)S(1)}, u32[]{:S(2)}, u32[]{:S(2)}) collective-permute-start(bf16[160,128]{1,0:T(8,128)(2,1)S(1)} %pad_maximum_fusion.5), channel_id=1, source_target_pairs={{0,2},{2,0},{1,3},{3,1},{4,6},{6,4},{5,7},{7,5},{8,10},{10,8},{9,1... | collective-permute-start | bytes 122888 | tf_op jit(solution)/shard_map/ppermute | solution.py:247
  60.4 0.3 collective-permute-start.13
  60.8 2.1 %collective-permute-done.14 = bf16[160,128]{1,0:T(8,128)(2,1)S(1)} collective-permute-done((bf16[160,128]{1,0:T(8,128)(2,1)S(1)}, bf16[160,128]{1,0:T(8,128)(2,1)S(1)}, u32[]{:S(2)}, u32[]{:S(2)}) %collective-permute-start.14) | collective-permute-done | bytes 40992 | tf_op jit(solution)/shard_map/ppermute | solution.py:247
  62.9 0.5 slice_bitcast_fusion
  63.4 2.9 %collective-permute-done.13 = bf16[1,288,128]{2,1,0:T(8,128)(2,1)S(1)} collective-permute-done((bf16[1,288,128]{2,1,0:T(8,128)(2,1)S(1)}, bf16[1,288,128]{2,1,0:T(8,128)(2,1)S(1)}, u32[]{:S(2)}, u32[]{:S(2)}) %collective-permute-start.13) | collective-permute-done | bytes 73760 | tf_op jit(solution)/shard_map/ppermute | solution.py:247
  66.3 0.7 %pad_maximum_fusion = f32[432,128]{1,0:T(8,128)} fusion(f32[144,128]{1,0:T(8,128)S(1)} %bitcast_add_fusion, f32[288,128]{1,0:T(8,128)S(1)} %add_bitcast_fusion), kind=kLoop, calls=%fused_computation.4 | loop fusion | flops 55296 | bytes 442368 | tf_op jit(solution)/shard_map/concatenate | solution.py:405
  (32 shorter events, 0.4 us)
Async XLA Ops:
  0.6 22.1 %copy-start.3 = (f32[128]{0:T(128)S(1)}, f32[128]{0:T(128)}, u32[]{:S(2)}) copy-start(f32[128]{0:T(128)} %param.6) | copy-start | bytes 1540
  0.6 22.1 %copy-start.4 = (f32[128]{0:T(128)S(1)}, f32[128]{0:T(128)}, u32[]{:S(2)}) copy-start(f32[128]{0:T(128)} %param.7) | copy-start | bytes 1540
  0.7 1.0 %copy-start = (bf16[1,4,4,64,128]{4,3,2,1,0:T(8,128)(2,1)S(1)}, bf16[1,4,4,64,128]{4,3,2,1,0:T(8,128)(2,1)}, u32[]{:S(2)}) copy-start(bf16[1,4,4,64,128]{4,3,2,1,0:T(8,128)(2,1)} %param.5) | copy-start | bytes 786436
  1.6 21.2 %copy-start.1 = (bf16[1,4,4,64,128]{4,3,2,1,0:T(8,128)(2,1)S(1)}, bf16[1,4,4,64,128]{4,3,2,1,0:T(8,128)(2,1)}, u32[]{:S(2)}) copy-start(bf16[1,4,4,64,128]{4,3,2,1,0:T(8,128)(2,1)} %param.5) | copy-start | bytes 786436
  1.6 21.2 %copy-start.2 = (bf16[1,4,4,64,256]{4,3,2,1,0:T(8,128)(2,1)S(1)}, bf16[1,4,4,64,256]{4,3,2,1,0:T(8,128)(2,1)}, u32[]{:S(2)}) copy-start(bf16[1,4,4,64,256]{4,3,2,1,0:T(8,128)(2,1)} %param.9) | copy-start | bytes 1572868
  1.8 9.1 %collective-permute-start = (f32[8,128]{1,0:T(8,128)S(1)}, f32[8,128]{1,0:T(8,128)S(1)}, u32[]{:S(2)}, u32[]{:S(2)}) collective-permute-start(f32[8,128]{1,0:T(8,128)S(1)} %shard_map.84), channel_id=1, source_target_pairs={{0,1},{1,0},{2,3},{3,2},{4,5},{5,4},{6,7},{7,6},{8,9},{9,8},{10,11... | collective-permute-start | bytes 12296 | tf_op jit(solution)/shard_map/ppermute | solution.py:247
  2.3 18.5 %collective-permute-start.3 = (bf16[2,256,128]{2,1,0:T(8,128)(2,1)S(1)}, bf16[2,256,128]{2,1,0:T(8,128)(2,1)S(1)}, u32[]{:S(2)}, u32[]{:S(2)}) collective-permute-start(bf16[2,256,128]{2,1,0:T(8,128)(2,1)S(1)} %bitcast.65), channel_id=1, source_target_pairs={{0,4},{4,8},{8,12},{1,5},{5,9},{9,13},{2,6},{6,10},{10,14},{3,7},{... | collective-permute-start | bytes 393224 | tf_op jit(solution)/shard_map/ppermute | solution.py:307
  7.8 13.1 %collective-permute-start.5 = (bf16[2,256,256]{2,1,0:T(8,128)(2,1)S(1)}, bf16[2,256,256]{2,1,0:T(8,128)(2,1)S(1)}, u32[]{:S(2)}, u32[]{:S(2)}) collective-permute-start(bf16[2,256,256]{2,1,0:T(8,128)(2,1)S(1)} %bitcast.64), channel_id=1, source_target_pairs={{4,0},{8,4},{12,8},{5,1},{9,5},{13,9},{6,2},{10,6},{14,10},{7,3},{... | collective-permute-start | bytes 786440 | tf_op jit(solution)/shard_map/ppermute | solution.py:306
  11.0 7.2 %collective-permute-start.1 = (f32[1,8,128]{2,1,0:T(8,128)S(1)}, f32[1,8,128]{2,1,0:T(8,128)S(1)}, u32[]{:S(2)}, u32[]{:S(2)}) collective-permute-start(f32[1,8,128]{2,1,0:T(8,128)S(1)} %add_bitcast_fusion.1), channel_id=1, source_target_pairs={{0,4},{4,0},{8,12},{12,8},{1,5},{5,1},{9,13},{13,9},{2,6},{6,2},{1... | collective-permute-start | bytes 12296 | tf_op jit(solution)/shard_map/ppermute | solution.py:247
  18.2 4.5 %collective-permute-start.2 = (f32[2,8,128]{2,1,0:T(8,128)S(1)}, f32[2,8,128]{2,1,0:T(8,128)S(1)}, u32[]{:S(2)}, u32[]{:S(2)}) collective-permute-start(f32[2,8,128]{2,1,0:T(8,128)S(1)} %pad_maximum_fusion.7), channel_id=1, source_target_pairs={{0,8},{4,12},{8,0},{12,4},{1,9},{5,13},{9,1},{13,5},{2,10},{6,14},... | collective-permute-start | bytes 24584 | tf_op jit(solution)/shard_map/ppermute | solution.py:247
  20.9 1.8 %collective-permute-start.6 = (bf16[6,64,256]{2,1,0:T(8,128)(2,1)S(1)}, bf16[6,64,256]{2,1,0:T(8,128)(2,1)S(1)}, u32[]{:S(2)}, u32[]{:S(2)}) collective-permute-start(bf16[6,64,256]{2,1,0:T(8,128)(2,1)S(1)} %pad_maximum_fusion.1), channel_id=1, source_target_pairs={{0,1},{1,0},{2,3},{3,2},{4,5},{5,4},{6,7},{7,6},{8,9},{9,8},{10,11... | collective-permute-start | bytes 589832 | tf_op jit(solution)/shard_map/ppermute | solution.py:247
  21.0 1.7 %collective-permute-start.4 = (bf16[6,64,128]{2,1,0:T(8,128)(2,1)S(1)}, bf16[6,64,128]{2,1,0:T(8,128)(2,1)S(1)}, u32[]{:S(2)}, u32[]{:S(2)}) collective-permute-start(bf16[6,64,128]{2,1,0:T(8,128)(2,1)S(1)} %pad_maximum_fusion.3), channel_id=1, source_target_pairs={{0,1},{1,0},{2,3},{3,2},{4,5},{5,4},{6,7},{7,6},{8,9},{9,8},{10,11... | collective-permute-start | bytes 294920 | tf_op jit(solution)/shard_map/ppermute | solution.py:247
  22.8 2.9 %copy-start.6 = (bf16[6,64,128]{2,1,0:T(8,128)(2,1)}, bf16[6,64,128]{2,1,0:T(8,128)(2,1)S(1)}, u32[]{:S(2)}) copy-start(bf16[6,64,128]{2,1,0:T(8,128)(2,1)S(1)} %collective-permute-done.4.edge_ref) | copy-start | bytes 294916
  22.8 3.0 %copy-start.5 = (bf16[3456,256]{1,0:T(8,128)(2,1)S(1)}, bf16[3456,256]{1,0:T(8,128)(2,1)}, u32[]{:S(2)}) copy-start(bf16[3456,256]{1,0:T(8,128)(2,1)} %w_hbm.3) | copy-start | bytes 5308420
  25.7 6.3 %collective-permute-start.7 = (bf16[3456,128]{1,0:T(8,128)(2,1)S(1)}, bf16[3456,128]{1,0:T(8,128)(2,1)S(1)}, u32[]{:S(2)}, u32[]{:S(2)}) collective-permute-start(bf16[3456,128]{1,0:T(8,128)(2,1)S(1)} %get-tuple-element.24), channel_id=1, source_target_pairs={{0,1},{1,0},{2,3},{3,2},{4,5},{5,4},{6,7},{7,6},{8,9},{9,8},{10,11... | collective-permute-start | bytes 2654216 | tf_op jit(solution)/shard_map/ppermute | solution.py:247
  33.6 2.0 %collective-permute-start.9 = (f32[2,128]{1,0:T(2,128)S(1)}, f32[2,128]{1,0:T(2,128)S(1)}, u32[]{:S(2)}, u32[]{:S(2)}) collective-permute-start(f32[2,128]{1,0:T(2,128)S(1)} %shard_map.88), channel_id=1, source_target_pairs={{0,1},{1,0},{2,3},{3,2},{4,5},{5,4},{6,7},{7,6},{8,9},{9,8},{10,11... | collective-permute-start | bytes 3080 | tf_op jit(solution)/shard_map/ppermute | solution.py:247
  34.0 5.9 %collective-permute-start.8 = (bf16[2,2,144,128]{3,2,1,0:T(8,128)(2,1)S(1)}, bf16[2,2,144,128]{3,2,1,0:T(8,128)(2,1)S(1)}, u32[]{:S(2)}, u32[]{:S(2)}) collective-permute-start(bf16[2,2,144,128]{3,2,1,0:T(8,128)(2,1)S(1)} %get-tuple-element.28), channel_id=1, source_target_pairs={{0,4},{4,0},{8,12},{12,8},{1,5},{5,1},{9,13},{13,9},{2,6},{6,2},{1... | collective-permute-start | bytes 442376 | tf_op jit(solution)/shard_map/ppermute | solution.py:247
  34.0 19.3 %collective-permute-start.11 = (bf16[4,1,288,128]{3,2,1,0:T(8,128)(2,1)S(1)}, bf16[4,1,288,128]{3,2,1,0:T(8,128)(2,1)S(1)}, u32[]{:S(2)}, u32[]{:S(2)}) collective-permute-start(bf16[4,1,288,128]{3,2,1,0:T(8,128)(2,1)S(1)} %get-tuple-element.29), channel_id=1, source_target_pairs={{0,2},{2,0},{1,3},{3,1},{4,6},{6,4},{5,7},{7,5},{8,10},{10,8},{9,1... | collective-permute-start | bytes 884744 | tf_op jit(solution)/shard_map/ppermute | solution.py:247
  40.0 13.3 %collective-permute-start.10 = (bf16[304,128]{1,0:T(8,128)(2,1)S(1)}, bf16[304,128]{1,0:T(8,128)(2,1)S(1)}, u32[]{:S(2)}, u32[]{:S(2)}) collective-permute-start(bf16[304,128]{1,0:T(8,128)(2,1)S(1)} %pad_maximum_fusion.4), channel_id=1, source_target_pairs={{0,8},{4,12},{8,0},{12,4},{1,9},{5,13},{9,1},{13,5},{2,10},{6,14},... | collective-permute-start | bytes 233480 | tf_op jit(solution)/shard_map/ppermute | solution.py:247
  42.7 0.9 %copy-start.7 = (bf16[6,64,128]{2,1,0:T(8,128)(2,1)S(1)}, bf16[6,64,128]{2,1,0:T(8,128)(2,1)}, u32[]{:S(2)}) copy-start(bf16[6,64,128]{2,1,0:T(8,128)(2,1)} %copy-done.6) | copy-start | bytes 294916
  53.5 5.3 %collective-permute-start.12 = (bf16[592,128]{1,0:T(8,128)(2,1)S(1)}, bf16[592,128]{1,0:T(8,128)(2,1)S(1)}, u32[]{:S(2)}, u32[]{:S(2)}) collective-permute-start(bf16[592,128]{1,0:T(8,128)(2,1)S(1)} %pad_maximum_fusion.2), channel_id=1, source_target_pairs={{0,4},{4,0},{8,12},{12,8},{1,5},{5,1},{9,13},{13,9},{2,6},{6,2},{1... | collective-permute-start | bytes 454664 | tf_op jit(solution)/shard_map/ppermute | solution.py:247
  58.8 4.1 %collective-permute-start.14 = (bf16[160,128]{1,0:T(8,128)(2,1)S(1)}, bf16[160,128]{1,0:T(8,128)(2,1)S(1)}, u32[]{:S(2)}, u32[]{:S(2)}) collective-permute-start(bf16[160,128]{1,0:T(8,128)(2,1)S(1)} %pad_maximum_fusion.5), channel_id=1, source_target_pairs={{0,2},{2,0},{1,3},{3,1},{4,6},{6,4},{5,7},{7,5},{8,10},{10,8},{9,1... | collective-permute-start | bytes 122888 | tf_op jit(solution)/shard_map/ppermute | solution.py:247
  60.4 5.8 %collective-permute-start.13 = (bf16[1,288,128]{2,1,0:T(8,128)(2,1)S(1)}, bf16[1,288,128]{2,1,0:T(8,128)(2,1)S(1)}, u32[]{:S(2)}, u32[]{:S(2)}) collective-permute-start(bf16[1,288,128]{2,1,0:T(8,128)(2,1)S(1)} %dynamic-slice_convert_fusion), channel_id=1, source_target_pairs={{0,8},{4,12},{8,0},{12,4},{1,9},{5,13},{9,1},{13,5},{2,10},{6,14},... | collective-permute-start | bytes 221192 | tf_op jit(solution)/shard_map/ppermute | solution.py:247

commit v3 on v1

v3 whole, which is shorter than its diff:
```python
import functools

import jax
import jax.numpy as jnp
from jax import lax
from jax.experimental import pallas as pl
from jax.experimental.pallas import tpu as pltpu
from jax.sharding import PartitionSpec as P

GROUPS = 32
OTHERS = (2, 3, 1)
F32, BF16 = jnp.float32, jnp.bfloat16
VMEM = pl.BlockSpec(memory_space=pltpu.VMEM)
SMEM = pl.BlockSpec(memory_space=pltpu.SMEM)
HBM = pl.BlockSpec(memory_space=pltpu.HBM)


def call(kernel, out_shape, inputs, scratch=(), flops=0, scalars=0, far=0):
    outs = jax.tree.leaves(out_shape)
    moved = sum(v.size * v.dtype.itemsize for v in list(inputs) + list(outs))
    return pl.pallas_call(
        kernel,
        out_shape=out_shape,
        in_specs=[SMEM] * scalars + [VMEM] * (len(inputs) - scalars - far) + [HBM] * far,
        out_specs=jax.tree.map(lambda _: VMEM, out_shape),
        scratch_shapes=list(scratch),
        cost_estimate=pl.CostEstimate(flops=0, bytes_accessed=moved, transcendentals=0),
        compiler_params=pltpu.CompilerParams(vmem_limit_bytes=16 << 20),
    )(*inputs)


def far(value):
    return pltpu.with_memory_space_constraint(value, pltpu.HBM)


def group_sum(rows, per_group):
    lane = lax.broadcasted_iota(jnp.int32, rows.shape, 1)
    lanes = rows.shape[1]
    step = 1
    while step < per_group:
        up = pltpu.roll(rows, lanes - step, 1)
        down = pltpu.roll(rows, step, 1)
        rows = rows + jnp.where((lane // step) % 2 == 0, up, down)
        step *= 2
    return rows


def prepare_kernel(per_group, place, x_hbm, g_hbm, sums_ref, last_ref, row_ref, x_row_ref, x_ref, sems):
    frames, rows, cols, chan_in = x_ref.shape
    row = jnp.where(place[1] == 0, rows - 1, 0)
    copies = [pltpu.make_async_copy(x_hbm.at[t], x_ref.at[t], sems.at[t]) for t in range(frames)]
    copies += [pltpu.make_async_copy(g_hbm.at[t, row], row_ref.at[t], sems.at[frames + t]) for t in range(frames)]
    for copy in copies:
        copy.start()
    firsts, squares = [], []
    for t in range(frames):
        copies[t].wait()
        v = x_ref[t].reshape(rows * cols, chan_in).astype(F32)
        firsts.append(jnp.sum(v, axis=0, keepdims=True))
        squares.append(jnp.sum(v * v, axis=0, keepdims=True))
        x_row_ref[t] = x_ref[t, row]
    last_ref[...] = x_ref[frames - 2 :]
    sums_ref[...] = group_sum(jnp.concatenate(firsts + squares, axis=0), per_group)
    for copy in copies[frames:]:
        copy.wait()


def edge_kernel(place, first_ref, *rest):
    o_ref = rest[-1]
    row = jnp.where(place[1] == 0, first_ref.shape[1] - 1, 0)
    at = 0
    for ref in (first_ref,) + rest[:-1]:
        for t in range(ref.shape[0]):
            o_ref[at + t] = ref[t, row]
        at += ref.shape[0]


def frame_stats(place, stats_ref, frames, per_frame):
    devices = stats_ref.shape[0] - 1
    mine = place[0]
    own = stats_ref[0]
    before = jnp.zeros_like(own)
    behind = jnp.zeros_like(own)
    for x in range(1, devices):
        other = jnp.bitwise_xor(mine, x)
        rows = stats_ref[x]
        before = before + jnp.where(other < mine - 1, rows, 0.0)
        behind = behind + jnp.where(other == mine - 1, rows, 0.0)

    def total(rows, at):
        return jnp.sum(rows[at : at + frames], axis=0, keepdims=True)

    first, square = total(before, 0), total(before, frames)
    means, inverses = [], []
    for k in range(2 * frames):
        rows, t = (behind, k) if k < frames else (own, k - frames)
        first = first + rows[t : t + 1]
        square = square + rows[frames + t : frames + t + 1]
        if k < frames - 2:
            continue
        shown = jnp.maximum(mine * frames + k - frames + 1, 1).astype(F32) * per_frame
        mean = first / shown
        variance = square / shown - mean * mean
        means.append(mean)
        inverses.append(lax.rsqrt(variance + 1e-05))
    return means, inverses


def pad_rows(core, own, edge, dst):
    rows = own.shape[1]
    zero = jnp.zeros_like(edge)
    dst[:, 0] = jnp.where(core == 0, zero, edge)
    dst[:, rows + 1] = jnp.where(core == 0, edge, zero)
    dst[:, 1 : rows + 1] = own


def by_taps(window, w_ref, tap, chan_in):
    size = 3 * chan_in
    start = tap * size if isinstance(tap, int) else pl.multiple_of(tap * size, size)
    return lax.dot_general(
        window, w_ref[pl.ds(start, size)], (((1,), (1,)), ((), ())), preferred_element_type=F32
    )


def own_grad_kernel(g_ref, w_ref, z_ref, gp_ref):
    frames, rows, cols, chan_out = g_ref.shape
    chan_in = z_ref.shape[3] // 3
    zero = jnp.zeros((frames, cols, chan_out), BF16)
    gp_ref[:, 0] = zero
    gp_ref[:, rows + 1] = zero
    gp_ref[:, 1 : rows + 1] = g_ref[...]
    for a in (2, 1, 0):
        n = frames - 2 + a
        for b in range(3):
            window = gp_ref[2 - a :, 2 - b : 2 - b + rows].reshape(n * rows * cols, chan_out)
            part = by_taps(window, w_ref, a * 3 + b, chan_in).reshape(n, rows, cols, 3 * chan_in)
            if a == 2 and b == 0:
                z_ref[...] = part
            else:
                z_ref[:n] += part


def gain_kernel(
    per_frame, place, stats_ref, x_ref, own_ref, next_ref, edge_ref, edge_next, w_ref, o_ref, gp_ref, z_ref
):
    frames, rows, cols, chan_out = own_ref.shape[:3] + (next_ref.shape[3],)
    chan_in = x_ref.shape[2]
    cells = rows * cols
    core = place[1]
    pad_rows(core, next_ref[...], edge_next[...], gp_ref)
    z_ref[...] = own_ref[...]
    for a in range(2):
        n = 2 - a
        for b in range(3):
            window = gp_ref[:n, 2 - b : 2 - b + rows].reshape(n * cells, chan_out)
            part = by_taps(window, w_ref, a * 3 + b, chan_in).reshape(n, rows, cols, 3 * chan_in)
            z_ref[frames - n :] += part
    row = jnp.where(core == 0, rows - 1, 0)
    tap_row = jnp.where(core == 0, 0, 2)
    for a in range(3):
        n = frames - 2 + a
        window = edge_ref[2 - a : frames].reshape(n * cols, chan_out)
        part = by_taps(window, w_ref, a * 3 + tap_row, chan_in)
        for t in range(n):
            z_ref[t, row] += part[t * cols : (t + 1) * cols]
    means, inverses = frame_stats(place, stats_ref, frames, per_frame)
    affine = stats_ref[stats_ref.shape[0] - 1]
    gain, bias = affine[:1], affine[1:2]
    col = lax.broadcasted_iota(jnp.int32, (cells, chan_in), 0) % cols
    by_gain = jnp.zeros((1, chan_in), F32)
    by_bias = jnp.zeros((1, chan_in), F32)
    for t in range(frames):
        z = z_ref[t].reshape(cells, 3 * chan_in)
        left = jnp.where(col == cols - 1, 0.0, pltpu.roll(z[:, :chan_in], cells - 1, 0))
        right = jnp.where(col == 0, 0.0, pltpu.roll(z[:, 2 * chan_in :], 1, 0))
        grad_hidden = left + z[:, chan_in : 2 * chan_in] + right
        normed = (x_ref[t].astype(F32) - means[2 + t]) * inverses[2 + t]
        act = normed * gain + bias
        sigma = lax.logistic(act)
        grad_act = grad_hidden * sigma * (1.0 + act * (1.0 - sigma))
        by_gain = by_gain + jnp.sum(grad_act * normed, axis=0, keepdims=True)
        by_bias = by_bias + jnp.sum(grad_act, axis=0, keepdims=True)
    o_ref[...] = jnp.concatenate([by_gain, by_bias], axis=0)


def kernel_grad_kernel(
    per_frame, late, skip, place, stats_ref, next_ref, edge_ref, edge_next, x_hbm, g_hbm, *rest
):
    keep_ref, send_ref, ht_ref, gp_ref, x_ref, g_ref, sems = rest
    frames, cells, chan_in = x_ref.shape
    rows, cols, chan_out = g_ref.shape[1:]
    core = place[1]
    copies = [pltpu.make_async_copy(x_hbm.at[t], x_ref.at[t], sems.at[t]) for t in range(frames)]
    copies.append(pltpu.make_async_copy(g_hbm, g_ref, sems.at[frames]))
    for copy in copies:
        copy.start()
    pad_rows(core, next_ref[...], edge_next[...], gp_ref.at[frames:])
    means, inverses = frame_stats(place, stats_ref, frames, per_frame)
    affine = stats_ref[stats_ref.shape[0] - 1]
    gain, bias = affine[:1], affine[1:2]
    block = 2 * cols
    lane = lax.broadcasted_iota(jnp.int32, (chan_in, block), 1) % cols
    for t in range(frames):
        copies[t].wait()
        for half in range(cells // block):
            v = x_ref[t, half * block : (half + 1) * block].astype(F32)
            act = (v - means[2 + t]) * inverses[2 + t] * gain + bias
            hidden = (act * lax.logistic(act)).astype(BF16).astype(F32)
            turned = hidden.T
            at = t * cells + half * block
            earlier = jnp.where(lane == 0, 0.0, pltpu.roll(turned, 1, 1))
            later = jnp.where(lane == cols - 1, 0.0, pltpu.roll(turned, block - 1, 1))
            for d, piece in enumerate((earlier, turned, later)):
                piece = piece.astype(BF16)
                for k in range(chan_in // 16):
                    to = late(d * (chan_in // 16) + k) * 16
                    ht_ref[to : to + 16, at : at + block] = piece[k * 16 : (k + 1) * 16]
    copies[frames].wait()
    pad_rows(core, g_ref[...], edge_ref[...], gp_ref.at[:frames])
    mine = chan_out // 2
    n = 3 * chan_in
    for a in range(3):
        for b in range(3):
            tap = a * 3 + b
            window = gp_ref[2 - a : 2 - a + frames, 2 - b : 2 - b + rows].reshape(frames * cells, chan_out)
            part = jnp.dot(ht_ref[...], window, preferred_element_type=F32)
            low, high = part[:, :mine], part[:, mine:]
            keep = jnp.where(core == 0, low, high)
            send = jnp.where(core == 0, high, low).astype(BF16)
            for begin, end, at in ((0, skip, tap * skip), (skip, n, 9 * skip + tap * (n - skip))):
                if end > begin:
                    keep_ref[at : at + end - begin] = keep[begin:end]
                    send_ref[at : at + end - begin] = send[begin:end]


def output_kernel(
    per_frame, place, stats_ref, x_ref, prev_ref, edge_ref, prev_edge, w_ref, o_ref, h_ref, acc_ref
):
    frames, rows, cols, chan_in = x_ref.shape
    begin, count = 0, frames
    mine, core = place[0], place[1]
    means, inverses = frame_stats(place, stats_ref, frames, per_frame)
    affine = stats_ref[stats_ref.shape[0] - 1]
    gain, bias = affine[:1], affine[1:2]

    def put(f, r0, rows_now, value, keep):
        act = (value.astype(F32) - means[f]) * inverses[f] * gain + bias
        hidden = act * lax.logistic(act)
        if keep is not None:
            hidden = jnp.where(keep, hidden, 0.0)
        n = rows_now * cols
        col = lax.broadcasted_iota(jnp.int32, (n, chan_in), 0) % cols
        earlier = jnp.where(col == 0, 0.0, pltpu.roll(hidden, 1, 0))
        later = jnp.where(col == cols - 1, 0.0, pltpu.roll(hidden, n - 1, 0))
        for d, piece in enumerate((earlier, hidden, later)):
            h_ref[f - begin, r0 : r0 + rows_now, :, d * chan_in : (d + 1) * chan_in] = piece.astype(BF16).reshape(
                rows_now, cols, chan_in
            )

    for f in range(begin, begin + count + 2):
        inside = (mine > 0) if f < 2 else None
        value = prev_ref[f] if f < 2 else x_ref[f - 2]
        put(f, 1, rows, value.reshape(rows * cols, chan_in), inside)
        for r0, here in ((0, core == 1), (rows + 1, core == 0)):
            put(f, r0, 1, prev_edge[f] if f < 2 else edge_ref[f - 2], here if inside is None else jnp.logical_and(here, inside))
    cells = count * rows * cols
    for a in range(3):
        for b in range(3):
            tap = a * 3 + b
            window = h_ref[a : a + count, b : b + rows].reshape(cells, 3 * chan_in)
            part = jnp.dot(window, w_ref[tap * 3 * chan_in : (tap + 1) * 3 * chan_in], preferred_element_type=F32)
            if tap == 0:
                acc_ref[...] = part
            elif tap < 8:
                acc_ref[...] += part
            else:
                o_ref[...] = (acc_ref[...] + part).astype(BF16)


def split_kernel(cut, rest, place, keep_ref, recv_ref, stay1, send1, stay2, *send2):
    tm = len(send2) + 1

    def total(at):
        rows = pl.ds(pl.multiple_of(at, 16), size)
        return keep_ref[rows] + recv_ref[rows].astype(F32)

    size = rest
    stay2[...] = total(place[0] * rest)
    for k, send in zip(OTHERS, send2):
        send[...] = total(jnp.bitwise_xor(place[0], k) * rest).astype(BF16)
    size = cut
    for t in range(tm):
        at = tm * rest + 2 * t * cut
        stay1[t * cut : (t + 1) * cut] = total(at + place[2] * cut)
        send1[t * cut : (t + 1) * cut] = total(at + (1 - place[2]) * cut).astype(BF16)


def put_rider(rider, dst, at):
    parts = []
    for _ in range(3):
        part = rider.astype(BF16)
        rider = rider - part.astype(F32)
        parts.append(part.astype(F32))
    parts.append(jnp.zeros((16 - 3 * rider.shape[0], rider.shape[1]), F32))
    dst[at : at + 16] = jnp.concatenate(parts, axis=0).astype(BF16)


def get_rider(src, at, n):
    rows = src[at : at + 16].astype(F32)
    return (rows[:n] + rows[n : 2 * n]) + rows[2 * n : 3 * n]


def middle_kernel(place, stay1_ref, recv1_ref, stay2_ref, b_ref, c_ref, a_ref, rider_ref, got_ref, *outs):
    stay1, sends, stay2, send2, rider_out = outs[0], outs[1:4], outs[4], outs[5], outs[6]
    rider = rider_ref[...] + got_ref[...]
    rider_out[...] = rider
    n = stay1.shape[0]

    def total(other):
        rows = pl.ds(pl.multiple_of(jnp.bitwise_xor(place[0], other) * n, 16), n)
        return stay1_ref[rows] + recv1_ref[rows].astype(F32)

    stay1[...] = total(0)
    for k, send in zip(OTHERS, sends):
        send[:n] = total(k).astype(BF16)
        put_rider(rider, send, n)
    m = stay2.shape[0]

    def summed(bit):
        rows = pl.ds(pl.multiple_of(bit * m, 16), m)
        first = stay2_ref[rows] + a_ref[rows].astype(F32)
        return first + (b_ref[rows].astype(F32) + c_ref[rows].astype(F32))

    stay2[...] = summed(place[2])
    send2[...] = summed(1 - place[2]).astype(BF16)


def last_kernel(stay1_ref, b_ref, c_ref, a_ref, stay2_ref, recv2_ref, rider_ref, o_ref, gain_ref, bias_ref):
    for k in range(stay2_ref.shape[0] // 16):
        two, one = slice(16 * k, 16 * k + 16), slice(32 * k, 32 * k + 32)
        near = stay1_ref[one] + a_ref[one].astype(F32)
        o_ref[48 * k : 48 * k + 32] = near + (b_ref[one].astype(F32) + c_ref[one].astype(F32))
        o_ref[48 * k + 32 : 48 * k + 48] = stay2_ref[two] + recv2_ref[two].astype(F32)
    n = stay1_ref.shape[0]
    near, b, c = (get_rider(ref, n, 2) for ref in (a_ref, b_ref, c_ref))
    rider = (rider_ref[...] + near) + (b + c)
    gain_ref[...] = rider[:1]
    bias_ref[...] = rider[1:]


def bits_of(axis):
    return [1 << k for k in range((lax.axis_size(axis) - 1).bit_length())]


def swap(value, axis, step):
    return lax.ppermute(value, axis, [(i, i ^ step) for i in range(lax.axis_size(axis))])


def together(*values):
    return lax.optimization_barrier(values)


def all_sum(value, axes):
    for axis in axes:
        for step in bits_of(axis):
            value = value + swap(value, axis, step)
    return value


def parted(value, axis, step):
    value = value.reshape((value.shape[0] // 2, 2) + value.shape[1:])
    bit = jnp.minimum(jnp.bitwise_and(lax.axis_index(axis), step), 1)
    keep = lax.dynamic_index_in_dim(value, bit, 1, keepdims=False)
    send = lax.dynamic_index_in_dim(value, 1 - bit, 1, keepdims=False)
    return keep, send.astype(BF16)


def body(clips, gain, bias, weight, cotangent):
    x, g = clips[0], cotangent[0]
    frames, rows, cols, chan_in = x.shape
    chan_out = g.shape[-1]
    per_group = chan_in // GROUPS
    tm, dp, width = (lax.axis_size(name) for name in ("tm", "dp", "width"))
    per_frame = float(rows * width * cols * per_group)
    z, core = lax.axis_index("tm"), lax.axis_index("width")
    place = jnp.stack([z, core, lax.axis_index("dp")]).astype(jnp.int32)
    cells = rows * cols
    shape = jax.ShapeDtypeStruct
    half = chan_out // 2

    up = [(i, i + 1) for i in range(tm - 1)]
    down = [(i + 1, i) for i in range(tm - 1)]
    affine = jnp.pad(jnp.stack([gain, bias]), ((0, 2 * frames - 2), (0, 0)))[None]
    x, g, place = together(x, g, place)
    g_first = g.reshape(frames, cells, chan_out)[:2]
    flat = x.reshape(frames, cells, chan_in)
    g_next = lax.ppermute(g_first, "tm", down).reshape(2, rows, cols, chan_out)
    sums, x_last, g_rows, x_rows = call(
        functools.partial(prepare_kernel, per_group),
        (
            shape((2 * frames, chan_in), F32),
            shape((2, rows, cols, chan_in), BF16),
            shape((frames, cols, chan_out), BF16),
            shape((frames, cols, chan_in), BF16),
        ),
        [place, far(x), far(g)],
        [pltpu.VMEM(x.shape, BF16), pltpu.SemaphoreType.DMA((2 * frames,))],
        scalars=1,
        far=2,
    )
    sums = sums + swap(sums, "width", 1)
    g_edge = swap(g_rows, "width", 1)
    x_edge = swap(x_rows, "width", 1)
    sums, g_next, g_edge, x_edge = together(sums, g_next, g_edge, x_edge)

    def edges(*values):
        rows_out = (sum(v.shape[0] for v in values), cols, values[0].shape[3])
        return call(edge_kernel, shape(rows_out, BF16), [place, *values], scalars=1)

    next_edge = swap(edges(g_next), "width", 1)
    stats = sums[None]
    for step in bits_of("tm"):
        stats = jnp.concatenate([stats, swap(stats, "tm", step)], axis=0)
    stats = jnp.concatenate([stats, affine], axis=0)
    stats, next_edge = together(stats, next_edge)

    share = 27 * chan_in // (tm * dp)
    pieces = share % 48 == 0 and tm == 4 and dp == 2
    count = 3 * chan_in // 48
    if pieces:
        skip = chan_in
        late = lambda k: k // 3 if k % 3 == 2 else count + k // 3 * 2 + k % 3
    else:
        skip = 0
        late = lambda k: k
    keep, send = call(
        functools.partial(kernel_grad_kernel, per_frame, late, skip),
        (shape((27 * chan_in, half), F32), shape((27 * chan_in, half), BF16)),
        [place, stats, g_next, g_edge, next_edge, far(flat), far(g)],
        [
            pltpu.VMEM((3 * chan_in, frames * cells), BF16),
            pltpu.VMEM((frames + 2, rows + 2, cols, chan_out), BF16),
            pltpu.VMEM(flat.shape, BF16),
            pltpu.VMEM(g.shape, BF16),
            pltpu.SemaphoreType.DMA((frames + 1,)),
        ],
        scalars=1,
        far=2,
    )
    recv = swap(send, "width", 1)
    send, x_last, x_rows = together(send, x_last, x_rows)
    x_prev = lax.ppermute(x_last, "tm", [(i, (i + 1) % tm) for i in range(tm)])
    turn = [(i * width + c, (i + 1) % tm * width + (c ^ 1)) for i in range(tm) for c in range(width)]
    prev_edge = lax.ppermute(x_rows[frames - 2 :], ("tm", "width"), turn)

    def own(g):
        return call(
            own_grad_kernel,
            shape((frames, rows, cols, 3 * chan_in), F32),
            [g, weight],
            [pltpu.VMEM((frames, rows + 2, cols, chan_out), BF16)],
        )

    def gains(stats, own_grad):
        return call(
            functools.partial(gain_kernel, per_frame),
            shape((2, chan_in), F32),
            [place, stats, flat, own_grad, g_next, g_edge, next_edge, weight],
            [
                pltpu.VMEM((2, rows + 2, cols, chan_out), BF16),
                pltpu.VMEM((frames, rows, cols, 3 * chan_in), F32),
            ],
            scalars=1,
        )

    def outputs(hold):
        return call(
            functools.partial(output_kernel, per_frame),
            shape((frames * cells, chan_out), BF16),
            [place, hold, x, x_prev, x_edge, prev_edge, weight],
            [
                pltpu.VMEM((frames + 2, rows + 2, cols, 3 * chan_in), BF16),
                pltpu.VMEM((frames * cells, chan_out), F32),
            ],
            scalars=1,
        )

    if not pieces:
        output = outputs(stats)
        one = keep + recv.astype(F32)
        one = jnp.moveaxis(one.reshape(tm, dp, share, half), 1, 0)
        for step in bits_of("dp"):
            one, send = parted(one, "dp", step)
            one = one + swap(send, "dp", step).astype(F32)
        one = one[0]
        for step in bits_of("tm"):
            one, send = parted(one, "tm", step)
            one = one + swap(send, "tm", step).astype(F32)
        rider = all_sum(gains(stats, own(g)), ("width", "dp", "tm"))
        grad_weight = one[0]
    else:
        rest = share // 3
        cut = share - rest

        def piece(n, kind):
            return shape((n, half), kind)

        both = dp * rest
        stay1, send1, stay2, *send2 = call(
            functools.partial(split_kernel, cut, both),
            [piece(tm * cut, F32), piece(tm * cut, BF16), piece(both, F32)] + [piece(both, BF16)] * (tm - 1),
            [place, keep, recv],
            scalars=1,
        )
        send1, hold, x_prev, prev_edge, g, *send2 = together(send1, stats, x_prev, prev_edge, g, *send2)
        recv1 = swap(send1, "dp", 1)
        recv2 = [swap(v, "tm", k) for k, v in zip(OTHERS, send2)]
        rider = gains(hold, own(g))
        rider = rider + swap(rider, "width", 1)
        rider, hold = together(rider, hold)
        got = swap(rider, "dp", 1)
        recv1, got, *recv2 = together(recv1, got, *recv2)
        stay1, *send1, stay2, send2, rider = call(
            middle_kernel,
            [piece(cut, F32)]
            + [piece(cut + 16, BF16)] * (tm - 1)
            + [piece(rest, F32), piece(rest, BF16), shape(rider.shape, F32)],
            [place, stay1, recv1, stay2, *recv2, rider, got],
            scalars=1,
        )
        send2, hold, *send1 = together(send2, hold, *send1)
        recv1 = [swap(v, "tm", k) for k, v in zip(OTHERS, send1)]
        recv2 = swap(send2, "dp", 1)
        output = outputs(hold)
        recv2, output, *recv1 = together(recv2, output, *recv1)
        row = shape((1, chan_in), F32)
        grad_weight, *rider = call(
            last_kernel, [piece(share, F32), row, row], [stay1, *recv1, stay2, recv2, rider]
        )
        rider = [v.reshape(chan_in) for v in rider]
    return (output.reshape(1, frames, rows, cols, chan_out), grad_weight, rider[0], rider[1])


def solution(mesh):
    return jax.shard_map(
        body,
        mesh=mesh,
        in_specs=(
            P(("groups", "dp"), "tm", "width", None, None),
            P(),
            P(),
            P(),
            P(("groups", "dp"), "tm", "width", None, None),
        ),
        out_specs=(
            P(("groups", "dp"), "tm", "width", None, None),
            P(("groups", "tm", "dp"), "width"),
            P("groups"),
            P("groups"),
        ),
        check_vma=False,
    )
```

time: 77.1 us -> 58.2 us (0.75)
  waiting for transfers between devices: 28.7 us -> 19.6 us
  local copies, waits for them, and re-layouts: 7.41 us -> 0.98 us
  starting transfers between devices: 25 us -> 19 us
  Pallas kernels: 11.6 us -> 16.9 us
  other arithmetic: 3.07 us -> 0.77 us
    ppermute x16 -> x17, waiting for transfers between devices: 25.2 us -> 8.36 us  [swap(): lax.ppermute(value, axis, [(i, i ^ step) for i in range(lax.axis_size(axi...]
    ppermute x2 -> x3, waiting for transfers between devices: 3.49 us -> 11.2 us  [the longest x1 6.28 us: body(): g_next = lax.ppermute(g_first, 'tm', down).reshape(2, rows, cols, chan_out)]
    ppermute x16 -> x17, starting transfers between devices: 22.3 us -> 15.5 us  [swap(): lax.ppermute(value, axis, [(i, i ^ step) for i in range(lax.axis_size(axi...]
    unnamed x18 -> x6, local copies, waits for them, and re-layouts: 5.66 us -> 0.01 us
    pallas_call x5 -> x9, Pallas kernels: 11.6 us -> 16.9 us  [call(): pl.pallas_call(kernel, out_shape=out_shape, in_specs=[SMEM] * scalars + [...]
    add x9 -> x2, other arithmetic: 1.53 us -> 0.01 us  [the longest x1 0.01 us: body(): rider = rider + swap(rider, 'width', 1)]
    concatenate x5 -> x2, other arithmetic: 1.38 us -> 0.01 us  [the longest x1 0.01 us: body(): stats = jnp.concatenate([stats, affine], axis=0)]
    ppermute x2 -> x0, local copies, waits for them, and re-layouts: 0.93 us -> none  [the longest x1 0.91 us: body(): x_prev = lax.ppermute(x[frames - 2:], 'tm', up)]
  transfers between devices with their start and end apart: 18 -> 20, of which waited for: 12 -> 10; matrix products, arithmetic and copies ran while one was open for 5% -> 1% of each run, Pallas kernels for 7% -> 19%
where the time goes in v3:
time: 58.2 us; the launch traced here: 57.9 us
  waiting for transfers between devices  19.6 us (34%)
  starting transfers between devices  19 us (33%)
  Pallas kernels  16.9 us (29%)
  local copies, waits for them, and re-layouts  0.98 us (2%)
  other arithmetic  0.77 us (1%)
  between operations  0.75 us (1%)
    pallas_call x9, Pallas kernels, call(): pl.pallas_call(kernel, out_shape=out_shape, in_specs=[SMEM] * scalars + [...  16.9 us
    ppermute x17, starting transfers between devices, swap(): lax.ppermute(value, axis, [(i, i ^ step) for i in range(lax.axis_size(axi...  15.5 us
    ppermute x17, waiting for transfers between devices, swap(): lax.ppermute(value, axis, [(i, i ^ step) for i in range(lax.axis_size(axi...  8.36 us
    ppermute x1, waiting for transfers between devices, body(): g_next = lax.ppermute(g_first, 'tm', down).reshape(2, rows, cols, chan_out)  6.28 us
    ppermute x1, waiting for transfers between devices, body(): prev_edge = lax.ppermute(x_rows[frames - 2:], ('tm', 'width'), turn)  4.71 us
    ppermute x1, starting transfers between devices, body(): prev_edge = lax.ppermute(x_rows[frames - 2:], ('tm', 'width'), turn)  1.34 us
    ppermute x1, starting transfers between devices, body(): g_next = lax.ppermute(g_first, 'tm', down).reshape(2, rows, cols, chan_out)  1.29 us
  transfers between devices with their start and end apart: 20, of which 10 were waited for; matrix products, arithmetic and copies ran while one was open for 1% of the time, Pallas kernels for 19%

profile of v3, /device:TPU:0, one launch (start us, length us, event | category | flops | bytes accessed | tf_op | source)
XLA Modules:
  0.0 57.9 jit_solution(4178084121628114833)
XLA Ops:
  0.6 0.1 pad_add_fusion.place
  0.7 1.0 %slice.9 = bf16[2,4,64,256]{3,2,1,0:T(8,128)(2,1)S(1)} slice(bf16[4,4,64,256]{3,2,1,0:T(8,128)(2,1)} %bitcast.16), slice={[0:2], [0:4], [0:64], [0:256]} | slice | bytes 524288 | tf_op jit(solution)/shard_map/slice | solution.py:395
  1.7 1.3 %collective-permute-start.1 = (bf16[2,256,256]{2,1,0:T(8,128)(2,1)S(1)}, bf16[2,256,256]{2,1,0:T(8,128)(2,1)S(1)}, u32[]{:S(2)}, u32[]{:S(2)}) collective-permute-start(bf16[2,256,256]{2,1,0:T(8,128)(2,1)S(1)} %bitcast.28), channel_id=1, source_target_pairs={{4,0},{8,4},{12,8},{5,1},{9,5},{13,9},{6,2},{10,6},{14,10},{7,3},{... | collective-permute-start | bytes 786440 | tf_op jit(solution)/shard_map/ppermute | solution.py:397
  3.0 1.8 %shard_map.84 = (f32[8,128]{1,0:T(8,128)S(1)}, bf16[2,4,64,128]{3,2,1,0:T(8,128)(2,1)S(1)}, bf16[4,64,256]{2,1,0:T(8,128)(2,1)S(1)}, bf16[4,64,128]{2,1,0:T(8,128)(2,1)S(1)}) custom-call(s32[3]{0:T(128)S(1)} %pad_add_fusion.place, bf16[4,4,64,128]{3,2,1,0:T(8,128)(2,1)} %bitcast.20, bf16[4,4,64,256]{3,2,1,0:T(8,128)(2,1)} %bitcast.17), custom_call_target="tpu_custom_call" | custom-call | bytes 1118220 | tf_op jit(solution)/shard_map/pallas_call | solution.py:21
  4.8 0.5 collective-permute-start.2
  5.3 0.1 collective-permute-start.3
  5.4 0.4 collective-permute-start
  5.8 0.8 %collective-permute-done = f32[8,128]{1,0:T(8,128)S(1)} collective-permute-done((f32[8,128]{1,0:T(8,128)S(1)}, f32[8,128]{1,0:T(8,128)S(1)}, u32[]{:S(2)}, u32[]{:S(2)}) %collective-permute-start) | collective-permute-done | bytes 4128 | tf_op jit(solution)/shard_map/ppermute | solution.py:356
  6.6 0.0 collective-permute-done.3.edge_ref
  6.6 0.0 collective-permute-done.2.edge_ref
  6.6 6.3 %collective-permute-done.1 = bf16[2,256,256]{2,1,0:T(8,128)(2,1)S(1)} collective-permute-done((bf16[2,256,256]{2,1,0:T(8,128)(2,1)S(1)}, bf16[2,256,256]{2,1,0:T(8,128)(2,1)S(1)}, u32[]{:S(2)}, u32[]{:S(2)}) %collective-permute-start.1) | collective-permute-done | bytes 262176 | tf_op jit(solution)/shard_map/ppermute | solution.py:397
  12.9 1.7 %collective-permute-start.4 = (f32[1,8,128]{2,1,0:T(8,128)S(1)}, f32[1,8,128]{2,1,0:T(8,128)S(1)}, u32[]{:S(2)}, u32[]{:S(2)}) collective-permute-start(f32[1,8,128]{2,1,0:T(8,128)S(1)} %bitcast.29), channel_id=1, source_target_pairs={{0,4},{4,0},{8,12},{12,8},{1,5},{5,1},{9,13},{13,9},{2,6},{6,2},{1... | collective-permute-start | bytes 12296 | tf_op jit(solution)/shard_map/ppermute | solution.py:356
  14.6 1.9 %collective-permute-done.4 = f32[1,8,128]{2,1,0:T(8,128)S(1)} collective-permute-done((f32[1,8,128]{2,1,0:T(8,128)S(1)}, f32[1,8,128]{2,1,0:T(8,128)S(1)}, u32[]{:S(2)}, u32[]{:S(2)}) %collective-permute-start.4) | collective-permute-done | bytes 4128 | tf_op jit(solution)/shard_map/ppermute | solution.py:356
  16.5 2.7 %collective-permute-start.5 = (f32[2,8,128]{2,1,0:T(8,128)S(1)}, f32[2,8,128]{2,1,0:T(8,128)S(1)}, u32[]{:S(2)}, u32[]{:S(2)}) collective-permute-start(f32[2,8,128]{2,1,0:T(8,128)S(1)} %pad_maximum_fusion.1), channel_id=1, source_target_pairs={{0,8},{4,12},{8,0},{12,4},{1,9},{5,13},{9,1},{13,5},{2,10},{6,14},... | collective-permute-start | bytes 24584 | tf_op jit(solution)/shard_map/ppermute | solution.py:356
  19.3 0.7 %fusion = f32[1,8,128]{2,1,0:T(8,128)S(1)} fusion(f32[1,128]{1,0:T(1,128)} %bitcast.32, f32[1,128]{1,0:T(1,128)} %bitcast.33), kind=kLoop, calls=%fused_computation.3 | loop fusion | flops 4096 | bytes 5120 | tf_op jit(solution)/shard_map/broadcast_in_dim | solution.py:393
  20.0 0.6 shard_map.85
  20.5 0.1 collective-permute-start.6
  20.6 0.5 collective-permute-done.5
  21.1 0.8 %collective-permute-done.6.edge_next = bf16[2,64,256]{2,1,0:T(8,128)(2,1)S(1)} collective-permute-done((bf16[2,64,256]{2,1,0:T(8,128)(2,1)S(1)}, bf16[2,64,256]{2,1,0:T(8,128)(2,1)S(1)}, u32[]{:S(2)}, u32[]{:S(2)}) %collective-permute-start.6) | collective-permute-done | bytes 65568 | tf_op jit(solution)/shard_map/ppermute | solution.py:356
  21.8 0.0 copy-start
  21.8 0.0 copy-start.1
  21.8 4.5 %shard_map.86 = (f32[3456,128]{1,0:T(8,128)S(1)}, bf16[3456,128]{1,0:T(8,128)(2,1)S(1)}) custom-call(s32[3]{0:T(128)S(1)} %pad_add_fusion.place, f32[5,8,128]{2,1,0:T(8,128)S(1)} %pad_maximum_fusion.stats_ref, bf16[2,4,64,256]{3,2,1,0:T(8,128)(2,1)S(1)} %bitcast.25, bf16[4,64,256]{2,1,0:T(8,128)(2,1)S(1)} %collective-permute-done.2.edge_ref, ...), custom_call_target="tpu_custom_call" | custom-call | bytes 3919884 | tf_op jit(solution)/shard_map/pallas_call | solution.py:21
  26.3 0.2 collective-permute-start.7
  26.5 0.9 %collective-permute-start.8 = (bf16[2,4,64,128]{3,2,1,0:T(8,128)(2,1)S(1)}, bf16[2,4,64,128]{3,2,1,0:T(8,128)(2,1)S(1)}, u32[]{:S(2)}, u32[]{:S(2)}) collective-permute-start(bf16[2,4,64,128]{3,2,1,0:T(8,128)(2,1)S(1)} %get-tuple-element.78), channel_id=1, source_target_pairs={{0,4},{4,8},{8,12},{12,0},{1,5},{5,9},{9,13},{13,1},{2,6},{6,10},{... | collective-permute-start | bytes 393224 | tf_op jit(solution)/shard_map/ppermute | solution.py:452
  27.4 1.3 %collective-permute-start.9 = (bf16[2,64,128]{2,1,0:T(8,128)(2,1)S(1)}, bf16[2,64,128]{2,1,0:T(8,128)(2,1)S(1)}, u32[]{:S(2)}, u32[]{:S(2)}) collective-permute-start(bf16[2,64,128]{2,1,0:T(8,128)(2,1)S(1)} %slice.11), channel_id=1, source_target_pairs={{0,5},{1,4},{4,9},{5,8},{8,13},{9,12},{12,1},{13,0},{2,7},{3,6},{6... | collective-permute-start | bytes 98312 | tf_op jit(solution)/shard_map/ppermute | solution.py:454
  28.8 0.0 collective-permute-done.7.recv_ref
  28.8 0.7 %shard_map.87 = (f32[1152,128]{1,0:T(8,128)S(1)}, bf16[1152,128]{1,0:T(8,128)(2,1)S(1)}, f32[288,128]{1,0:T(8,128)S(1)}, bf16[288,128]{1,0:T(8,128)(2,1)S(1)}, b...) custom-call(s32[3]{0:T(128)S(1)} %pad_add_fusion.place, f32[3456,128]{1,0:T(8,128)S(1)} %get-tuple-element.73.keep_ref, ...), custom_call_target="tpu_custom_call" | custom-call | bytes 3907596 | tf_op jit(solution)/shard_map/pallas_call | solution.py:21
  29.5 4.7 %collective-permute-done.9.prev_edge = bf16[2,64,128]{2,1,0:T(8,128)(2,1)S(1)} collective-permute-done((bf16[2,64,128]{2,1,0:T(8,128)(2,1)S(1)}, bf16[2,64,128]{2,1,0:T(8,128)(2,1)S(1)}, u32[]{:S(2)}, u32[]{:S(2)}) %collective-permute-start.9) | collective-permute-done | bytes 32800 | tf_op jit(solution)/shard_map/ppermute | solution.py:454
  34.2 0.2 collective-permute-done.8.prev_ref
  34.4 0.0 copy-start.2
  34.4 1.5 %collective-permute-start.10 = (bf16[1152,128]{1,0:T(8,128)(2,1)S(1)}, bf16[1152,128]{1,0:T(8,128)(2,1)S(1)}, u32[]{:S(2)}, u32[]{:S(2)}) collective-permute-start(bf16[1152,128]{1,0:T(8,128)(2,1)S(1)} %get-tuple-element.83), channel_id=1, source_target_pairs={{0,2},{2,0},{1,3},{3,1},{4,6},{6,4},{5,7},{7,5},{8,10},{10,8},{9,1... | collective-permute-start | bytes 884744 | tf_op jit(solution)/shard_map/ppermute | solution.py:356
  35.9 0.2 collective-permute-start.13
  36.1 1.3 %collective-permute-start.14 = (bf16[288,128]{1,0:T(8,128)(2,1)S(1)}, bf16[288,128]{1,0:T(8,128)(2,1)S(1)}, u32[]{:S(2)}, u32[]{:S(2)}) collective-permute-start(bf16[288,128]{1,0:T(8,128)(2,1)S(1)} %get-tuple-element.88), channel_id=1, source_target_pairs={{0,12},{4,8},{8,4},{12,0},{1,13},{5,9},{9,5},{13,1},{2,14},{6,10},... | collective-permute-start | bytes 221192 | tf_op jit(solution)/shard_map/ppermute | solution.py:356
  37.5 1.9 %collective-permute-start.15 = (bf16[288,128]{1,0:T(8,128)(2,1)S(1)}, bf16[288,128]{1,0:T(8,128)(2,1)S(1)}, u32[]{:S(2)}, u32[]{:S(2)}) collective-permute-start(bf16[288,128]{1,0:T(8,128)(2,1)S(1)} %get-tuple-element.89), channel_id=1, source_target_pairs={{0,4},{4,0},{8,12},{12,8},{1,5},{5,1},{9,13},{13,9},{2,6},{6,2},{1... | collective-permute-start | bytes 221192 | tf_op jit(solution)/shard_map/ppermute | solution.py:356
  39.4 0.0 copy-done
  39.4 0.0 copy-done.1
  39.4 2.0 %shard_map.88.own_ref = f32[4,4,64,384]{3,2,1,0:T(8,128)S(1)} custom-call(bf16[4,4,64,256]{3,2,1,0:T(8,128)(2,1)S(1)} %bitcast.19, bf16[3456,256]{1,0:T(8,128)(2,1)S(1)} %copy-done), custom_call_target="tpu_custom_call" | custom-call | bytes 3866624 | tf_op jit(solution)/shard_map/pallas_call | solution.py:21
  41.4 0.0 copy-done.2
  41.4 1.8 %shard_map.89 = f32[2,128]{1,0:T(2,128)S(1)} custom-call(s32[3]{0:T(128)S(1)} %pad_add_fusion.place, f32[5,8,128]{2,1,0:T(8,128)S(1)} %pad_maximum_fusion.stats_ref, bf16[4,256,128]{2,1,0:T(8,128)(2,1)S(1)} %bitcast.22, f32[4,4,64,384]{3,2,1,0:T(8,128)S(1)} %shard_map.88.own_ref, bf16[2,4,64,256]{3,2,1,0:T(8,128)(2,1)S(1)} %bitcast.26, ...), custom_call_target="tpu_custom_call" | custom-call | bytes 4084748 | tf_op jit(solution)/shard_map/pallas_call | solution.py:21
  43.2 0.1 collective-permute-start.11
  43.3 1.1 %collective-permute-done.11 = f32[2,128]{1,0:T(2,128)S(1)} collective-permute-done((f32[2,128]{1,0:T(2,128)S(1)}, f32[2,128]{1,0:T(2,128)S(1)}, u32[]{:S(2)}, u32[]{:S(2)}) %collective-permute-start.11) | collective-permute-done | bytes 1056 | tf_op jit(solution)/shard_map/ppermute | solution.py:356
  44.5 0.5 collective-permute-start.12
  45.0 3.0 %collective-permute-done.12.got_ref = f32[2,128]{1,0:T(2,128)S(1)} collective-permute-done((f32[2,128]{1,0:T(2,128)S(1)}, f32[2,128]{1,0:T(2,128)S(1)}, u32[]{:S(2)}, u32[]{:S(2)}) %collective-permute-start.12) | collective-permute-done | bytes 1056 | tf_op jit(solution)/shard_map/ppermute | solution.py:356
  48.0 0.0 collective-permute-done.13.b_ref
  48.0 0.0 collective-permute-done.14.c_ref
  48.0 0.0 collective-permute-done.15.a_ref
  48.0 0.0 collective-permute-done.10.recv1_ref
  48.0 0.6 %shard_map.90 = (f32[288,128]{1,0:T(8,128)S(1)}, bf16[304,128]{1,0:T(8,128)(2,1)S(1)}, bf16[304,128]{1,0:T(8,128)(2,1)S(1)}, bf16[304,128]{1,0:T(8,128)(2,1)S(1)...) custom-call(s32[3]{0:T(128)S(1)} %pad_add_fusion.place, ...), custom_call_target="tpu_custom_call" | custom-call | bytes 1747980 | tf_op jit(solution)/shard_map/pallas_call | solution.py:21
  48.7 1.2 %collective-permute-start.17 = (bf16[304,128]{1,0:T(8,128)(2,1)S(1)}, bf16[304,128]{1,0:T(8,128)(2,1)S(1)}, u32[]{:S(2)}, u32[]{:S(2)}) collective-permute-start(bf16[304,128]{1,0:T(8,128)(2,1)S(1)} %get-tuple-element.106), channel_id=1, source_target_pairs={{0,8},{4,12},{8,0},{12,4},{1,9},{5,13},{9,1},{13,5},{2,10},{6,14},... | collective-permute-start | bytes 233480 | tf_op jit(solution)/shard_map/ppermute | solution.py:356
  49.9 1.4 %collective-permute-start.18 = (bf16[304,128]{1,0:T(8,128)(2,1)S(1)}, bf16[304,128]{1,0:T(8,128)(2,1)S(1)}, u32[]{:S(2)}, u32[]{:S(2)}) collective-permute-start(bf16[304,128]{1,0:T(8,128)(2,1)S(1)} %get-tuple-element.107), channel_id=1, source_target_pairs={{0,12},{4,8},{8,4},{12,0},{1,13},{5,9},{9,5},{13,1},{2,14},{6,10},... | collective-permute-start | bytes 233480 | tf_op jit(solution)/shard_map/ppermute | solution.py:356
  51.2 1.0 %collective-permute-start.19 = (bf16[304,128]{1,0:T(8,128)(2,1)S(1)}, bf16[304,128]{1,0:T(8,128)(2,1)S(1)}, u32[]{:S(2)}, u32[]{:S(2)}) collective-permute-start(bf16[304,128]{1,0:T(8,128)(2,1)S(1)} %get-tuple-element.108), channel_id=1, source_target_pairs={{0,4},{4,0},{8,12},{12,8},{1,5},{5,1},{9,13},{13,9},{2,6},{6,2},{1... | collective-permute-start | bytes 233480 | tf_op jit(solution)/shard_map/ppermute | solution.py:356
  52.2 0.5 collective-permute-start.16
  52.8 4.2 %shard_map.91 = bf16[1024,256]{1,0:T(8,128)(2,1)} custom-call(s32[3]{0:T(128)S(1)} %pad_add_fusion.place, f32[5,8,128]{2,1,0:T(8,128)S(1)} %pad_maximum_fusion.stats_ref, bf16[4,4,64,128]{3,2,1,0:T(8,128)(2,1)S(1)} %bitcast.23, bf16[2,4,64,128]{3,2,1,0:T(8,128)(2,1)S(1)} %collective-permute-done.8.prev_ref, ...), custom_call_target="tpu_custom_call" | custom-call | bytes 2805772 | tf_op jit(solution)/shard_map/pallas_call | solution.py:21
  56.9 0.0 collective-permute-done.16.recv2_ref
  57.0 0.0 collective-permute-done.17.b_ref
  57.0 0.0 collective-permute-done.18.c_ref
  57.0 0.2 collective-permute-done.19.a_ref
  57.2 0.7 %shard_map.92 = (f32[432,128]{1,0:T(8,128)}, f32[1,128]{1,0:T(1,128)}, f32[1,128]{1,0:T(1,128)}) custom-call(f32[288,128]{1,0:T(8,128)S(1)} %get-tuple-element.110.stay1_ref, bf16[304,128]{1,0:T(8,128)(2,1)S(1)} %collective-permute-done.17.b_ref, bf16[304,128]{1,0:T(8,128)(2,1)S(1)} %collective-permute-done.18.c_ref, ...), custom_call_target="tpu_custom_call" | custom-call | bytes 714752 | tf_op jit(solution)/shard_map/pallas_call | solution.py:21
  (5 shorter events, 0.0 us)
Async XLA Ops:
  1.7 11.2 %collective-permute-start.1 = (bf16[2,256,256]{2,1,0:T(8,128)(2,1)S(1)}, bf16[2,256,256]{2,1,0:T(8,128)(2,1)S(1)}, u32[]{:S(2)}, u32[]{:S(2)}) collective-permute-start(bf16[2,256,256]{2,1,0:T(8,128)(2,1)S(1)} %bitcast.28), channel_id=1, source_target_pairs={{4,0},{8,4},{12,8},{5,1},{9,5},{13,9},{6,2},{10,6},{14,10},{7,3},{... | collective-permute-start | bytes 786440 | tf_op jit(solution)/shard_map/ppermute | solution.py:397
  4.8 1.9 %collective-permute-start.2 = (bf16[4,64,256]{2,1,0:T(8,128)(2,1)S(1)}, bf16[4,64,256]{2,1,0:T(8,128)(2,1)S(1)}, u32[]{:S(2)}, u32[]{:S(2)}) collective-permute-start(bf16[4,64,256]{2,1,0:T(8,128)(2,1)S(1)} %get-tuple-element.66), channel_id=1, source_target_pairs={{0,1},{1,0},{2,3},{3,2},{4,5},{5,4},{6,7},{7,6},{8,9},{9,8},{10,11... | collective-permute-start | bytes 393224 | tf_op jit(solution)/shard_map/ppermute | solution.py:356
  5.3 1.3 %collective-permute-start.3 = (bf16[4,64,128]{2,1,0:T(8,128)(2,1)S(1)}, bf16[4,64,128]{2,1,0:T(8,128)(2,1)S(1)}, u32[]{:S(2)}, u32[]{:S(2)}) collective-permute-start(bf16[4,64,128]{2,1,0:T(8,128)(2,1)S(1)} %get-tuple-element.79), channel_id=1, source_target_pairs={{0,1},{1,0},{2,3},{3,2},{4,5},{5,4},{6,7},{7,6},{8,9},{9,8},{10,11... | collective-permute-start | bytes 196616 | tf_op jit(solution)/shard_map/ppermute | solution.py:356
  5.4 1.3 %collective-permute-start = (f32[8,128]{1,0:T(8,128)S(1)}, f32[8,128]{1,0:T(8,128)S(1)}, u32[]{:S(2)}, u32[]{:S(2)}) collective-permute-start(f32[8,128]{1,0:T(8,128)S(1)} %get-tuple-element.65), channel_id=1, source_target_pairs={{0,1},{1,0},{2,3},{3,2},{4,5},{5,4},{6,7},{7,6},{8,9},{9,8},{10,11... | collective-permute-start | bytes 12296 | tf_op jit(solution)/shard_map/ppermute | solution.py:356
  12.9 3.6 %collective-permute-start.4 = (f32[1,8,128]{2,1,0:T(8,128)S(1)}, f32[1,8,128]{2,1,0:T(8,128)S(1)}, u32[]{:S(2)}, u32[]{:S(2)}) collective-permute-start(f32[1,8,128]{2,1,0:T(8,128)S(1)} %bitcast.29), channel_id=1, source_target_pairs={{0,4},{4,0},{8,12},{12,8},{1,5},{5,1},{9,13},{13,9},{2,6},{6,2},{1... | collective-permute-start | bytes 12296 | tf_op jit(solution)/shard_map/ppermute | solution.py:356
  16.5 4.5 %collective-permute-start.5 = (f32[2,8,128]{2,1,0:T(8,128)S(1)}, f32[2,8,128]{2,1,0:T(8,128)S(1)}, u32[]{:S(2)}, u32[]{:S(2)}) collective-permute-start(f32[2,8,128]{2,1,0:T(8,128)S(1)} %pad_maximum_fusion.1), channel_id=1, source_target_pairs={{0,8},{4,12},{8,0},{12,4},{1,9},{5,13},{9,1},{13,5},{2,10},{6,14},... | collective-permute-start | bytes 24584 | tf_op jit(solution)/shard_map/ppermute | solution.py:356
  20.5 1.3 %collective-permute-start.6 = (bf16[2,64,256]{2,1,0:T(8,128)(2,1)S(1)}, bf16[2,64,256]{2,1,0:T(8,128)(2,1)S(1)}, u32[]{:S(2)}, u32[]{:S(2)}) collective-permute-start(bf16[2,64,256]{2,1,0:T(8,128)(2,1)S(1)} %shard_map.85), channel_id=1, source_target_pairs={{0,1},{1,0},{2,3},{3,2},{4,5},{5,4},{6,7},{7,6},{8,9},{9,8},{10,11... | collective-permute-start | bytes 196616 | tf_op jit(solution)/shard_map/ppermute | solution.py:356
  21.8 17.6 %copy-start = (bf16[3456,256]{1,0:T(8,128)(2,1)S(1)}, bf16[3456,256]{1,0:T(8,128)(2,1)}, u32[]{:S(2)}) copy-start(bf16[3456,256]{1,0:T(8,128)(2,1)} %w_ref.5) | copy-start | bytes 5308420
  21.8 17.6 %copy-start.1 = (bf16[1,4,4,64,256]{4,3,2,1,0:T(8,128)(2,1)S(1)}, bf16[1,4,4,64,256]{4,3,2,1,0:T(8,128)(2,1)}, u32[]{:S(2)}) copy-start(bf16[1,4,4,64,256]{4,3,2,1,0:T(8,128)(2,1)} %param.9) | copy-start | bytes 1572868
  26.3 2.5 %collective-permute-start.7 = (bf16[3456,128]{1,0:T(8,128)(2,1)S(1)}, bf16[3456,128]{1,0:T(8,128)(2,1)S(1)}, u32[]{:S(2)}, u32[]{:S(2)}) collective-permute-start(bf16[3456,128]{1,0:T(8,128)(2,1)S(1)} %get-tuple-element.74), channel_id=1, source_target_pairs={{0,1},{1,0},{2,3},{3,2},{4,5},{5,4},{6,7},{7,6},{8,9},{9,8},{10,11... | collective-permute-start | bytes 2654216 | tf_op jit(solution)/shard_map/ppermute | solution.py:356
  26.5 7.9 %collective-permute-start.8 = (bf16[2,4,64,128]{3,2,1,0:T(8,128)(2,1)S(1)}, bf16[2,4,64,128]{3,2,1,0:T(8,128)(2,1)S(1)}, u32[]{:S(2)}, u32[]{:S(2)}) collective-permute-start(bf16[2,4,64,128]{3,2,1,0:T(8,128)(2,1)S(1)} %get-tuple-element.78), channel_id=1, source_target_pairs={{0,4},{4,8},{8,12},{12,0},{1,5},{5,9},{9,13},{13,1},{2,6},{6,10},{... | collective-permute-start | bytes 393224 | tf_op jit(solution)/shard_map/ppermute | solution.py:452
  27.4 6.8 %collective-permute-start.9 = (bf16[2,64,128]{2,1,0:T(8,128)(2,1)S(1)}, bf16[2,64,128]{2,1,0:T(8,128)(2,1)S(1)}, u32[]{:S(2)}, u32[]{:S(2)}) collective-permute-start(bf16[2,64,128]{2,1,0:T(8,128)(2,1)S(1)} %slice.11), channel_id=1, source_target_pairs={{0,5},{1,4},{4,9},{5,8},{8,13},{9,12},{12,1},{13,0},{2,7},{3,6},{6... | collective-permute-start | bytes 98312 | tf_op jit(solution)/shard_map/ppermute | solution.py:454
  34.4 7.0 %copy-start.2 = (bf16[1,4,4,64,128]{4,3,2,1,0:T(8,128)(2,1)S(1)}, bf16[1,4,4,64,128]{4,3,2,1,0:T(8,128)(2,1)}, u32[]{:S(2)}) copy-start(bf16[1,4,4,64,128]{4,3,2,1,0:T(8,128)(2,1)} %param.5) | copy-start | bytes 786436
  34.4 13.6 %collective-permute-start.10 = (bf16[1152,128]{1,0:T(8,128)(2,1)S(1)}, bf16[1152,128]{1,0:T(8,128)(2,1)S(1)}, u32[]{:S(2)}, u32[]{:S(2)}) collective-permute-start(bf16[1152,128]{1,0:T(8,128)(2,1)S(1)} %get-tuple-element.83), channel_id=1, source_target_pairs={{0,2},{2,0},{1,3},{3,1},{4,6},{6,4},{5,7},{7,5},{8,10},{10,8},{9,1... | collective-permute-start | bytes 884744 | tf_op jit(solution)/shard_map/ppermute | solution.py:356
  35.9 12.1 %collective-permute-start.13 = (bf16[288,128]{1,0:T(8,128)(2,1)S(1)}, bf16[288,128]{1,0:T(8,128)(2,1)S(1)}, u32[]{:S(2)}, u32[]{:S(2)}) collective-permute-start(bf16[288,128]{1,0:T(8,128)(2,1)S(1)} %get-tuple-element.87), channel_id=1, source_target_pairs={{0,8},{4,12},{8,0},{12,4},{1,9},{5,13},{9,1},{13,5},{2,10},{6,14},... | collective-permute-start | bytes 221192 | tf_op jit(solution)/shard_map/ppermute | solution.py:356
  36.1 11.9 %collective-permute-start.14 = (bf16[288,128]{1,0:T(8,128)(2,1)S(1)}, bf16[288,128]{1,0:T(8,128)(2,1)S(1)}, u32[]{:S(2)}, u32[]{:S(2)}) collective-permute-start(bf16[288,128]{1,0:T(8,128)(2,1)S(1)} %get-tuple-element.88), channel_id=1, source_target_pairs={{0,12},{4,8},{8,4},{12,0},{1,13},{5,9},{9,5},{13,1},{2,14},{6,10},... | collective-permute-start | bytes 221192 | tf_op jit(solution)/shard_map/ppermute | solution.py:356
  37.5 10.6 %collective-permute-start.15 = (bf16[288,128]{1,0:T(8,128)(2,1)S(1)}, bf16[288,128]{1,0:T(8,128)(2,1)S(1)}, u32[]{:S(2)}, u32[]{:S(2)}) collective-permute-start(bf16[288,128]{1,0:T(8,128)(2,1)S(1)} %get-tuple-element.89), channel_id=1, source_target_pairs={{0,4},{4,0},{8,12},{12,8},{1,5},{5,1},{9,13},{13,9},{2,6},{6,2},{1... | collective-permute-start | bytes 221192 | tf_op jit(solution)/shard_map/ppermute | solution.py:356
  43.2 1.2 %collective-permute-start.11 = (f32[2,128]{1,0:T(2,128)S(1)}, f32[2,128]{1,0:T(2,128)S(1)}, u32[]{:S(2)}, u32[]{:S(2)}) collective-permute-start(f32[2,128]{1,0:T(2,128)S(1)} %shard_map.89), channel_id=1, source_target_pairs={{0,1},{1,0},{2,3},{3,2},{4,5},{5,4},{6,7},{7,6},{8,9},{9,8},{10,11... | collective-permute-start | bytes 3080 | tf_op jit(solution)/shard_map/ppermute | solution.py:356
  44.5 3.6 %collective-permute-start.12 = (f32[2,128]{1,0:T(2,128)S(1)}, f32[2,128]{1,0:T(2,128)S(1)}, u32[]{:S(2)}, u32[]{:S(2)}) collective-permute-start(f32[2,128]{1,0:T(2,128)S(1)} %add.9.rider_ref), channel_id=1, source_target_pairs={{0,2},{2,0},{1,3},{3,1},{4,6},{6,4},{5,7},{7,5},{8,10},{10,8},{9,1... | collective-permute-start | bytes 3080 | tf_op jit(solution)/shard_map/ppermute | solution.py:356
  48.7 8.3 %collective-permute-start.17 = (bf16[304,128]{1,0:T(8,128)(2,1)S(1)}, bf16[304,128]{1,0:T(8,128)(2,1)S(1)}, u32[]{:S(2)}, u32[]{:S(2)}) collective-permute-start(bf16[304,128]{1,0:T(8,128)(2,1)S(1)} %get-tuple-element.106), channel_id=1, source_target_pairs={{0,8},{4,12},{8,0},{12,4},{1,9},{5,13},{9,1},{13,5},{2,10},{6,14},... | collective-permute-start | bytes 233480 | tf_op jit(solution)/shard_map/ppermute | solution.py:356
  49.9 7.1 %collective-permute-start.18 = (bf16[304,128]{1,0:T(8,128)(2,1)S(1)}, bf16[304,128]{1,0:T(8,128)(2,1)S(1)}, u32[]{:S(2)}, u32[]{:S(2)}) collective-permute-start(bf16[304,128]{1,0:T(8,128)(2,1)S(1)} %get-tuple-element.107), channel_id=1, source_target_pairs={{0,12},{4,8},{8,4},{12,0},{1,13},{5,9},{9,5},{13,1},{2,14},{6,10},... | collective-permute-start | bytes 233480 | tf_op jit(solution)/shard_map/ppermute | solution.py:356
  51.2 6.0 %collective-permute-start.19 = (bf16[304,128]{1,0:T(8,128)(2,1)S(1)}, bf16[304,128]{1,0:T(8,128)(2,1)S(1)}, u32[]{:S(2)}, u32[]{:S(2)}) collective-permute-start(bf16[304,128]{1,0:T(8,128)(2,1)S(1)} %get-tuple-element.108), channel_id=1, source_target_pairs={{0,4},{4,0},{8,12},{12,8},{1,5},{5,1},{9,13},{13,9},{2,6},{6,2},{1... | collective-permute-start | bytes 233480 | tf_op jit(solution)/shard_map/ppermute | solution.py:356
  52.2 4.7 %collective-permute-start.16 = (bf16[144,128]{1,0:T(8,128)(2,1)S(1)}, bf16[144,128]{1,0:T(8,128)(2,1)S(1)}, u32[]{:S(2)}, u32[]{:S(2)}) collective-permute-start(bf16[144,128]{1,0:T(8,128)(2,1)S(1)} %get-tuple-element.101), channel_id=1, source_target_pairs={{0,2},{2,0},{1,3},{3,1},{4,6},{6,4},{5,7},{7,5},{8,10},{10,8},{9,1... | collective-permute-start | bytes 110600 | tf_op jit(solution)/shard_map/ppermute | solution.py:356

commit v4 on v3

--- a/solution.py
+++ b/solution.py
@@ -45,11 +45,11 @@
     return rows
 
 
-def prepare_kernel(per_group, place, x_hbm, g_hbm, sums_ref, last_ref, row_ref, x_row_ref, x_ref, sems):
+def prepare_kernel(per_group, place, x_hbm, g_hbm, sums_ref, last_ref, row_ref, x_row_ref, x_ref, g_ref, sems):
     frames, rows, cols, chan_in = x_ref.shape
     row = jnp.where(place[1] == 0, rows - 1, 0)
     copies = [pltpu.make_async_copy(x_hbm.at[t], x_ref.at[t], sems.at[t]) for t in range(frames)]
-    copies += [pltpu.make_async_copy(g_hbm.at[t, row], row_ref.at[t], sems.at[frames + t]) for t in range(frames)]
+    copies += [pltpu.make_async_copy(g_hbm.at[t], g_ref.at[t], sems.at[frames + t]) for t in range(frames)]
     for copy in copies:
         copy.start()
     firsts, squares = [], []
@@ -61,8 +61,9 @@
         x_row_ref[t] = x_ref[t, row]
     last_ref[...] = x_ref[frames - 2 :]
     sums_ref[...] = group_sum(jnp.concatenate(firsts + squares, axis=0), per_group)
-    for copy in copies[frames:]:
-        copy.wait()
+    for t in range(frames):
+        copies[frames + t].wait()
+        row_ref[t] = g_ref[t, row]
 
 
 def edge_kernel(place, first_ref, *rest):
@@ -184,16 +185,13 @@
 
 
 def kernel_grad_kernel(
-    per_frame, late, skip, place, stats_ref, next_ref, edge_ref, edge_next, x_hbm, g_hbm, *rest
+    per_frame, late, skip, place, stats_ref, next_ref, edge_ref, edge_next, x_ref, g_ref, *rest
 ):
-    keep_ref, send_ref, ht_ref, gp_ref, x_ref, g_ref, sems = rest
+    keep_ref, send_ref, ht_ref, gp_ref = rest
     frames, cells, chan_in = x_ref.shape
     rows, cols, chan_out = g_ref.shape[1:]
     core = place[1]
-    copies = [pltpu.make_async_copy(x_hbm.at[t], x_ref.at[t], sems.at[t]) for t in range(frames)]
-    copies.append(pltpu.make_async_copy(g_hbm, g_ref, sems.at[frames]))
-    for copy in copies:
-        copy.start()
+    pad_rows(core, g_ref[...], edge_ref[...], gp_ref.at[:frames])
     pad_rows(core, next_ref[...], edge_next[...], gp_ref.at[frames:])
     means, inverses = frame_stats(place, stats_ref, frames, per_frame)
     affine = stats_ref[stats_ref.shape[0] - 1]
@@ -201,7 +199,6 @@
     block = 2 * cols
     lane = lax.broadcasted_iota(jnp.int32, (chan_in, block), 1) % cols
     for t in range(frames):
-        copies[t].wait()
         for half in range(cells // block):
             v = x_ref[t, half * block : (half + 1) * block].astype(F32)
             act = (v - means[2 + t]) * inverses[2 + t] * gain + bias
@@ -215,8 +212,6 @@
                 for k in range(chan_in // 16):
                     to = late(d * (chan_in // 16) + k) * 16
                     ht_ref[to : to + 16, at : at + block] = piece[k * 16 : (k + 1) * 16]
-    copies[frames].wait()
-    pad_rows(core, g_ref[...], edge_ref[...], gp_ref.at[:frames])
     mine = chan_out // 2
     n = 3 * chan_in
     for a in range(3):
@@ -395,23 +390,34 @@
     g_first = g.reshape(frames, cells, chan_out)[:2]
     flat = x.reshape(frames, cells, chan_in)
     g_next = lax.ppermute(g_first, "tm", down).reshape(2, rows, cols, chan_out)
-    sums, x_last, g_rows, x_rows = call(
+    sums, x_last, g_rows, x_rows, x_near, g_near = call(
         functools.partial(prepare_kernel, per_group),
         (
             shape((2 * frames, chan_in), F32),
             shape((2, rows, cols, chan_in), BF16),
             shape((frames, cols, chan_out), BF16),
             shape((frames, cols, chan_in), BF16),
+            shape(x.shape, BF16),
+            shape(g.shape, BF16),
         ),
         [place, far(x), far(g)],
-        [pltpu.VMEM(x.shape, BF16), pltpu.SemaphoreType.DMA((2 * frames,))],
+        [pltpu.SemaphoreType.DMA((2 * frames,))],
         scalars=1,
         far=2,
     )
     sums = sums + swap(sums, "width", 1)
     g_edge = swap(g_rows, "width", 1)
     x_edge = swap(x_rows, "width", 1)
-    sums, g_next, g_edge, x_edge = together(sums, g_next, g_edge, x_edge)
+    x, g = x_near, g_near
+    flat = x.reshape(frames, cells, chan_in)
+    sums, g = together(sums, g)
+    own_grad = call(
+        own_grad_kernel,
+        shape((frames, rows, cols, 3 * chan_in), F32),
+        [g, weight],
+        [pltpu.VMEM((frames, rows + 2, cols, chan_out), BF16)],
+    )
+    sums, g_next, g_edge, x_edge, own_grad = together(sums, g_next, g_edge, x_edge, own_grad)
 
     def edges(*values):
         rows_out = (sum(v.shape[0] for v in values), cols, values[0].shape[3])
@@ -422,7 +428,10 @@
     for step in bits_of("tm"):
         stats = jnp.concatenate([stats, swap(stats, "tm", step)], axis=0)
     stats = jnp.concatenate([stats, affine], axis=0)
-    stats, next_edge = together(stats, next_edge)
+    stats, next_edge, x_last, x_rows = together(stats, next_edge, x_last, x_rows)
+    x_prev = lax.ppermute(x_last, "tm", [(i, (i + 1) % tm) for i in range(tm)])
+    turn = [(i * width + c, (i + 1) % tm * width + (c ^ 1)) for i in range(tm) for c in range(width)]
+    prev_edge = lax.ppermute(x_rows[frames - 2 :], ("tm", "width"), turn)
 
     share = 27 * chan_in // (tm * dp)
     pieces = share % 48 == 0 and tm == 4 and dp == 2
@@ -436,42 +445,26 @@
     keep, send = call(
         functools.partial(kernel_grad_kernel, per_frame, late, skip),
         (shape((27 * chan_in, half), F32), shape((27 * chan_in, half), BF16)),
-        [place, stats, g_next, g_edge, next_edge, far(flat), far(g)],
+        [place, stats, g_next, g_edge, next_edge, flat, g],
         [
             pltpu.VMEM((3 * chan_in, frames * cells), BF16),
             pltpu.VMEM((frames + 2, rows + 2, cols, chan_out), BF16),
-            pltpu.VMEM(flat.shape, BF16),
-            pltpu.VMEM(g.shape, BF16),
-            pltpu.SemaphoreType.DMA((frames + 1,)),
         ],
         scalars=1,
-        far=2,
     )
+    send, x_prev, prev_edge, hold = together(send, x_prev, prev_edge, stats)
     recv = swap(send, "width", 1)
-    send, x_last, x_rows = together(send, x_last, x_rows)
-    x_prev = lax.ppermute(x_last, "tm", [(i, (i + 1) % tm) for i in range(tm)])
-    turn = [(i * width + c, (i + 1) % tm * width + (c ^ 1)) for i in range(tm) for c in range(width)]
-    prev_edge = lax.ppermute(x_rows[frames - 2 :], ("tm", "width"), turn)
-
-    def own(g):
-        return call(
-            own_grad_kernel,
-            shape((frames, rows, cols, 3 * chan_in), F32),
-            [g, weight],
-            [pltpu.VMEM((frames, rows + 2, cols, chan_out), BF16)],
-        )
-
-    def gains(stats, own_grad):
-        return call(
-            functools.partial(gain_kernel, per_frame),
-            shape((2, chan_in), F32),
-            [place, stats, flat, own_grad, g_next, g_edge, next_edge, weight],
-            [
-                pltpu.VMEM((2, rows + 2, cols, chan_out), BF16),
-                pltpu.VMEM((frames, rows, cols, 3 * chan_in), F32),
-            ],
-            scalars=1,
-        )
+    local = call(
+        functools.partial(gain_kernel, per_frame),
+        shape((2, chan_in), F32),
+        [place, hold, flat, own_grad, g_next, g_edge, next_edge, weight],
+        [
+            pltpu.VMEM((2, rows + 2, cols, chan_out), BF16),
+            pltpu.VMEM((frames, rows, cols, 3 * chan_in), F32),
+        ],
+        scalars=1,
+    )
+    recv, local = together(recv, local)
 
     def outputs(hold):
         return call(
@@ -496,7 +489,7 @@
         for step in bits_of("tm"):
             one, send = parted(one, "tm", step)
             one = one + swap(send, "tm", step).astype(F32)
-        rider = all_sum(gains(stats, own(g)), ("width", "dp", "tm"))
+        rider = all_sum(local, ("width", "dp", "tm"))
         grad_weight = one[0]
     else:
         rest = share // 3
@@ -512,12 +505,10 @@
             [place, keep, recv],
             scalars=1,
         )
-        send1, hold, x_prev, prev_edge, g, *send2 = together(send1, stats, x_prev, prev_edge, g, *send2)
+        rider = local + swap(local, "width", 1)
+        send1, hold, rider, *send2 = together(send1, hold, rider, *send2)
         recv1 = swap(send1, "dp", 1)
         recv2 = [swap(v, "tm", k) for k, v in zip(OTHERS, send2)]
-        rider = gains(hold, own(g))
-        rider = rider + swap(rider, "width", 1)
-        rider, hold = together(rider, hold)
         got = swap(rider, "dp", 1)
         recv1, got, *recv2 = together(recv1, got, *recv2)
         stay1, *send1, stay2, send2, rider = call(

time: 58.2 us -> 53.5 us (0.919)
  waiting for transfers between devices: 19.6 us -> 16.1 us
  Pallas kernels: 16.9 us -> 15.3 us
  local copies, waits for them, and re-layouts: 0.98 us -> 2.46 us
  other arithmetic: 0.77 us -> 0.1 us
    ppermute x1, waiting for transfers between devices: 6.28 us -> 2.72 us  [body(): g_next = lax.ppermute(g_first, 'tm', down).reshape(2, rows, cols, chan_out)]
    ppermute x1, waiting for transfers between devices: 4.71 us -> 2.73 us  [body(): prev_edge = lax.ppermute(x_rows[frames - 2:], ('tm', 'width'), turn)]
    ppermute x17, waiting for transfers between devices: 8.36 us -> 10.2 us  [swap(): lax.ppermute(value, axis, [(i, i ^ step) for i in range(lax.axis_size(axi...]
    pallas_call x9, Pallas kernels: 16.9 us -> 15.3 us  [call(): pl.pallas_call(kernel, out_shape=out_shape, in_specs=[SMEM] * scalars + [...]
    unnamed x6 -> x8, local copies, waits for them, and re-layouts: 0.01 us -> 1.49 us
    ppermute x1, starting transfers between devices: 1.34 us -> 0.01 us  [body(): prev_edge = lax.ppermute(x_rows[frames - 2:], ('tm', 'width'), turn)]
    ppermute x1, starting transfers between devices: 0.89 us -> 1.65 us  [body(): x_prev = lax.ppermute(x_last, 'tm', [(i, (i + 1) % tm) for i in range(tm)])]
    broadcast_in_dim x1, other arithmetic: 0.68 us -> 0.01 us  [body(): jnp.pad(jnp.stack([gain, bias]), ((0, 2 * frames - 2), (0, 0)))[None]]
  transfers between devices with their start and end apart: 20 -> 20, of which waited for: 10 -> 13; matrix products, arithmetic and copies ran while one was open for 1% -> 0% of each run, Pallas kernels for 19% -> 26%
where the time goes in v4:
time: 53.5 us; the launch traced here: 53.3 us
  starting transfers between devices  18.5 us (35%)
  waiting for transfers between devices  16.1 us (30%)
  Pallas kernels  15.3 us (29%)
  local copies, waits for them, and re-layouts  2.46 us (5%)
  between operations  0.73 us (1%)
    ppermute x17, starting transfers between devices, swap(): lax.ppermute(value, axis, [(i, i ^ step) for i in range(lax.axis_size(axi...  15.6 us
    pallas_call x9, Pallas kernels, call(): pl.pallas_call(kernel, out_shape=out_shape, in_specs=[SMEM] * scalars + [...  15.3 us
    ppermute x17, waiting for transfers between devices, swap(): lax.ppermute(value, axis, [(i, i ^ step) for i in range(lax.axis_size(axi...  10.2 us
    ppermute x1, waiting for transfers between devices, body(): prev_edge = lax.ppermute(x_rows[frames - 2:], ('tm', 'width'), turn)  2.73 us
    ppermute x1, waiting for transfers between devices, body(): g_next = lax.ppermute(g_first, 'tm', down).reshape(2, rows, cols, chan_out)  2.72 us
    ppermute x1, starting transfers between devices, body(): x_prev = lax.ppermute(x_last, 'tm', [(i, (i + 1) % tm) for i in range(tm)])  1.65 us
    unnamed x8, local copies, waits for them, and re-layouts  1.49 us
    ppermute x1, starting transfers between devices, body(): g_next = lax.ppermute(g_first, 'tm', down).reshape(2, rows, cols, chan_out)  1.29 us
  transfers between devices with their start and end apart: 20, of which 13 were waited for; matrix products, arithmetic and copies ran while one was open for 0% of the time, Pallas kernels for 26%

profile of v4, /device:TPU:0, one launch (start us, length us, event | category | flops | bytes accessed | tf_op | source)
XLA Modules:
  0.0 53.3 jit_solution(1675471994706355448)
XLA Ops:
  0.6 0.1 pad_add_fusion.place
  0.7 1.0 %slice.9 = bf16[2,4,64,256]{3,2,1,0:T(8,128)(2,1)S(1)} slice(bf16[4,4,64,256]{3,2,1,0:T(8,128)(2,1)} %bitcast.21), slice={[0:2], [0:4], [0:64], [0:256]} | slice | bytes 524288 | tf_op jit(solution)/shard_map/slice | solution.py:390
  1.7 1.3 %collective-permute-start.1 = (bf16[2,256,256]{2,1,0:T(8,128)(2,1)S(1)}, bf16[2,256,256]{2,1,0:T(8,128)(2,1)S(1)}, u32[]{:S(2)}, u32[]{:S(2)}) collective-permute-start(bf16[2,256,256]{2,1,0:T(8,128)(2,1)S(1)} %bitcast.24), channel_id=1, source_target_pairs={{4,0},{8,4},{12,8},{5,1},{9,5},{13,9},{6,2},{10,6},{14,10},{7,3},{... | collective-permute-start | bytes 786440 | tf_op jit(solution)/shard_map/ppermute | solution.py:392
  3.0 1.8 %shard_map.84 = (f32[8,128]{1,0:T(8,128)S(1)}, bf16[2,4,64,128]{3,2,1,0:T(8,128)(2,1)S(1)}, bf16[4,64,256]{2,1,0:T(8,128)(2,1)S(1)}, bf16[4,64,128]{2,1,0:T(8,12...) custom-call(s32[3]{0:T(128)S(1)} %pad_add_fusion.place, ...), custom_call_target="tpu_custom_call" | custom-call | bytes 1904652 | tf_op jit(solution)/shard_map/pallas_call | solution.py:21
  4.8 0.5 collective-permute-start.2
  5.3 0.1 collective-permute-start.3
  5.4 0.4 collective-permute-start
  5.8 0.8 %collective-permute-done = f32[8,128]{1,0:T(8,128)S(1)} collective-permute-done((f32[8,128]{1,0:T(8,128)S(1)}, f32[8,128]{1,0:T(8,128)S(1)}, u32[]{:S(2)}, u32[]{:S(2)}) %collective-permute-start) | collective-permute-done | bytes 4128 | tf_op jit(solution)/shard_map/ppermute | solution.py:351
  6.7 0.0 copy-start
  6.7 1.5 %copy-done = bf16[3456,256]{1,0:T(8,128)(2,1)S(1)} copy-done((bf16[3456,256]{1,0:T(8,128)(2,1)S(1)}, bf16[3456,256]{1,0:T(8,128)(2,1)}, u32[]{:S(2)}) %copy-start) | copy-done | bytes 1769496
  8.2 0.0 copy-start.2
  8.2 0.0 copy-start.3
  8.2 0.0 copy-start.1
  8.2 2.0 %shard_map.85.own_ref = f32[4,4,64,384]{3,2,1,0:T(8,128)S(1)} custom-call(bf16[4,4,64,256]{3,2,1,0:T(8,128)(2,1)S(1)} %get-tuple-element.77.g_ref, bf16[3456,256]{1,0:T(8,128)(2,1)S(1)} %copy-done), custom_call_target="tpu_custom_call" | custom-call | bytes 3866624 | tf_op jit(solution)/shard_map/pallas_call | solution.py:21
  10.2 0.0 collective-permute-done.3.edge_ref
  10.2 0.0 collective-permute-done.2.edge_ref
  10.2 2.7 %collective-permute-done.1 = bf16[2,256,256]{2,1,0:T(8,128)(2,1)S(1)} collective-permute-done((bf16[2,256,256]{2,1,0:T(8,128)(2,1)S(1)}, bf16[2,256,256]{2,1,0:T(8,128)(2,1)S(1)}, u32[]{:S(2)}, u32[]{:S(2)}) %collective-permute-start.1) | collective-permute-done | bytes 262176 | tf_op jit(solution)/shard_map/ppermute | solution.py:392
  12.9 1.7 %collective-permute-start.4 = (f32[1,8,128]{2,1,0:T(8,128)S(1)}, f32[1,8,128]{2,1,0:T(8,128)S(1)}, u32[]{:S(2)}, u32[]{:S(2)}) collective-permute-start(f32[1,8,128]{2,1,0:T(8,128)S(1)} %bitcast.26), channel_id=1, source_target_pairs={{0,4},{4,0},{8,12},{12,8},{1,5},{5,1},{9,13},{13,9},{2,6},{6,2},{1... | collective-permute-start | bytes 12296 | tf_op jit(solution)/shard_map/ppermute | solution.py:351
  14.6 1.9 %collective-permute-done.4 = f32[1,8,128]{2,1,0:T(8,128)S(1)} collective-permute-done((f32[1,8,128]{2,1,0:T(8,128)S(1)}, f32[1,8,128]{2,1,0:T(8,128)S(1)}, u32[]{:S(2)}, u32[]{:S(2)}) %collective-permute-start.4) | collective-permute-done | bytes 4128 | tf_op jit(solution)/shard_map/ppermute | solution.py:351
  16.5 2.7 %collective-permute-start.5 = (f32[2,8,128]{2,1,0:T(8,128)S(1)}, f32[2,8,128]{2,1,0:T(8,128)S(1)}, u32[]{:S(2)}, u32[]{:S(2)}) collective-permute-start(f32[2,8,128]{2,1,0:T(8,128)S(1)} %pad_maximum_fusion.1), channel_id=1, source_target_pairs={{0,8},{4,12},{8,0},{12,4},{1,9},{5,13},{9,1},{13,5},{2,10},{6,14},... | collective-permute-start | bytes 24584 | tf_op jit(solution)/shard_map/ppermute | solution.py:351
  19.3 0.0 copy-done.2
  19.3 0.0 copy-done.3
  19.3 0.6 %shard_map.86 = bf16[2,64,256]{2,1,0:T(8,128)(2,1)S(1)} custom-call(s32[3]{0:T(128)S(1)} %pad_add_fusion.place, bf16[2,4,64,256]{3,2,1,0:T(8,128)(2,1)S(1)} %bitcast.18), custom_call_target="tpu_custom_call" | custom-call | bytes 327692 | tf_op jit(solution)/shard_map/pallas_call | solution.py:21
  19.8 0.1 collective-permute-start.6
  19.9 1.1 %collective-permute-done.5 = f32[2,8,128]{2,1,0:T(8,128)S(1)} collective-permute-done((f32[2,8,128]{2,1,0:T(8,128)S(1)}, f32[2,8,128]{2,1,0:T(8,128)S(1)}, u32[]{:S(2)}, u32[]{:S(2)}) %collective-permute-start.5) | collective-permute-done | bytes 8224 | tf_op jit(solution)/shard_map/ppermute | solution.py:351
  21.1 0.1 collective-permute-done.6.edge_next
  21.2 1.6 %collective-permute-start.7 = (bf16[2,4,64,128]{3,2,1,0:T(8,128)(2,1)S(1)}, bf16[2,4,64,128]{3,2,1,0:T(8,128)(2,1)S(1)}, u32[]{:S(2)}, u32[]{:S(2)}) collective-permute-start(bf16[2,4,64,128]{3,2,1,0:T(8,128)(2,1)S(1)} %get-tuple-element.87), channel_id=1, source_target_pairs={{0,4},{4,8},{8,12},{12,0},{1,5},{5,9},{9,13},{13,1},{2,6},{6,10},{... | collective-permute-start | bytes 393224 | tf_op jit(solution)/shard_map/ppermute | solution.py:432
  22.8 0.0 collective-permute-start.8
  22.8 2.9 %shard_map.87 = (f32[3456,128]{1,0:T(8,128)S(1)}, bf16[3456,128]{1,0:T(8,128)(2,1)S(1)}) custom-call(s32[3]{0:T(128)S(1)} %pad_add_fusion.place, f32[5,8,128]{2,1,0:T(8,128)S(1)} %pad_maximum_fusion.stats_ref, bf16[2,4,64,256]{3,2,1,0:T(8,128)(2,1)S(1)} %bitcast.19, bf16[4,64,256]{2,1,0:T(8,128)(2,1)S(1)} %collective-permute-done.2.edge_ref, ...), custom_call_target="tpu_custom_call" | custom-call | bytes 3919884 | tf_op jit(solution)/shard_map/pallas_call | solution.py:21
  25.7 2.7 %collective-permute-done.8.prev_edge = bf16[2,64,128]{2,1,0:T(8,128)(2,1)S(1)} collective-permute-done((bf16[2,64,128]{2,1,0:T(8,128)(2,1)S(1)}, bf16[2,64,128]{2,1,0:T(8,128)(2,1)S(1)}, u32[]{:S(2)}, u32[]{:S(2)}) %collective-permute-start.8) | collective-permute-done | bytes 32800 | tf_op jit(solution)/shard_map/ppermute | solution.py:434
  28.4 0.4 collective-permute-done.7.prev_ref
  28.9 0.2 collective-permute-start.9
  29.1 0.0 copy-done.1
  29.1 1.8 %shard_map.88 = f32[2,128]{1,0:T(2,128)S(1)} custom-call(s32[3]{0:T(128)S(1)} %pad_add_fusion.place, f32[5,8,128]{2,1,0:T(8,128)S(1)} %pad_maximum_fusion.stats_ref, bf16[4,256,128]{2,1,0:T(8,128)(2,1)S(1)} %bitcast.17, f32[4,4,64,384]{3,2,1,0:T(8,128)S(1)} %shard_map.85.own_ref, bf16[2,4,64,256]{3,2,1,0:T(8,128)(2,1)S(1)} %bitcast.20, ...), custom_call_target="tpu_custom_call" | custom-call | bytes 4084748 | tf_op jit(solution)/shard_map/pallas_call | solution.py:21
  30.9 0.4 collective-permute-done.9.recv_ref
  31.3 0.2 collective-permute-start.10
  31.5 0.7 %shard_map.89 = (f32[1152,128]{1,0:T(8,128)S(1)}, bf16[1152,128]{1,0:T(8,128)(2,1)S(1)}, f32[288,128]{1,0:T(8,128)S(1)}, bf16[288,128]{1,0:T(8,128)(2,1)S(1)}, b...) custom-call(s32[3]{0:T(128)S(1)} %pad_add_fusion.place, f32[3456,128]{1,0:T(8,128)S(1)} %get-tuple-element.85.keep_ref, ...), custom_call_target="tpu_custom_call" | custom-call | bytes 3907596 | tf_op jit(solution)/shard_map/pallas_call | solution.py:21
  32.2 0.2 collective-permute-done.10
  32.4 1.5 %collective-permute-start.11 = (bf16[1152,128]{1,0:T(8,128)(2,1)S(1)}, bf16[1152,128]{1,0:T(8,128)(2,1)S(1)}, u32[]{:S(2)}, u32[]{:S(2)}) collective-permute-start(bf16[1152,128]{1,0:T(8,128)(2,1)S(1)} %get-tuple-element.99), channel_id=1, source_target_pairs={{0,2},{2,0},{1,3},{3,1},{4,6},{6,4},{5,7},{7,5},{8,10},{10,8},{9,1... | collective-permute-start | bytes 884744 | tf_op jit(solution)/shard_map/ppermute | solution.py:351
  33.9 0.3 collective-permute-start.13
  34.2 1.6 %collective-permute-start.14 = (bf16[288,128]{1,0:T(8,128)(2,1)S(1)}, bf16[288,128]{1,0:T(8,128)(2,1)S(1)}, u32[]{:S(2)}, u32[]{:S(2)}) collective-permute-start(bf16[288,128]{1,0:T(8,128)(2,1)S(1)} %get-tuple-element.102), channel_id=1, source_target_pairs={{0,12},{4,8},{8,4},{12,0},{1,13},{5,9},{9,5},{13,1},{2,14},{6,10},... | collective-permute-start | bytes 221192 | tf_op jit(solution)/shard_map/ppermute | solution.py:351
  35.8 1.6 %collective-permute-start.15 = (bf16[288,128]{1,0:T(8,128)(2,1)S(1)}, bf16[288,128]{1,0:T(8,128)(2,1)S(1)}, u32[]{:S(2)}, u32[]{:S(2)}) collective-permute-start(bf16[288,128]{1,0:T(8,128)(2,1)S(1)} %get-tuple-element.103), channel_id=1, source_target_pairs={{0,4},{4,0},{8,12},{12,8},{1,5},{5,1},{9,13},{13,9},{2,6},{6,2},{1... | collective-permute-start | bytes 221192 | tf_op jit(solution)/shard_map/ppermute | solution.py:351
  37.4 0.5 %collective-permute-start.12 = (f32[2,128]{1,0:T(2,128)S(1)}, f32[2,128]{1,0:T(2,128)S(1)}, u32[]{:S(2)}, u32[]{:S(2)}) collective-permute-start(f32[2,128]{1,0:T(2,128)S(1)} %add.9.rider_ref), channel_id=1, source_target_pairs={{0,2},{2,0},{1,3},{3,1},{4,6},{6,4},{5,7},{7,5},{8,10},{10,8},{9,1... | collective-permute-start | bytes 3080 | tf_op jit(solution)/shard_map/ppermute | solution.py:351
  38.0 3.6 %collective-permute-done.12.got_ref = f32[2,128]{1,0:T(2,128)S(1)} collective-permute-done((f32[2,128]{1,0:T(2,128)S(1)}, f32[2,128]{1,0:T(2,128)S(1)}, u32[]{:S(2)}, u32[]{:S(2)}) %collective-permute-start.12) | collective-permute-done | bytes 1056 | tf_op jit(solution)/shard_map/ppermute | solution.py:351
  41.6 0.0 collective-permute-done.13.b_ref
  41.6 0.0 collective-permute-done.14.c_ref
  41.6 0.9 %collective-permute-done.15.a_ref = bf16[288,128]{1,0:T(8,128)(2,1)S(1)} collective-permute-done((bf16[288,128]{1,0:T(8,128)(2,1)S(1)}, bf16[288,128]{1,0:T(8,128)(2,1)S(1)}, u32[]{:S(2)}, u32[]{:S(2)}) %collective-permute-start.15) | collective-permute-done | bytes 73760 | tf_op jit(solution)/shard_map/ppermute | solution.py:351
  42.5 0.0 collective-permute-done.11.recv1_ref
  42.5 0.6 %shard_map.90 = (f32[288,128]{1,0:T(8,128)S(1)}, bf16[304,128]{1,0:T(8,128)(2,1)S(1)}, bf16[304,128]{1,0:T(8,128)(2,1)S(1)}, bf16[304,128]{1,0:T(8,128)(2,1)S(1)...) custom-call(s32[3]{0:T(128)S(1)} %pad_add_fusion.place, ...), custom_call_target="tpu_custom_call" | custom-call | bytes 1747980 | tf_op jit(solution)/shard_map/pallas_call | solution.py:21
  43.2 1.2 %collective-permute-start.17 = (bf16[304,128]{1,0:T(8,128)(2,1)S(1)}, bf16[304,128]{1,0:T(8,128)(2,1)S(1)}, u32[]{:S(2)}, u32[]{:S(2)}) collective-permute-start(bf16[304,128]{1,0:T(8,128)(2,1)S(1)} %get-tuple-element.120), channel_id=1, source_target_pairs={{0,8},{4,12},{8,0},{12,4},{1,9},{5,13},{9,1},{13,5},{2,10},{6,14},... | collective-permute-start | bytes 233480 | tf_op jit(solution)/shard_map/ppermute | solution.py:351
  44.4 2.2 %collective-permute-start.18 = (bf16[304,128]{1,0:T(8,128)(2,1)S(1)}, bf16[304,128]{1,0:T(8,128)(2,1)S(1)}, u32[]{:S(2)}, u32[]{:S(2)}) collective-permute-start(bf16[304,128]{1,0:T(8,128)(2,1)S(1)} %get-tuple-element.121), channel_id=1, source_target_pairs={{0,12},{4,8},{8,4},{12,0},{1,13},{5,9},{9,5},{13,1},{2,14},{6,10},... | collective-permute-start | bytes 233480 | tf_op jit(solution)/shard_map/ppermute | solution.py:351
  46.5 0.2 collective-permute-start.19
  46.7 0.6 %collective-permute-start.16 = (bf16[144,128]{1,0:T(8,128)(2,1)S(1)}, bf16[144,128]{1,0:T(8,128)(2,1)S(1)}, u32[]{:S(2)}, u32[]{:S(2)}) collective-permute-start(bf16[144,128]{1,0:T(8,128)(2,1)S(1)} %get-tuple-element.115), channel_id=1, source_target_pairs={{0,2},{2,0},{1,3},{3,1},{4,6},{6,4},{5,7},{7,5},{8,10},{10,8},{9,1... | collective-permute-start | bytes 110600 | tf_op jit(solution)/shard_map/ppermute | solution.py:351
  47.3 4.2 %shard_map.91 = bf16[1024,256]{1,0:T(8,128)(2,1)} custom-call(s32[3]{0:T(128)S(1)} %pad_add_fusion.place, f32[5,8,128]{2,1,0:T(8,128)S(1)} %pad_maximum_fusion.stats_ref, bf16[4,4,64,128]{3,2,1,0:T(8,128)(2,1)S(1)} %get-tuple-element.84.x_ref, bf16[2,4,64,128]{3,2,1,0:T(8,128)(2,1)S(1)} %collective-permute-done.7.prev_ref, ...), custom_call_target="tpu_custom_call" | custom-call | bytes 2805772 | tf_op jit(solution)/shard_map/pallas_call | solution.py:21
  51.5 0.0 collective-permute-done.16.recv2_ref
  51.5 0.7 %collective-permute-done.17.b_ref = bf16[304,128]{1,0:T(8,128)(2,1)S(1)} collective-permute-done((bf16[304,128]{1,0:T(8,128)(2,1)S(1)}, bf16[304,128]{1,0:T(8,128)(2,1)S(1)}, u32[]{:S(2)}, u32[]{:S(2)}) %collective-permute-start.17) | collective-permute-done | bytes 77856 | tf_op jit(solution)/shard_map/ppermute | solution.py:351
  52.2 0.0 collective-permute-done.18.c_ref
  52.2 0.3 collective-permute-done.19.a_ref
  52.5 0.7 %shard_map.92 = (f32[432,128]{1,0:T(8,128)}, f32[1,128]{1,0:T(1,128)}, f32[1,128]{1,0:T(1,128)}) custom-call(f32[288,128]{1,0:T(8,128)S(1)} %get-tuple-element.124.stay1_ref, bf16[304,128]{1,0:T(8,128)(2,1)S(1)} %collective-permute-done.17.b_ref, bf16[304,128]{1,0:T(8,128)(2,1)S(1)} %collective-permute-done.18.c_ref, ...), custom_call_target="tpu_custom_call" | custom-call | bytes 714752 | tf_op jit(solution)/shard_map/pallas_call | solution.py:21
  (6 shorter events, 0.0 us)
Async XLA Ops:
  1.7 11.2 %collective-permute-start.1 = (bf16[2,256,256]{2,1,0:T(8,128)(2,1)S(1)}, bf16[2,256,256]{2,1,0:T(8,128)(2,1)S(1)}, u32[]{:S(2)}, u32[]{:S(2)}) collective-permute-start(bf16[2,256,256]{2,1,0:T(8,128)(2,1)S(1)} %bitcast.24), channel_id=1, source_target_pairs={{4,0},{8,4},{12,8},{5,1},{9,5},{13,9},{6,2},{10,6},{14,10},{7,3},{... | collective-permute-start | bytes 786440 | tf_op jit(solution)/shard_map/ppermute | solution.py:392
  4.8 5.4 %collective-permute-start.2 = (bf16[4,64,256]{2,1,0:T(8,128)(2,1)S(1)}, bf16[4,64,256]{2,1,0:T(8,128)(2,1)S(1)}, u32[]{:S(2)}, u32[]{:S(2)}) collective-permute-start(bf16[4,64,256]{2,1,0:T(8,128)(2,1)S(1)} %get-tuple-element.75), channel_id=1, source_target_pairs={{0,1},{1,0},{2,3},{3,2},{4,5},{5,4},{6,7},{7,6},{8,9},{9,8},{10,11... | collective-permute-start | bytes 393224 | tf_op jit(solution)/shard_map/ppermute | solution.py:351
  5.3 4.8 %collective-permute-start.3 = (bf16[4,64,128]{2,1,0:T(8,128)(2,1)S(1)}, bf16[4,64,128]{2,1,0:T(8,128)(2,1)S(1)}, u32[]{:S(2)}, u32[]{:S(2)}) collective-permute-start(bf16[4,64,128]{2,1,0:T(8,128)(2,1)S(1)} %get-tuple-element.88), channel_id=1, source_target_pairs={{0,1},{1,0},{2,3},{3,2},{4,5},{5,4},{6,7},{7,6},{8,9},{9,8},{10,11... | collective-permute-start | bytes 196616 | tf_op jit(solution)/shard_map/ppermute | solution.py:351
  5.4 1.3 %collective-permute-start = (f32[8,128]{1,0:T(8,128)S(1)}, f32[8,128]{1,0:T(8,128)S(1)}, u32[]{:S(2)}, u32[]{:S(2)}) collective-permute-start(f32[8,128]{1,0:T(8,128)S(1)} %get-tuple-element.72), channel_id=1, source_target_pairs={{0,1},{1,0},{2,3},{3,2},{4,5},{5,4},{6,7},{7,6},{8,9},{9,8},{10,11... | collective-permute-start | bytes 12296 | tf_op jit(solution)/shard_map/ppermute | solution.py:351
  6.7 1.5 %copy-start = (bf16[3456,256]{1,0:T(8,128)(2,1)S(1)}, bf16[3456,256]{1,0:T(8,128)(2,1)}, u32[]{:S(2)}) copy-start(bf16[3456,256]{1,0:T(8,128)(2,1)} %w_ref.5) | copy-start | bytes 5308420
  8.2 11.1 %copy-start.2 = (f32[128]{0:T(128)S(1)}, f32[128]{0:T(128)}, u32[]{:S(2)}) copy-start(f32[128]{0:T(128)} %param.7) | copy-start | bytes 1540
  8.2 11.1 %copy-start.3 = (f32[128]{0:T(128)S(1)}, f32[128]{0:T(128)}, u32[]{:S(2)}) copy-start(f32[128]{0:T(128)} %param.6) | copy-start | bytes 1540
  8.2 20.9 %copy-start.1 = (bf16[3456,256]{1,0:T(8,128)(2,1)S(1)}, bf16[3456,256]{1,0:T(8,128)(2,1)}, u32[]{:S(2)}) copy-start(bf16[3456,256]{1,0:T(8,128)(2,1)} %w_ref.5) | copy-start | bytes 5308420
  12.9 3.6 %collective-permute-start.4 = (f32[1,8,128]{2,1,0:T(8,128)S(1)}, f32[1,8,128]{2,1,0:T(8,128)S(1)}, u32[]{:S(2)}, u32[]{:S(2)}) collective-permute-start(f32[1,8,128]{2,1,0:T(8,128)S(1)} %bitcast.26), channel_id=1, source_target_pairs={{0,4},{4,0},{8,12},{12,8},{1,5},{5,1},{9,13},{13,9},{2,6},{6,2},{1... | collective-permute-start | bytes 12296 | tf_op jit(solution)/shard_map/ppermute | solution.py:351
  16.5 4.5 %collective-permute-start.5 = (f32[2,8,128]{2,1,0:T(8,128)S(1)}, f32[2,8,128]{2,1,0:T(8,128)S(1)}, u32[]{:S(2)}, u32[]{:S(2)}) collective-permute-start(f32[2,8,128]{2,1,0:T(8,128)S(1)} %pad_maximum_fusion.1), channel_id=1, source_target_pairs={{0,8},{4,12},{8,0},{12,4},{1,9},{5,13},{9,1},{13,5},{2,10},{6,14},... | collective-permute-start | bytes 24584 | tf_op jit(solution)/shard_map/ppermute | solution.py:351
  19.8 1.3 %collective-permute-start.6 = (bf16[2,64,256]{2,1,0:T(8,128)(2,1)S(1)}, bf16[2,64,256]{2,1,0:T(8,128)(2,1)S(1)}, u32[]{:S(2)}, u32[]{:S(2)}) collective-permute-start(bf16[2,64,256]{2,1,0:T(8,128)(2,1)S(1)} %shard_map.86), channel_id=1, source_target_pairs={{0,1},{1,0},{2,3},{3,2},{4,5},{5,4},{6,7},{7,6},{8,9},{9,8},{10,11... | collective-permute-start | bytes 196616 | tf_op jit(solution)/shard_map/ppermute | solution.py:351
  21.2 7.7 %collective-permute-start.7 = (bf16[2,4,64,128]{3,2,1,0:T(8,128)(2,1)S(1)}, bf16[2,4,64,128]{3,2,1,0:T(8,128)(2,1)S(1)}, u32[]{:S(2)}, u32[]{:S(2)}) collective-permute-start(bf16[2,4,64,128]{3,2,1,0:T(8,128)(2,1)S(1)} %get-tuple-element.87), channel_id=1, source_target_pairs={{0,4},{4,8},{8,12},{12,0},{1,5},{5,9},{9,13},{13,1},{2,6},{6,10},{... | collective-permute-start | bytes 393224 | tf_op jit(solution)/shard_map/ppermute | solution.py:432
  22.8 5.6 %collective-permute-start.8 = (bf16[2,64,128]{2,1,0:T(8,128)(2,1)S(1)}, bf16[2,64,128]{2,1,0:T(8,128)(2,1)S(1)}, u32[]{:S(2)}, u32[]{:S(2)}) collective-permute-start(bf16[2,64,128]{2,1,0:T(8,128)(2,1)S(1)} %slice.11), channel_id=1, source_target_pairs={{0,5},{1,4},{4,9},{5,8},{8,13},{9,12},{12,1},{13,0},{2,7},{3,6},{6... | collective-permute-start | bytes 98312 | tf_op jit(solution)/shard_map/ppermute | solution.py:434
  28.9 2.4 %collective-permute-start.9 = (bf16[3456,128]{1,0:T(8,128)(2,1)S(1)}, bf16[3456,128]{1,0:T(8,128)(2,1)S(1)}, u32[]{:S(2)}, u32[]{:S(2)}) collective-permute-start(bf16[3456,128]{1,0:T(8,128)(2,1)S(1)} %get-tuple-element.89), channel_id=1, source_target_pairs={{0,1},{1,0},{2,3},{3,2},{4,5},{5,4},{6,7},{7,6},{8,9},{9,8},{10,11... | collective-permute-start | bytes 2654216 | tf_op jit(solution)/shard_map/ppermute | solution.py:351
  31.3 1.1 %collective-permute-start.10 = (f32[2,128]{1,0:T(2,128)S(1)}, f32[2,128]{1,0:T(2,128)S(1)}, u32[]{:S(2)}, u32[]{:S(2)}) collective-permute-start(f32[2,128]{1,0:T(2,128)S(1)} %shard_map.88), channel_id=1, source_target_pairs={{0,1},{1,0},{2,3},{3,2},{4,5},{5,4},{6,7},{7,6},{8,9},{9,8},{10,11... | collective-permute-start | bytes 3080 | tf_op jit(solution)/shard_map/ppermute | solution.py:351
  32.4 10.1 %collective-permute-start.11 = (bf16[1152,128]{1,0:T(8,128)(2,1)S(1)}, bf16[1152,128]{1,0:T(8,128)(2,1)S(1)}, u32[]{:S(2)}, u32[]{:S(2)}) collective-permute-start(bf16[1152,128]{1,0:T(8,128)(2,1)S(1)} %get-tuple-element.99), channel_id=1, source_target_pairs={{0,2},{2,0},{1,3},{3,1},{4,6},{6,4},{5,7},{7,5},{8,10},{10,8},{9,1... | collective-permute-start | bytes 884744 | tf_op jit(solution)/shard_map/ppermute | solution.py:351
  33.9 7.7 %collective-permute-start.13 = (bf16[288,128]{1,0:T(8,128)(2,1)S(1)}, bf16[288,128]{1,0:T(8,128)(2,1)S(1)}, u32[]{:S(2)}, u32[]{:S(2)}) collective-permute-start(bf16[288,128]{1,0:T(8,128)(2,1)S(1)} %get-tuple-element.101), channel_id=1, source_target_pairs={{0,8},{4,12},{8,0},{12,4},{1,9},{5,13},{9,1},{13,5},{2,10},{6,14},... | collective-permute-start | bytes 221192 | tf_op jit(solution)/shard_map/ppermute | solution.py:351
  34.2 7.4 %collective-permute-start.14 = (bf16[288,128]{1,0:T(8,128)(2,1)S(1)}, bf16[288,128]{1,0:T(8,128)(2,1)S(1)}, u32[]{:S(2)}, u32[]{:S(2)}) collective-permute-start(bf16[288,128]{1,0:T(8,128)(2,1)S(1)} %get-tuple-element.102), channel_id=1, source_target_pairs={{0,12},{4,8},{8,4},{12,0},{1,13},{5,9},{9,5},{13,1},{2,14},{6,10},... | collective-permute-start | bytes 221192 | tf_op jit(solution)/shard_map/ppermute | solution.py:351
  35.8 6.8 %collective-permute-start.15 = (bf16[288,128]{1,0:T(8,128)(2,1)S(1)}, bf16[288,128]{1,0:T(8,128)(2,1)S(1)}, u32[]{:S(2)}, u32[]{:S(2)}) collective-permute-start(bf16[288,128]{1,0:T(8,128)(2,1)S(1)} %get-tuple-element.103), channel_id=1, source_target_pairs={{0,4},{4,0},{8,12},{12,8},{1,5},{5,1},{9,13},{13,9},{2,6},{6,2},{1... | collective-permute-start | bytes 221192 | tf_op jit(solution)/shard_map/ppermute | solution.py:351
  37.4 4.2 %collective-permute-start.12 = (f32[2,128]{1,0:T(2,128)S(1)}, f32[2,128]{1,0:T(2,128)S(1)}, u32[]{:S(2)}, u32[]{:S(2)}) collective-permute-start(f32[2,128]{1,0:T(2,128)S(1)} %add.9.rider_ref), channel_id=1, source_target_pairs={{0,2},{2,0},{1,3},{3,1},{4,6},{6,4},{5,7},{7,5},{8,10},{10,8},{9,1... | collective-permute-start | bytes 3080 | tf_op jit(solution)/shard_map/ppermute | solution.py:351
  43.2 9.0 %collective-permute-start.17 = (bf16[304,128]{1,0:T(8,128)(2,1)S(1)}, bf16[304,128]{1,0:T(8,128)(2,1)S(1)}, u32[]{:S(2)}, u32[]{:S(2)}) collective-permute-start(bf16[304,128]{1,0:T(8,128)(2,1)S(1)} %get-tuple-element.120), channel_id=1, source_target_pairs={{0,8},{4,12},{8,0},{12,4},{1,9},{5,13},{9,1},{13,5},{2,10},{6,14},... | collective-permute-start | bytes 233480 | tf_op jit(solution)/shard_map/ppermute | solution.py:351
  44.4 7.8 %collective-permute-start.18 = (bf16[304,128]{1,0:T(8,128)(2,1)S(1)}, bf16[304,128]{1,0:T(8,128)(2,1)S(1)}, u32[]{:S(2)}, u32[]{:S(2)}) collective-permute-start(bf16[304,128]{1,0:T(8,128)(2,1)S(1)} %get-tuple-element.121), channel_id=1, source_target_pairs={{0,12},{4,8},{8,4},{12,0},{1,13},{5,9},{9,5},{13,1},{2,14},{6,10},... | collective-permute-start | bytes 233480 | tf_op jit(solution)/shard_map/ppermute | solution.py:351
  46.5 6.0 %collective-permute-start.19 = (bf16[304,128]{1,0:T(8,128)(2,1)S(1)}, bf16[304,128]{1,0:T(8,128)(2,1)S(1)}, u32[]{:S(2)}, u32[]{:S(2)}) collective-permute-start(bf16[304,128]{1,0:T(8,128)(2,1)S(1)} %get-tuple-element.122), channel_id=1, source_target_pairs={{0,4},{4,0},{8,12},{12,8},{1,5},{5,1},{9,13},{13,9},{2,6},{6,2},{1... | collective-permute-start | bytes 233480 | tf_op jit(solution)/shard_map/ppermute | solution.py:351
  46.7 4.8 %collective-permute-start.16 = (bf16[144,128]{1,0:T(8,128)(2,1)S(1)}, bf16[144,128]{1,0:T(8,128)(2,1)S(1)}, u32[]{:S(2)}, u32[]{:S(2)}) collective-permute-start(bf16[144,128]{1,0:T(8,128)(2,1)S(1)} %get-tuple-element.115), channel_id=1, source_target_pairs={{0,2},{2,0},{1,3},{3,1},{4,6},{6,4},{5,7},{7,5},{8,10},{10,8},{9,1... | collective-permute-start | bytes 110600 | tf_op jit(solution)/shard_map/ppermute | solution.py:351

commit v5 on v4

--- a/solution.py
+++ b/solution.py
@@ -45,7 +45,7 @@
     return rows
 
 
-def prepare_kernel(per_group, place, x_hbm, g_hbm, sums_ref, last_ref, row_ref, x_row_ref, x_ref, g_ref, sems):
+def prepare_kernel(per_group, place, x_hbm, g_hbm, sums_ref, odd_ref, even_ref, row_ref, x_row_ref, x_ref, g_ref, sems):
     frames, rows, cols, chan_in = x_ref.shape
     row = jnp.where(place[1] == 0, rows - 1, 0)
     copies = [pltpu.make_async_copy(x_hbm.at[t], x_ref.at[t], sems.at[t]) for t in range(frames)]
@@ -59,21 +59,28 @@
         firsts.append(jnp.sum(v, axis=0, keepdims=True))
         squares.append(jnp.sum(v * v, axis=0, keepdims=True))
         x_row_ref[t] = x_ref[t, row]
-    last_ref[...] = x_ref[frames - 2 :]
     sums_ref[...] = group_sum(jnp.concatenate(firsts + squares, axis=0), per_group)
     for t in range(frames):
         copies[frames + t].wait()
         row_ref[t] = g_ref[t, row]
-
-
-def edge_kernel(place, first_ref, *rest):
-    o_ref = rest[-1]
-    row = jnp.where(place[1] == 0, first_ref.shape[1] - 1, 0)
-    at = 0
-    for ref in (first_ref,) + rest[:-1]:
-        for t in range(ref.shape[0]):
-            o_ref[at + t] = ref[t, row]
-        at += ref.shape[0]
+    even = jnp.bitwise_and(place[0], 1) == 0
+    for t in range(2):
+        clip, low = x_ref[frames - 2 + t], g_ref[t, :, :, :chan_in]
+        odd_ref[t, :, :, :chan_in] = jnp.where(even, clip, low)
+        even_ref[t, :, :, :chan_in] = jnp.where(even, low, clip)
+        odd_ref[t, :, :, chan_in:] = g_ref[t, :, :, chan_in:]
+        even_ref[t, :, :, chan_in:] = g_ref[t, :, :, chan_in:]
+
+
+def arrived_kernel(place, odd_ref, even_ref, next_ref, prev_ref, edge_ref):
+    chan_in, chan_out = prev_ref.shape[3], next_ref.shape[3]
+    even = jnp.bitwise_and(place[0], 1) == 0
+    row = jnp.where(place[1] == 0, next_ref.shape[1] - 1, 0)
+    for t in range(2):
+        next_ref[t] = jnp.where(even, odd_ref[t], even_ref[t])
+        prev_ref[t] = jnp.where(even, even_ref[t, :, :, :chan_in], odd_ref[t, :, :, :chan_in])
+        edge_ref[t, :, :chan_out] = next_ref[t, row]
+        edge_ref[t, :, chan_out:] = prev_ref[t, row]
 
 
 def frame_stats(place, stats_ref, frames, per_frame):
@@ -148,7 +155,7 @@
     chan_in = x_ref.shape[2]
     cells = rows * cols
     core = place[1]
-    pad_rows(core, next_ref[...], edge_next[...], gp_ref)
+    pad_rows(core, next_ref[...], edge_next[:, :, :chan_out], gp_ref)
     z_ref[...] = own_ref[...]
     for a in range(2):
         n = 2 - a
@@ -192,7 +199,7 @@
     rows, cols, chan_out = g_ref.shape[1:]
     core = place[1]
     pad_rows(core, g_ref[...], edge_ref[...], gp_ref.at[:frames])
-    pad_rows(core, next_ref[...], edge_next[...], gp_ref.at[frames:])
+    pad_rows(core, next_ref[...], edge_next[:, :, :chan_out], gp_ref.at[frames:])
     means, inverses = frame_stats(place, stats_ref, frames, per_frame)
     affine = stats_ref[stats_ref.shape[0] - 1]
     gain, bias = affine[:1], affine[1:2]
@@ -228,11 +235,10 @@
                     send_ref[at : at + end - begin] = send[begin:end]
 
 
-def output_kernel(
-    per_frame, place, stats_ref, x_ref, prev_ref, edge_ref, prev_edge, w_ref, o_ref, h_ref, acc_ref
+def hidden_kernel(
+    per_frame, place, stats_ref, x_ref, prev_ref, edge_ref, prev_edge, h_ref
 ):
     frames, rows, cols, chan_in = x_ref.shape
-    begin, count = 0, frames
     mine, core = place[0], place[1]
     means, inverses = frame_stats(place, stats_ref, frames, per_frame)
     affine = stats_ref[stats_ref.shape[0] - 1]
@@ -248,22 +254,27 @@
         earlier = jnp.where(col == 0, 0.0, pltpu.roll(hidden, 1, 0))
         later = jnp.where(col == cols - 1, 0.0, pltpu.roll(hidden, n - 1, 0))
         for d, piece in enumerate((earlier, hidden, later)):
-            h_ref[f - begin, r0 : r0 + rows_now, :, d * chan_in : (d + 1) * chan_in] = piece.astype(BF16).reshape(
+            h_ref[f, r0 : r0 + rows_now, :, d * chan_in : (d + 1) * chan_in] = piece.astype(BF16).reshape(
                 rows_now, cols, chan_in
             )
 
-    for f in range(begin, begin + count + 2):
+    for f in range(frames + 2):
         inside = (mine > 0) if f < 2 else None
         value = prev_ref[f] if f < 2 else x_ref[f - 2]
         put(f, 1, rows, value.reshape(rows * cols, chan_in), inside)
         for r0, here in ((0, core == 1), (rows + 1, core == 0)):
-            put(f, r0, 1, prev_edge[f] if f < 2 else edge_ref[f - 2], here if inside is None else jnp.logical_and(here, inside))
-    cells = count * rows * cols
+            put(f, r0, 1, prev_edge[f, :, prev_edge.shape[2] - chan_in :] if f < 2 else edge_ref[f - 2], here if inside is None else jnp.logical_and(here, inside))
+
+
+def output_kernel(h_ref, w_ref, o_ref, acc_ref):
+    frames, rows, cols, size = h_ref.shape
+    frames, rows = frames - 2, rows - 2
+    cells = frames * rows * cols
     for a in range(3):
         for b in range(3):
             tap = a * 3 + b
-            window = h_ref[a : a + count, b : b + rows].reshape(cells, 3 * chan_in)
-            part = jnp.dot(window, w_ref[tap * 3 * chan_in : (tap + 1) * 3 * chan_in], preferred_element_type=F32)
+            window = h_ref[a : a + frames, b : b + rows].reshape(cells, size)
+            part = jnp.dot(window, w_ref[tap * size : (tap + 1) * size], preferred_element_type=F32)
             if tap == 0:
                 acc_ref[...] = part
             elif tap < 8:
@@ -383,18 +394,16 @@
     shape = jax.ShapeDtypeStruct
     half = chan_out // 2
 
-    up = [(i, i + 1) for i in range(tm - 1)]
-    down = [(i + 1, i) for i in range(tm - 1)]
+    odd_pairs = [(i, i ^ 1) for i in range(tm)]
+    even_pairs = [(i, i + 1 if i % 2 else i - 1) for i in range(1, tm - 1)]
     affine = jnp.pad(jnp.stack([gain, bias]), ((0, 2 * frames - 2), (0, 0)))[None]
     x, g, place = together(x, g, place)
-    g_first = g.reshape(frames, cells, chan_out)[:2]
-    flat = x.reshape(frames, cells, chan_in)
-    g_next = lax.ppermute(g_first, "tm", down).reshape(2, rows, cols, chan_out)
-    sums, x_last, g_rows, x_rows, x_near, g_near = call(
+    sums, to_odd, to_even, g_rows, x_rows, x_near, g_near = call(
         functools.partial(prepare_kernel, per_group),
         (
             shape((2 * frames, chan_in), F32),
-            shape((2, rows, cols, chan_in), BF16),
+            shape((2, rows, cols, chan_out), BF16),
+            shape((2, rows, cols, chan_out), BF16),
             shape((frames, cols, chan_out), BF16),
             shape((frames, cols, chan_in), BF16),
             shape(x.shape, BF16),
@@ -405,6 +414,8 @@
         scalars=1,
         far=2,
     )
+    from_odd = lax.ppermute(to_odd, "tm", odd_pairs)
+    from_even = lax.ppermute(to_even, "tm", even_pairs)
     sums = sums + swap(sums, "width", 1)
     g_edge = swap(g_rows, "width", 1)
     x_edge = swap(x_rows, "width", 1)
@@ -417,21 +428,28 @@
         [g, weight],
         [pltpu.VMEM((frames, rows + 2, cols, chan_out), BF16)],
     )
-    sums, g_next, g_edge, x_edge, own_grad = together(sums, g_next, g_edge, x_edge, own_grad)
-
-    def edges(*values):
-        rows_out = (sum(v.shape[0] for v in values), cols, values[0].shape[3])
-        return call(edge_kernel, shape(rows_out, BF16), [place, *values], scalars=1)
-
-    next_edge = swap(edges(g_next), "width", 1)
-    stats = sums[None]
-    for step in bits_of("tm"):
-        stats = jnp.concatenate([stats, swap(stats, "tm", step)], axis=0)
+    sums, from_odd, from_even, g_edge, x_edge, own_grad = together(sums, from_odd, from_even, g_edge, x_edge, own_grad)
+
+    g_next, x_prev, next_edge = call(
+        arrived_kernel,
+        (
+            shape((2, rows, cols, chan_out), BF16),
+            shape((2, rows, cols, chan_in), BF16),
+            shape((2, cols, chan_out + chan_in), BF16),
+        ),
+        [place, from_odd, from_even],
+        scalars=1,
+    )
+    next_edge = swap(next_edge, "width", 1)
+    if tm <= 4:
+        found = [sums] + [swap(sums, "tm", k) for k in range(1, tm)]
+        stats = jnp.stack(found)
+    else:
+        stats = sums[None]
+        for step in bits_of("tm"):
+            stats = jnp.concatenate([stats, swap(stats, "tm", step)], axis=0)
     stats = jnp.concatenate([stats, affine], axis=0)
-    stats, next_edge, x_last, x_rows = together(stats, next_edge, x_last, x_rows)
-    x_prev = lax.ppermute(x_last, "tm", [(i, (i + 1) % tm) for i in range(tm)])
-    turn = [(i * width + c, (i + 1) % tm * width + (c ^ 1)) for i in range(tm) for c in range(width)]
-    prev_edge = lax.ppermute(x_rows[frames - 2 :], ("tm", "width"), turn)
+    stats, next_edge, x_prev = together(stats, next_edge, x_prev)
 
     share = 27 * chan_in // (tm * dp)
     pieces = share % 48 == 0 and tm == 4 and dp == 2
@@ -452,7 +470,7 @@
         ],
         scalars=1,
     )
-    send, x_prev, prev_edge, hold = together(send, x_prev, prev_edge, stats)
+    send, hold = together(send, stats)
     recv = swap(send, "width", 1)
     local = call(
         functools.partial(gain_kernel, per_frame),
@@ -466,20 +484,24 @@
     )
     recv, local = together(recv, local)
 
-    def outputs(hold):
+    def activations(hold):
         return call(
-            functools.partial(output_kernel, per_frame),
-            shape((frames * cells, chan_out), BF16),
-            [place, hold, x, x_prev, x_edge, prev_edge, weight],
-            [
-                pltpu.VMEM((frames + 2, rows + 2, cols, 3 * chan_in), BF16),
-                pltpu.VMEM((frames * cells, chan_out), F32),
-            ],
+            functools.partial(hidden_kernel, per_frame),
+            shape((frames + 2, rows + 2, cols, 3 * chan_in), BF16),
+            [place, hold, x, x_prev, x_edge, next_edge],
             scalars=1,
         )
 
+    def outputs(hidden):
+        return call(
+            output_kernel,
+            shape((frames * cells, chan_out), BF16),
+            [hidden, weight],
+            [pltpu.VMEM((frames * cells, chan_out), F32)],
+        )
+
     if not pieces:
-        output = outputs(stats)
+        output = outputs(activations(stats))
         one = keep + recv.astype(F32)
         one = jnp.moveaxis(one.reshape(tm, dp, share, half), 1, 0)
         for step in bits_of("dp"):
@@ -507,10 +529,11 @@
         )
         rider = local + swap(local, "width", 1)
         send1, hold, rider, *send2 = together(send1, hold, rider, *send2)
+        recv2 = [swap(send2[0], "tm", OTHERS[0])]
         recv1 = swap(send1, "dp", 1)
-        recv2 = [swap(v, "tm", k) for k, v in zip(OTHERS, send2)]
+        recv2 += [swap(v, "tm", k) for k, v in zip(OTHERS[1:], send2[1:])]
         got = swap(rider, "dp", 1)
-        recv1, got, *recv2 = together(recv1, got, *recv2)
+        recv1, got, hidden, *recv2 = together(recv1, got, activations(hold), *recv2)
         stay1, *send1, stay2, send2, rider = call(
             middle_kernel,
             [piece(cut, F32)]
@@ -519,10 +542,10 @@
             [place, stay1, recv1, stay2, *recv2, rider, got],
             scalars=1,
         )
-        send2, hold, *send1 = together(send2, hold, *send1)
+        send2, hidden, *send1 = together(send2, hidden, *send1)
         recv1 = [swap(v, "tm", k) for k, v in zip(OTHERS, send1)]
         recv2 = swap(send2, "dp", 1)
-        output = outputs(hold)
+        output = outputs(hidden)
         recv2, output, *recv1 = together(recv2, output, *recv1)
         row = shape((1, chan_in), F32)
         grad_weight, *rider = call(

time: 53.5 us -> 50 us (0.935)
  waiting for transfers between devices: 16.1 us -> 10.7 us
  starting transfers between devices: 18.5 us -> 20.8 us
  local copies, waits for them, and re-layouts: 2.46 us -> 1.5 us
  Pallas kernels: 15.3 us -> 15.9 us
    ppermute x3 -> x2, waiting for transfers between devices: 5.89 us -> 0.36 us  [the longest x1 0.36 us: body(): from_odd = lax.ppermute(to_odd, 'tm', odd_pairs)]
    ppermute x17 -> x18, starting transfers between devices: 15.6 us -> 17 us  [swap(): lax.ppermute(value, axis, [(i, i ^ step) for i in range(lax.axis_size(axi...]
    slice x2 -> x0, local copies, waits for them, and re-layouts: 0.97 us -> none  [the longest x1 0.97 us: body(): g_first = g.reshape(frames, cells, chan_out)[:2]]
    ppermute x3 -> x2, starting transfers between devices: 2.94 us -> 3.75 us  [the longest x1 3.09 us: body(): from_odd = lax.ppermute(to_odd, 'tm', odd_pairs)]
    pallas_call x9 -> x10, Pallas kernels: 15.3 us -> 15.9 us  [call(): pl.pallas_call(kernel, out_shape=out_shape, in_specs=[SMEM] * scalars + [...]
    ppermute x17 -> x18, waiting for transfers between devices: 10.2 us -> 10.3 us  [swap(): lax.ppermute(value, axis, [(i, i ^ step) for i in range(lax.axis_size(axi...]
    unnamed x8 -> x12, local copies, waits for them, and re-layouts: 1.49 us -> 1.5 us
  transfers between devices with their start and end apart: 20 -> 20, of which waited for: 13 -> 10; matrix products, arithmetic and copies ran while one was open for 0% -> 0% of each run, Pallas kernels for 26% -> 20%
where the time goes in v5:
time: 50 us; the launch traced here: 49.8 us
  starting transfers between devices  20.8 us (42%)
  Pallas kernels  15.9 us (32%)
  waiting for transfers between devices  10.7 us (21%)
  local copies, waits for them, and re-layouts  1.5 us (3%)
  between operations  0.8 us (2%)
    ppermute x18, starting transfers between devices, swap(): lax.ppermute(value, axis, [(i, i ^ step) for i in range(lax.axis_size(axi...  17 us
    pallas_call x10, Pallas kernels, call(): pl.pallas_call(kernel, out_shape=out_shape, in_specs=[SMEM] * scalars + [...  15.9 us
    ppermute x18, waiting for transfers between devices, swap(): lax.ppermute(value, axis, [(i, i ^ step) for i in range(lax.axis_size(axi...  10.3 us
    ppermute x1, starting transfers between devices, body(): from_odd = lax.ppermute(to_odd, 'tm', odd_pairs)  3.09 us
    unnamed x12, local copies, waits for them, and re-layouts  1.5 us
  transfers between devices with their start and end apart: 20, of which 10 were waited for; matrix products, arithmetic and copies ran while one was open for 0% of the time, Pallas kernels for 20%

profile of v5, /device:TPU:0, one launch (start us, length us, event | category | flops | bytes accessed | tf_op | source)
XLA Modules:
  0.0 49.8 jit_solution(15153773630578226079)
XLA Ops:
  0.6 0.1 pad_add_fusion.place
  0.7 1.9 %shard_map.84 = (f32[8,128]{1,0:T(8,128)S(1)}, bf16[2,4,64,256]{3,2,1,0:T(8,128)(2,1)S(1)}, bf16[2,4,64,256]{3,2,1,0:T(8,128)(2,1)S(1)}, bf16[4,64,256]{2,1,0:T(...) custom-call(s32[3]{0:T(128)S(1)} %pad_add_fusion.place, ...), custom_call_target="tpu_custom_call" | custom-call | bytes 2297868 | tf_op jit(solution)/shard_map/pallas_call | solution.py:21
  2.6 3.1 %collective-permute-start.1 = (bf16[2,4,64,256]{3,2,1,0:T(8,128)(2,1)S(1)}, bf16[2,4,64,256]{3,2,1,0:T(8,128)(2,1)S(1)}, u32[]{:S(2)}, u32[]{:S(2)}) collective-permute-start(bf16[2,4,64,256]{3,2,1,0:T(8,128)(2,1)S(1)} %get-tuple-element.78), channel_id=1, source_target_pairs={{0,4},{4,0},{8,12},{12,8},{1,5},{5,1},{9,13},{13,9},{2,6},{6,2},{1... | collective-permute-start | bytes 786440 | tf_op jit(solution)/shard_map/ppermute | solution.py:417
  5.7 0.7 %collective-permute-start.2 = (bf16[2,4,64,256]{3,2,1,0:T(8,128)(2,1)S(1)}, bf16[2,4,64,256]{3,2,1,0:T(8,128)(2,1)S(1)}, u32[]{:S(2)}, u32[]{:S(2)}) collective-permute-start(bf16[2,4,64,256]{3,2,1,0:T(8,128)(2,1)S(1)} %get-tuple-element.79), channel_id=1, source_target_pairs={{4,8},{8,4},{5,9},{9,5},{6,10},{10,6},{7,11},{11,7},{20,24},{24,20... | collective-permute-start | bytes 786440 | tf_op jit(solution)/shard_map/ppermute | solution.py:418
  6.4 0.1 collective-permute-start.3
  6.5 0.5 collective-permute-start.4
  7.0 0.1 collective-permute-start
  7.0 1.1 %collective-permute-done = f32[8,128]{1,0:T(8,128)S(1)} collective-permute-done((f32[8,128]{1,0:T(8,128)S(1)}, f32[8,128]{1,0:T(8,128)S(1)}, u32[]{:S(2)}, u32[]{:S(2)}) %collective-permute-start) | collective-permute-done | bytes 4128 | tf_op jit(solution)/shard_map/ppermute | solution.py:362
  8.1 0.0 copy-start
  8.1 1.5 %copy-done = bf16[3456,256]{1,0:T(8,128)(2,1)S(1)} copy-done((bf16[3456,256]{1,0:T(8,128)(2,1)S(1)}, bf16[3456,256]{1,0:T(8,128)(2,1)}, u32[]{:S(2)}) %copy-start) | copy-done | bytes 1769496
  9.6 0.0 copy-start.2
  9.6 0.0 copy-start.3
  9.6 2.0 %shard_map.85.own_ref = f32[4,4,64,384]{3,2,1,0:T(8,128)S(1)} custom-call(bf16[4,4,64,256]{3,2,1,0:T(8,128)(2,1)S(1)} %get-tuple-element.82.g_ref, bf16[3456,256]{1,0:T(8,128)(2,1)S(1)} %copy-done), custom_call_target="tpu_custom_call" | custom-call | bytes 3866624 | tf_op jit(solution)/shard_map/pallas_call | solution.py:21
  11.6 0.0 copy-start.1
  11.6 0.0 collective-permute-done.4.edge_ref
  11.6 0.0 collective-permute-done.3.edge_ref
  11.7 0.4 collective-permute-done.1.odd_ref
  12.0 0.0 collective-permute-done.2.even_ref
  12.0 3.8 %collective-permute-start.7 = (f32[8,128]{1,0:T(8,128)S(1)}, f32[8,128]{1,0:T(8,128)S(1)}, u32[]{:S(2)}, u32[]{:S(2)}) collective-permute-start(f32[8,128]{1,0:T(8,128)S(1)} %add.8), channel_id=1, source_target_pairs={{0,12},{4,8},{8,4},{12,0},{1,13},{5,9},{9,5},{13,1},{2,14},{6,10},... | collective-permute-start | bytes 12296 | tf_op jit(solution)/shard_map/ppermute | solution.py:362
  15.8 2.5 %collective-permute-start.6 = (f32[8,128]{1,0:T(8,128)S(1)}, f32[8,128]{1,0:T(8,128)S(1)}, u32[]{:S(2)}, u32[]{:S(2)}) collective-permute-start(f32[8,128]{1,0:T(8,128)S(1)} %add.8), channel_id=1, source_target_pairs={{0,8},{4,12},{8,0},{12,4},{1,9},{5,13},{9,1},{13,5},{2,10},{6,14},... | collective-permute-start | bytes 12296 | tf_op jit(solution)/shard_map/ppermute | solution.py:362
  18.2 0.3 collective-permute-start.5
  18.5 0.6 %shard_map.86 = (bf16[2,4,64,256]{3,2,1,0:T(8,128)(2,1)S(1)}, bf16[2,4,64,128]{3,2,1,0:T(8,128)(2,1)S(1)}, bf16[2,64,384]{2,1,0:T(8,128)(2,1)S(1)}) custom-call(s32[3]{0:T(128)S(1)} %pad_add_fusion.place, bf16[2,4,64,256]{3,2,1,0:T(8,128)(2,1)S(1)} %collective-permute-done.1.odd_ref, bf16[2,4,64,256]{3,2,1,0:T(8,128)(2,1)S(1)} %collective-permute-done.2.even_ref), custom_call_target="tpu_custom_call" | custom-call | bytes 1015820 | tf_op jit(solution)/shard_map/pallas_call | solution.py:21
  19.1 0.1 collective-permute-start.8
  19.2 2.6 %collective-permute-done.5 = f32[8,128]{1,0:T(8,128)S(1)} collective-permute-done((f32[8,128]{1,0:T(8,128)S(1)}, f32[8,128]{1,0:T(8,128)S(1)}, u32[]{:S(2)}, u32[]{:S(2)}) %collective-permute-start.5) | collective-permute-done | bytes 4128 | tf_op jit(solution)/shard_map/ppermute | solution.py:362
  21.9 0.0 collective-permute-done.6
  21.9 0.0 collective-permute-done.7
  21.9 0.0 copy-done.2
  21.9 0.0 copy-done.3
  21.9 0.0 collective-permute-done.8.edge_next.prev_edge
  21.9 2.9 %shard_map.87 = (f32[3456,128]{1,0:T(8,128)S(1)}, bf16[3456,128]{1,0:T(8,128)(2,1)S(1)}) custom-call(s32[3]{0:T(128)S(1)} %pad_add_fusion.place, f32[5,8,128]{2,1,0:T(8,128)S(1)} %constant_dynamic-update-slice_fusion.stats_ref, bf16[2,4,64,256]{3,2,1,0:T(8,128)(2,1)S(1)} %get-tuple-element.89.next_ref, ...), custom_call_target="tpu_custom_call" | custom-call | bytes 3952652 | tf_op jit(solution)/shard_map/pallas_call | solution.py:21
  24.8 0.1 collective-permute-start.9
  24.9 0.0 copy-done.1
  24.9 1.8 %shard_map.88 = f32[2,128]{1,0:T(2,128)S(1)} custom-call(s32[3]{0:T(128)S(1)} %pad_add_fusion.place, f32[5,8,128]{2,1,0:T(8,128)S(1)} %constant_dynamic-update-slice_fusion.stats_ref, bf16[4,256,128]{2,1,0:T(8,128)(2,1)S(1)} %bitcast.24, f32[4,4,64,384]{3,2,1,0:T(8,128)S(1)} %shard_map.85.own_ref, bf16[2,4,64,256]{3,2,1,0:T(8,128)(2,1)S(1)} %get-tuple-element.89.next_ref, ...), custom_call_target="tpu_custom_call" | custom-call | bytes 4117516 | tf_op jit(solution)/shard_map/pallas_call | solution.py:21
  26.7 0.6 %collective-permute-done.9.recv_ref = bf16[3456,128]{1,0:T(8,128)(2,1)S(1)} collective-permute-done((bf16[3456,128]{1,0:T(8,128)(2,1)S(1)}, bf16[3456,128]{1,0:T(8,128)(2,1)S(1)}, u32[]{:S(2)}, u32[]{:S(2)}) %collective-permute-start.9) | collective-permute-done | bytes 884768 | tf_op jit(solution)/shard_map/ppermute | solution.py:362
  27.3 0.1 collective-permute-start.10
  27.4 0.7 %shard_map.89 = (f32[1152,128]{1,0:T(8,128)S(1)}, bf16[1152,128]{1,0:T(8,128)(2,1)S(1)}, f32[288,128]{1,0:T(8,128)S(1)}, bf16[288,128]{1,0:T(8,128)(2,1)S(1)}, b...) custom-call(s32[3]{0:T(128)S(1)} %pad_add_fusion.place, f32[3456,128]{1,0:T(8,128)S(1)} %get-tuple-element.93.keep_ref, ...), custom_call_target="tpu_custom_call" | custom-call | bytes 3907596 | tf_op jit(solution)/shard_map/pallas_call | solution.py:21
  28.2 0.3 collective-permute-done.10
  28.4 1.5 %collective-permute-start.11 = (bf16[1152,128]{1,0:T(8,128)(2,1)S(1)}, bf16[1152,128]{1,0:T(8,128)(2,1)S(1)}, u32[]{:S(2)}, u32[]{:S(2)}) collective-permute-start(bf16[1152,128]{1,0:T(8,128)(2,1)S(1)} %get-tuple-element.105), channel_id=1, source_target_pairs={{0,2},{2,0},{1,3},{3,1},{4,6},{6,4},{5,7},{7,5},{8,10},{10,8},{9,1... | collective-permute-start | bytes 884744 | tf_op jit(solution)/shard_map/ppermute | solution.py:362
  29.9 1.5 %collective-permute-start.13 = (bf16[288,128]{1,0:T(8,128)(2,1)S(1)}, bf16[288,128]{1,0:T(8,128)(2,1)S(1)}, u32[]{:S(2)}, u32[]{:S(2)}) collective-permute-start(bf16[288,128]{1,0:T(8,128)(2,1)S(1)} %get-tuple-element.110), channel_id=1, source_target_pairs={{0,8},{4,12},{8,0},{12,4},{1,9},{5,13},{9,1},{13,5},{2,10},{6,14},... | collective-permute-start | bytes 221192 | tf_op jit(solution)/shard_map/ppermute | solution.py:362
  31.4 2.0 %collective-permute-start.14 = (bf16[288,128]{1,0:T(8,128)(2,1)S(1)}, bf16[288,128]{1,0:T(8,128)(2,1)S(1)}, u32[]{:S(2)}, u32[]{:S(2)}) collective-permute-start(bf16[288,128]{1,0:T(8,128)(2,1)S(1)} %get-tuple-element.111), channel_id=1, source_target_pairs={{0,12},{4,8},{8,4},{12,0},{1,13},{5,9},{9,5},{13,1},{2,14},{6,10},... | collective-permute-start | bytes 221192 | tf_op jit(solution)/shard_map/ppermute | solution.py:362
  33.5 0.0 collective-permute-start.15
  33.5 0.5 %collective-permute-start.12 = (f32[2,128]{1,0:T(2,128)S(1)}, f32[2,128]{1,0:T(2,128)S(1)}, u32[]{:S(2)}, u32[]{:S(2)}) collective-permute-start(f32[2,128]{1,0:T(2,128)S(1)} %add.9.rider_ref), channel_id=1, source_target_pairs={{0,2},{2,0},{1,3},{3,1},{4,6},{6,4},{5,7},{7,5},{8,10},{10,8},{9,1... | collective-permute-start | bytes 3080 | tf_op jit(solution)/shard_map/ppermute | solution.py:362
  34.0 1.1 %shard_map.90.h_ref = bf16[6,6,64,384]{3,2,1,0:T(8,128)(2,1)S(1)} custom-call(s32[3]{0:T(128)S(1)} %pad_add_fusion.place, f32[5,8,128]{2,1,0:T(8,128)S(1)} %constant_dynamic-update-slice_fusion.stats_ref, bf16[4,4,64,128]{3,2,1,0:T(8,128)(2,1)S(1)} %get-tuple-element.92.x_ref, bf16[2,4,64,128]{3,2,1,0:T(8,128)(2,1)S(1)} %get-tuple-element.108.prev_ref, ...), custom_call_target="tpu_custom_call" | custom-call | bytes 2347020 | tf_op jit(solution)/shard_map/pallas_call | solution.py:21
  35.1 2.5 %collective-permute-done.12.got_ref = f32[2,128]{1,0:T(2,128)S(1)} collective-permute-done((f32[2,128]{1,0:T(2,128)S(1)}, f32[2,128]{1,0:T(2,128)S(1)}, u32[]{:S(2)}, u32[]{:S(2)}) %collective-permute-start.12) | collective-permute-done | bytes 1056 | tf_op jit(solution)/shard_map/ppermute | solution.py:362
  37.6 1.2 %collective-permute-done.13.b_ref = bf16[288,128]{1,0:T(8,128)(2,1)S(1)} collective-permute-done((bf16[288,128]{1,0:T(8,128)(2,1)S(1)}, bf16[288,128]{1,0:T(8,128)(2,1)S(1)}, u32[]{:S(2)}, u32[]{:S(2)}) %collective-permute-start.13) | collective-permute-done | bytes 73760 | tf_op jit(solution)/shard_map/ppermute | solution.py:362
  38.8 0.0 collective-permute-done.14.c_ref
  38.8 0.5 %collective-permute-done.15.a_ref = bf16[288,128]{1,0:T(8,128)(2,1)S(1)} collective-permute-done((bf16[288,128]{1,0:T(8,128)(2,1)S(1)}, bf16[288,128]{1,0:T(8,128)(2,1)S(1)}, u32[]{:S(2)}, u32[]{:S(2)}) %collective-permute-start.15) | collective-permute-done | bytes 73760 | tf_op jit(solution)/shard_map/ppermute | solution.py:362
  39.3 0.0 collective-permute-done.11.recv1_ref
  39.3 0.6 %shard_map.91 = (f32[288,128]{1,0:T(8,128)S(1)}, bf16[304,128]{1,0:T(8,128)(2,1)S(1)}, bf16[304,128]{1,0:T(8,128)(2,1)S(1)}, bf16[304,128]{1,0:T(8,128)(2,1)S(1)...) custom-call(s32[3]{0:T(128)S(1)} %pad_add_fusion.place, ...), custom_call_target="tpu_custom_call" | custom-call | bytes 1747980 | tf_op jit(solution)/shard_map/pallas_call | solution.py:21
  39.9 2.0 %collective-permute-start.17 = (bf16[304,128]{1,0:T(8,128)(2,1)S(1)}, bf16[304,128]{1,0:T(8,128)(2,1)S(1)}, u32[]{:S(2)}, u32[]{:S(2)}) collective-permute-start(bf16[304,128]{1,0:T(8,128)(2,1)S(1)} %get-tuple-element.126), channel_id=1, source_target_pairs={{0,8},{4,12},{8,0},{12,4},{1,9},{5,13},{9,1},{13,5},{2,10},{6,14},... | collective-permute-start | bytes 233480 | tf_op jit(solution)/shard_map/ppermute | solution.py:362
  41.9 1.4 %collective-permute-start.18 = (bf16[304,128]{1,0:T(8,128)(2,1)S(1)}, bf16[304,128]{1,0:T(8,128)(2,1)S(1)}, u32[]{:S(2)}, u32[]{:S(2)}) collective-permute-start(bf16[304,128]{1,0:T(8,128)(2,1)S(1)} %get-tuple-element.127), channel_id=1, source_target_pairs={{0,12},{4,8},{8,4},{12,0},{1,13},{5,9},{9,5},{13,1},{2,14},{6,10},... | collective-permute-start | bytes 233480 | tf_op jit(solution)/shard_map/ppermute | solution.py:362
  43.3 0.2 collective-permute-start.19
  43.5 0.5 %collective-permute-start.16 = (bf16[144,128]{1,0:T(8,128)(2,1)S(1)}, bf16[144,128]{1,0:T(8,128)(2,1)S(1)}, u32[]{:S(2)}, u32[]{:S(2)}) collective-permute-start(bf16[144,128]{1,0:T(8,128)(2,1)S(1)} %get-tuple-element.124), channel_id=1, source_target_pairs={{0,2},{2,0},{1,3},{3,1},{4,6},{6,4},{5,7},{7,5},{8,10},{10,8},{9,1... | collective-permute-start | bytes 110600 | tf_op jit(solution)/shard_map/ppermute | solution.py:362
  44.0 3.4 %shard_map.92 = bf16[1024,256]{1,0:T(8,128)(2,1)} custom-call(bf16[6,6,64,384]{3,2,1,0:T(8,128)(2,1)S(1)} %shard_map.90.h_ref, bf16[3456,256]{1,0:T(8,128)(2,1)S(1)} %copy-done.1), custom_call_target="tpu_custom_call" | custom-call | bytes 4063232 | tf_op jit(solution)/shard_map/pallas_call | solution.py:21
  47.4 0.0 collective-permute-done.16.recv2_ref
  47.5 1.2 %collective-permute-done.17.b_ref = bf16[304,128]{1,0:T(8,128)(2,1)S(1)} collective-permute-done((bf16[304,128]{1,0:T(8,128)(2,1)S(1)}, bf16[304,128]{1,0:T(8,128)(2,1)S(1)}, u32[]{:S(2)}, u32[]{:S(2)}) %collective-permute-start.17) | collective-permute-done | bytes 77856 | tf_op jit(solution)/shard_map/ppermute | solution.py:362
  48.7 0.0 collective-permute-done.18.c_ref
  48.7 0.3 collective-permute-done.19.a_ref
  49.0 0.7 %shard_map.93 = (f32[432,128]{1,0:T(8,128)}, f32[1,128]{1,0:T(1,128)}, f32[1,128]{1,0:T(1,128)}) custom-call(f32[288,128]{1,0:T(8,128)S(1)} %get-tuple-element.130.stay1_ref, bf16[304,128]{1,0:T(8,128)(2,1)S(1)} %collective-permute-done.17.b_ref, bf16[304,128]{1,0:T(8,128)(2,1)S(1)} %collective-permute-done.18.c_ref, ...), custom_call_target="tpu_custom_call" | custom-call | bytes 714752 | tf_op jit(solution)/shard_map/pallas_call | solution.py:21
  (7 shorter events, 0.0 us)
Async XLA Ops:
  2.6 9.4 %collective-permute-start.1 = (bf16[2,4,64,256]{3,2,1,0:T(8,128)(2,1)S(1)}, bf16[2,4,64,256]{3,2,1,0:T(8,128)(2,1)S(1)}, u32[]{:S(2)}, u32[]{:S(2)}) collective-permute-start(bf16[2,4,64,256]{3,2,1,0:T(8,128)(2,1)S(1)} %get-tuple-element.78), channel_id=1, source_target_pairs={{0,4},{4,0},{8,12},{12,8},{1,5},{5,1},{9,13},{13,9},{2,6},{6,2},{1... | collective-permute-start | bytes 786440 | tf_op jit(solution)/shard_map/ppermute | solution.py:417
  5.7 6.3 %collective-permute-start.2 = (bf16[2,4,64,256]{3,2,1,0:T(8,128)(2,1)S(1)}, bf16[2,4,64,256]{3,2,1,0:T(8,128)(2,1)S(1)}, u32[]{:S(2)}, u32[]{:S(2)}) collective-permute-start(bf16[2,4,64,256]{3,2,1,0:T(8,128)(2,1)S(1)} %get-tuple-element.79), channel_id=1, source_target_pairs={{4,8},{8,4},{5,9},{9,5},{6,10},{10,6},{7,11},{11,7},{20,24},{24,20... | collective-permute-start | bytes 786440 | tf_op jit(solution)/shard_map/ppermute | solution.py:418
  6.4 5.3 %collective-permute-start.3 = (bf16[4,64,256]{2,1,0:T(8,128)(2,1)S(1)}, bf16[4,64,256]{2,1,0:T(8,128)(2,1)S(1)}, u32[]{:S(2)}, u32[]{:S(2)}) collective-permute-start(bf16[4,64,256]{2,1,0:T(8,128)(2,1)S(1)} %get-tuple-element.80), channel_id=1, source_target_pairs={{0,1},{1,0},{2,3},{3,2},{4,5},{5,4},{6,7},{7,6},{8,9},{9,8},{10,11... | collective-permute-start | bytes 393224 | tf_op jit(solution)/shard_map/ppermute | solution.py:362
  6.5 5.2 %collective-permute-start.4 = (bf16[4,64,128]{2,1,0:T(8,128)(2,1)S(1)}, bf16[4,64,128]{2,1,0:T(8,128)(2,1)S(1)}, u32[]{:S(2)}, u32[]{:S(2)}) collective-permute-start(bf16[4,64,128]{2,1,0:T(8,128)(2,1)S(1)} %get-tuple-element.81), channel_id=1, source_target_pairs={{0,1},{1,0},{2,3},{3,2},{4,5},{5,4},{6,7},{7,6},{8,9},{9,8},{10,11... | collective-permute-start | bytes 196616 | tf_op jit(solution)/shard_map/ppermute | solution.py:362
  7.0 1.2 %collective-permute-start = (f32[8,128]{1,0:T(8,128)S(1)}, f32[8,128]{1,0:T(8,128)S(1)}, u32[]{:S(2)}, u32[]{:S(2)}) collective-permute-start(f32[8,128]{1,0:T(8,128)S(1)} %get-tuple-element.75), channel_id=1, source_target_pairs={{0,1},{1,0},{2,3},{3,2},{4,5},{5,4},{6,7},{7,6},{8,9},{9,8},{10,11... | collective-permute-start | bytes 12296 | tf_op jit(solution)/shard_map/ppermute | solution.py:362
  8.1 1.5 %copy-start = (bf16[3456,256]{1,0:T(8,128)(2,1)S(1)}, bf16[3456,256]{1,0:T(8,128)(2,1)}, u32[]{:S(2)}) copy-start(bf16[3456,256]{1,0:T(8,128)(2,1)} %w_ref.5) | copy-start | bytes 5308420
  9.6 12.3 %copy-start.2 = (f32[128]{0:T(128)S(1)}, f32[128]{0:T(128)}, u32[]{:S(2)}) copy-start(f32[128]{0:T(128)} %param.7) | copy-start | bytes 1540
  9.6 12.3 %copy-start.3 = (f32[128]{0:T(128)S(1)}, f32[128]{0:T(128)}, u32[]{:S(2)}) copy-start(f32[128]{0:T(128)} %param.6) | copy-start | bytes 1540
  11.6 13.3 %copy-start.1 = (bf16[3456,256]{1,0:T(8,128)(2,1)S(1)}, bf16[3456,256]{1,0:T(8,128)(2,1)}, u32[]{:S(2)}) copy-start(bf16[3456,256]{1,0:T(8,128)(2,1)} %w_ref.5) | copy-start | bytes 5308420
  12.0 9.8 %collective-permute-start.7 = (f32[8,128]{1,0:T(8,128)S(1)}, f32[8,128]{1,0:T(8,128)S(1)}, u32[]{:S(2)}, u32[]{:S(2)}) collective-permute-start(f32[8,128]{1,0:T(8,128)S(1)} %add.8), channel_id=1, source_target_pairs={{0,12},{4,8},{8,4},{12,0},{1,13},{5,9},{9,5},{13,1},{2,14},{6,10},... | collective-permute-start | bytes 12296 | tf_op jit(solution)/shard_map/ppermute | solution.py:362
  15.8 6.1 %collective-permute-start.6 = (f32[8,128]{1,0:T(8,128)S(1)}, f32[8,128]{1,0:T(8,128)S(1)}, u32[]{:S(2)}, u32[]{:S(2)}) collective-permute-start(f32[8,128]{1,0:T(8,128)S(1)} %add.8), channel_id=1, source_target_pairs={{0,8},{4,12},{8,0},{12,4},{1,9},{5,13},{9,1},{13,5},{2,10},{6,14},... | collective-permute-start | bytes 12296 | tf_op jit(solution)/shard_map/ppermute | solution.py:362
  18.2 3.6 %collective-permute-start.5 = (f32[8,128]{1,0:T(8,128)S(1)}, f32[8,128]{1,0:T(8,128)S(1)}, u32[]{:S(2)}, u32[]{:S(2)}) collective-permute-start(f32[8,128]{1,0:T(8,128)S(1)} %add.8), channel_id=1, source_target_pairs={{0,4},{4,0},{8,12},{12,8},{1,5},{5,1},{9,13},{13,9},{2,6},{6,2},{1... | collective-permute-start | bytes 12296 | tf_op jit(solution)/shard_map/ppermute | solution.py:362
  19.1 2.8 %collective-permute-start.8 = (bf16[2,64,384]{2,1,0:T(8,128)(2,1)S(1)}, bf16[2,64,384]{2,1,0:T(8,128)(2,1)S(1)}, u32[]{:S(2)}, u32[]{:S(2)}) collective-permute-start(bf16[2,64,384]{2,1,0:T(8,128)(2,1)S(1)} %get-tuple-element.86), channel_id=1, source_target_pairs={{0,1},{1,0},{2,3},{3,2},{4,5},{5,4},{6,7},{7,6},{8,9},{9,8},{10,11... | collective-permute-start | bytes 294920 | tf_op jit(solution)/shard_map/ppermute | solution.py:362
  24.8 2.5 %collective-permute-start.9 = (bf16[3456,128]{1,0:T(8,128)(2,1)S(1)}, bf16[3456,128]{1,0:T(8,128)(2,1)S(1)}, u32[]{:S(2)}, u32[]{:S(2)}) collective-permute-start(bf16[3456,128]{1,0:T(8,128)(2,1)S(1)} %get-tuple-element.95), channel_id=1, source_target_pairs={{0,1},{1,0},{2,3},{3,2},{4,5},{5,4},{6,7},{7,6},{8,9},{9,8},{10,11... | collective-permute-start | bytes 2654216 | tf_op jit(solution)/shard_map/ppermute | solution.py:362
  27.3 1.1 %collective-permute-start.10 = (f32[2,128]{1,0:T(2,128)S(1)}, f32[2,128]{1,0:T(2,128)S(1)}, u32[]{:S(2)}, u32[]{:S(2)}) collective-permute-start(f32[2,128]{1,0:T(2,128)S(1)} %shard_map.88), channel_id=1, source_target_pairs={{0,1},{1,0},{2,3},{3,2},{4,5},{5,4},{6,7},{7,6},{8,9},{9,8},{10,11... | collective-permute-start | bytes 3080 | tf_op jit(solution)/shard_map/ppermute | solution.py:362
  28.4 10.8 %collective-permute-start.11 = (bf16[1152,128]{1,0:T(8,128)(2,1)S(1)}, bf16[1152,128]{1,0:T(8,128)(2,1)S(1)}, u32[]{:S(2)}, u32[]{:S(2)}) collective-permute-start(bf16[1152,128]{1,0:T(8,128)(2,1)S(1)} %get-tuple-element.105), channel_id=1, source_target_pairs={{0,2},{2,0},{1,3},{3,1},{4,6},{6,4},{5,7},{7,5},{8,10},{10,8},{9,1... | collective-permute-start | bytes 884744 | tf_op jit(solution)/shard_map/ppermute | solution.py:362
  29.9 8.8 %collective-permute-start.13 = (bf16[288,128]{1,0:T(8,128)(2,1)S(1)}, bf16[288,128]{1,0:T(8,128)(2,1)S(1)}, u32[]{:S(2)}, u32[]{:S(2)}) collective-permute-start(bf16[288,128]{1,0:T(8,128)(2,1)S(1)} %get-tuple-element.110), channel_id=1, source_target_pairs={{0,8},{4,12},{8,0},{12,4},{1,9},{5,13},{9,1},{13,5},{2,10},{6,14},... | collective-permute-start | bytes 221192 | tf_op jit(solution)/shard_map/ppermute | solution.py:362
  31.4 7.3 %collective-permute-start.14 = (bf16[288,128]{1,0:T(8,128)(2,1)S(1)}, bf16[288,128]{1,0:T(8,128)(2,1)S(1)}, u32[]{:S(2)}, u32[]{:S(2)}) collective-permute-start(bf16[288,128]{1,0:T(8,128)(2,1)S(1)} %get-tuple-element.111), channel_id=1, source_target_pairs={{0,12},{4,8},{8,4},{12,0},{1,13},{5,9},{9,5},{13,1},{2,14},{6,10},... | collective-permute-start | bytes 221192 | tf_op jit(solution)/shard_map/ppermute | solution.py:362
  33.5 5.8 %collective-permute-start.15 = (bf16[288,128]{1,0:T(8,128)(2,1)S(1)}, bf16[288,128]{1,0:T(8,128)(2,1)S(1)}, u32[]{:S(2)}, u32[]{:S(2)}) collective-permute-start(bf16[288,128]{1,0:T(8,128)(2,1)S(1)} %get-tuple-element.112), channel_id=1, source_target_pairs={{0,4},{4,0},{8,12},{12,8},{1,5},{5,1},{9,13},{13,9},{2,6},{6,2},{1... | collective-permute-start | bytes 221192 | tf_op jit(solution)/shard_map/ppermute | solution.py:362
  33.5 4.2 %collective-permute-start.12 = (f32[2,128]{1,0:T(2,128)S(1)}, f32[2,128]{1,0:T(2,128)S(1)}, u32[]{:S(2)}, u32[]{:S(2)}) collective-permute-start(f32[2,128]{1,0:T(2,128)S(1)} %add.9.rider_ref), channel_id=1, source_target_pairs={{0,2},{2,0},{1,3},{3,1},{4,6},{6,4},{5,7},{7,5},{8,10},{10,8},{9,1... | collective-permute-start | bytes 3080 | tf_op jit(solution)/shard_map/ppermute | solution.py:362
  39.9 8.8 %collective-permute-start.17 = (bf16[304,128]{1,0:T(8,128)(2,1)S(1)}, bf16[304,128]{1,0:T(8,128)(2,1)S(1)}, u32[]{:S(2)}, u32[]{:S(2)}) collective-permute-start(bf16[304,128]{1,0:T(8,128)(2,1)S(1)} %get-tuple-element.126), channel_id=1, source_target_pairs={{0,8},{4,12},{8,0},{12,4},{1,9},{5,13},{9,1},{13,5},{2,10},{6,14},... | collective-permute-start | bytes 233480 | tf_op jit(solution)/shard_map/ppermute | solution.py:362
  41.9 6.8 %collective-permute-start.18 = (bf16[304,128]{1,0:T(8,128)(2,1)S(1)}, bf16[304,128]{1,0:T(8,128)(2,1)S(1)}, u32[]{:S(2)}, u32[]{:S(2)}) collective-permute-start(bf16[304,128]{1,0:T(8,128)(2,1)S(1)} %get-tuple-element.127), channel_id=1, source_target_pairs={{0,12},{4,8},{8,4},{12,0},{1,13},{5,9},{9,5},{13,1},{2,14},{6,10},... | collective-permute-start | bytes 233480 | tf_op jit(solution)/shard_map/ppermute | solution.py:362
  43.3 5.7 %collective-permute-start.19 = (bf16[304,128]{1,0:T(8,128)(2,1)S(1)}, bf16[304,128]{1,0:T(8,128)(2,1)S(1)}, u32[]{:S(2)}, u32[]{:S(2)}) collective-permute-start(bf16[304,128]{1,0:T(8,128)(2,1)S(1)} %get-tuple-element.128), channel_id=1, source_target_pairs={{0,4},{4,0},{8,12},{12,8},{1,5},{5,1},{9,13},{13,9},{2,6},{6,2},{1... | collective-permute-start | bytes 233480 | tf_op jit(solution)/shard_map/ppermute | solution.py:362
  43.5 4.0 %collective-permute-start.16 = (bf16[144,128]{1,0:T(8,128)(2,1)S(1)}, bf16[144,128]{1,0:T(8,128)(2,1)S(1)}, u32[]{:S(2)}, u32[]{:S(2)}) collective-permute-start(bf16[144,128]{1,0:T(8,128)(2,1)S(1)} %get-tuple-element.124), channel_id=1, source_target_pairs={{0,2},{2,0},{1,3},{3,1},{4,6},{6,4},{5,7},{7,5},{8,10},{10,8},{9,1... | collective-permute-start | bytes 110600 | tf_op jit(solution)/shard_map/ppermute | solution.py:362

commit v6 on v5

--- a/solution.py
+++ b/solution.py
@@ -59,16 +59,25 @@
         firsts.append(jnp.sum(v, axis=0, keepdims=True))
         squares.append(jnp.sum(v * v, axis=0, keepdims=True))
         x_row_ref[t] = x_ref[t, row]
-    sums_ref[...] = group_sum(jnp.concatenate(firsts + squares, axis=0), per_group)
+    total = group_sum(jnp.concatenate(firsts + squares, axis=0), per_group)
+    sums_ref[...] = total
+    parts = []
+    for _ in range(3):
+        parts.append(total.astype(BF16).astype(F32))
+        total = total - parts[-1]
+    n = rows * cols
+    odd_ref[2 * n :, :chan_in] = jnp.concatenate(parts[:2], axis=0).astype(BF16)
+    odd_ref[2 * n :, chan_in:] = jnp.concatenate([parts[2], jnp.zeros_like(total)], axis=0).astype(BF16)
     for t in range(frames):
         copies[frames + t].wait()
         row_ref[t] = g_ref[t, row]
     even = jnp.bitwise_and(place[0], 1) == 0
     for t in range(2):
         clip, low = x_ref[frames - 2 + t], g_ref[t, :, :, :chan_in]
-        odd_ref[t, :, :, :chan_in] = jnp.where(even, clip, low)
+        here = slice(t * n, (t + 1) * n)
+        odd_ref[here, :chan_in] = jnp.where(even, clip, low).reshape(n, chan_in)
         even_ref[t, :, :, :chan_in] = jnp.where(even, low, clip)
-        odd_ref[t, :, :, chan_in:] = g_ref[t, :, :, chan_in:]
+        odd_ref[here, chan_in:] = g_ref[t, :, :, chan_in:].reshape(n, chan_in)
         even_ref[t, :, :, chan_in:] = g_ref[t, :, :, chan_in:]
 
 
@@ -76,9 +85,11 @@
     chan_in, chan_out = prev_ref.shape[3], next_ref.shape[3]
     even = jnp.bitwise_and(place[0], 1) == 0
     row = jnp.where(place[1] == 0, next_ref.shape[1] - 1, 0)
+    n = next_ref.shape[1] * next_ref.shape[2]
     for t in range(2):
-        next_ref[t] = jnp.where(even, odd_ref[t], even_ref[t])
-        prev_ref[t] = jnp.where(even, even_ref[t, :, :, :chan_in], odd_ref[t, :, :, :chan_in])
+        odd = odd_ref[t * n : (t + 1) * n].reshape(next_ref.shape[1:])
+        next_ref[t] = jnp.where(even, odd, even_ref[t])
+        prev_ref[t] = jnp.where(even, even_ref[t, :, :, :chan_in], odd[:, :, :chan_in])
         edge_ref[t, :, :chan_out] = next_ref[t, row]
         edge_ref[t, :, chan_out:] = prev_ref[t, row]
 
@@ -402,7 +413,7 @@
         functools.partial(prepare_kernel, per_group),
         (
             shape((2 * frames, chan_in), F32),
-            shape((2, rows, cols, chan_out), BF16),
+            shape((2 * cells + 4 * frames, chan_out), BF16),
             shape((2, rows, cols, chan_out), BF16),
             shape((frames, cols, chan_out), BF16),
             shape((frames, cols, chan_in), BF16),
@@ -416,7 +427,6 @@
     )
     from_odd = lax.ppermute(to_odd, "tm", odd_pairs)
     from_even = lax.ppermute(to_even, "tm", even_pairs)
-    sums = sums + swap(sums, "width", 1)
     g_edge = swap(g_rows, "width", 1)
     x_edge = swap(x_rows, "width", 1)
     x, g = x_near, g_near
@@ -441,15 +451,14 @@
         scalars=1,
     )
     next_edge = swap(next_edge, "width", 1)
-    if tm <= 4:
-        found = [sums] + [swap(sums, "tm", k) for k in range(1, tm)]
-        stats = jnp.stack(found)
-    else:
-        stats = sums[None]
-        for step in bits_of("tm"):
-            stats = jnp.concatenate([stats, swap(stats, "tm", step)], axis=0)
+    near = from_odd[2 * cells :].astype(F32)
+    near = (near[: 2 * frames, :chan_in] + near[2 * frames :, :chan_in]) + near[: 2 * frames, chan_in:]
+    stats = jnp.stack([sums, near])
+    for step in bits_of("tm")[1:]:
+        stats = jnp.concatenate([stats, swap(stats, "tm", step)], axis=0)
+    stats, next_edge, g_next, x_prev = together(stats, next_edge, g_next, x_prev)
+    stats = stats + swap(stats, "width", 1)
     stats = jnp.concatenate([stats, affine], axis=0)
-    stats, next_edge, x_prev = together(stats, next_edge, x_prev)
 
     share = 27 * chan_in // (tm * dp)
     pieces = share % 48 == 0 and tm == 4 and dp == 2

time: 50 us -> 48.9 us (0.978)
  waiting for transfers between devices: 10.7 us -> 9.79 us
    ppermute x18 -> x16, waiting for transfers between devices: 10.3 us -> 8.09 us  [swap(): lax.ppermute(value, axis, [(i, i ^ step) for i in range(lax.axis_size(axi...]
    ppermute x1, waiting for transfers between devices: 0.36 us -> 1.69 us  [body(): from_odd = lax.ppermute(to_odd, 'tm', odd_pairs)]
    ppermute x18 -> x16, starting transfers between devices: 17 us -> 16.9 us  [swap(): lax.ppermute(value, axis, [(i, i ^ step) for i in range(lax.axis_size(axi...]
    unnamed x12 -> x8, local copies, waits for them, and re-layouts: 1.5 us -> 1.49 us
  transfers between devices with their start and end apart: 20 -> 18, of which waited for: 10 -> 12; matrix products, arithmetic and copies ran while one was open for 0% -> 0% of each run, Pallas kernels for 20% -> 20%
where the time goes in v6:
time: 48.9 us; the launch traced here: 48.7 us
  starting transfers between devices  20.6 us (42%)
  Pallas kernels  15.9 us (33%)
  waiting for transfers between devices  9.79 us (20%)
  local copies, waits for them, and re-layouts  1.49 us (3%)
  between operations  0.76 us (2%)
    ppermute x16, starting transfers between devices, swap(): lax.ppermute(value, axis, [(i, i ^ step) for i in range(lax.axis_size(axi...  16.9 us
    pallas_call x10, Pallas kernels, call(): pl.pallas_call(kernel, out_shape=out_shape, in_specs=[SMEM] * scalars + [...  15.9 us
    ppermute x16, waiting for transfers between devices, swap(): lax.ppermute(value, axis, [(i, i ^ step) for i in range(lax.axis_size(axi...  8.09 us
    ppermute x1, starting transfers between devices, body(): from_odd = lax.ppermute(to_odd, 'tm', odd_pairs)  3.09 us
    ppermute x1, waiting for transfers between devices, body(): from_odd = lax.ppermute(to_odd, 'tm', odd_pairs)  1.69 us
    unnamed x8, local copies, waits for them, and re-layouts  1.49 us
  transfers between devices with their start and end apart: 18, of which 12 were waited for; matrix products, arithmetic and copies ran while one was open for 0% of the time, Pallas kernels for 20%

profile of v6, /device:TPU:0, one launch (start us, length us, event | category | flops | bytes accessed | tf_op | source)
XLA Modules:
  0.0 48.7 jit_solution(12670637414321353838)
XLA Ops:
  0.6 0.1 pad_add_fusion.place
  0.7 1.9 %shard_map.84 = (f32[8,128]{1,0:T(8,128)S(1)}, bf16[528,256]{1,0:T(8,128)(2,1)S(1)}, bf16[2,4,64,256]{3,2,1,0:T(8,128)(2,1)S(1)}, bf16[4,64,256]{2,1,0:T(8,128)(...) custom-call(s32[3]{0:T(128)S(1)} %pad_add_fusion.place, ...), custom_call_target="tpu_custom_call" | custom-call | bytes 2306060 | tf_op jit(solution)/shard_map/pallas_call | solution.py:21
  2.6 3.1 %collective-permute-start = (bf16[528,256]{1,0:T(8,128)(2,1)S(1)}, bf16[528,256]{1,0:T(8,128)(2,1)S(1)}, u32[]{:S(2)}, u32[]{:S(2)}) collective-permute-start(bf16[528,256]{1,0:T(8,128)(2,1)S(1)} %get-tuple-element.79), channel_id=1, source_target_pairs={{0,4},{4,0},{8,12},{12,8},{1,5},{5,1},{9,13},{13,9},{2,6},{6,2},{1... | collective-permute-start | bytes 811016 | tf_op jit(solution)/shard_map/ppermute | solution.py:428
  5.7 0.7 %collective-permute-start.1 = (bf16[2,4,64,256]{3,2,1,0:T(8,128)(2,1)S(1)}, bf16[2,4,64,256]{3,2,1,0:T(8,128)(2,1)S(1)}, u32[]{:S(2)}, u32[]{:S(2)}) collective-permute-start(bf16[2,4,64,256]{3,2,1,0:T(8,128)(2,1)S(1)} %get-tuple-element.80), channel_id=1, source_target_pairs={{4,8},{8,4},{5,9},{9,5},{6,10},{10,6},{7,11},{11,7},{20,24},{24,20... | collective-permute-start | bytes 786440 | tf_op jit(solution)/shard_map/ppermute | solution.py:429
  6.4 0.1 collective-permute-start.2
  6.5 0.5 %collective-permute-start.3 = (bf16[4,64,128]{2,1,0:T(8,128)(2,1)S(1)}, bf16[4,64,128]{2,1,0:T(8,128)(2,1)S(1)}, u32[]{:S(2)}, u32[]{:S(2)}) collective-permute-start(bf16[4,64,128]{2,1,0:T(8,128)(2,1)S(1)} %get-tuple-element.82), channel_id=1, source_target_pairs={{0,1},{1,0},{2,3},{3,2},{4,5},{5,4},{6,7},{7,6},{8,9},{9,8},{10,11... | collective-permute-start | bytes 196616 | tf_op jit(solution)/shard_map/ppermute | solution.py:373
  7.0 0.0 copy-start
  7.0 1.5 %copy-done = bf16[3456,256]{1,0:T(8,128)(2,1)S(1)} copy-done((bf16[3456,256]{1,0:T(8,128)(2,1)S(1)}, bf16[3456,256]{1,0:T(8,128)(2,1)}, u32[]{:S(2)}) %copy-start) | copy-done | bytes 1769496
  8.4 0.0 copy-start.2
  8.4 0.0 copy-start.3
  8.4 2.0 %shard_map.85.own_ref = f32[4,4,64,384]{3,2,1,0:T(8,128)S(1)} custom-call(bf16[4,4,64,256]{3,2,1,0:T(8,128)(2,1)S(1)} %get-tuple-element.83.g_ref, bf16[3456,256]{1,0:T(8,128)(2,1)S(1)} %copy-done), custom_call_target="tpu_custom_call" | custom-call | bytes 3866624 | tf_op jit(solution)/shard_map/pallas_call | solution.py:21
  10.5 0.0 copy-start.1
  10.5 0.0 collective-permute-done.3.edge_ref
  10.5 0.0 collective-permute-done.2.edge_ref
  10.5 0.0 collective-permute-done.1.even_ref
  10.5 1.7 %collective-permute-done.odd_ref = bf16[528,256]{1,0:T(8,128)(2,1)S(1)} collective-permute-done((bf16[528,256]{1,0:T(8,128)(2,1)S(1)}, bf16[528,256]{1,0:T(8,128)(2,1)S(1)}, u32[]{:S(2)}, u32[]{:S(2)}) %collective-permute-start) | collective-permute-done | bytes 270368 | tf_op jit(solution)/shard_map/ppermute | solution.py:428
  12.2 5.8 %collective-permute-start.4 = (f32[2,8,128]{2,1,0:T(8,128)S(1)}, f32[2,8,128]{2,1,0:T(8,128)S(1)}, u32[]{:S(2)}, u32[]{:S(2)}) collective-permute-start(f32[2,8,128]{2,1,0:T(8,128)S(1)} %pad_maximum_fusion.2), channel_id=1, source_target_pairs={{0,8},{4,12},{8,0},{12,4},{1,9},{5,13},{9,1},{13,5},{2,10},{6,14},... | collective-permute-start | bytes 24584 | tf_op jit(solution)/shard_map/ppermute | solution.py:373
  18.0 0.6 %shard_map.86 = (bf16[2,4,64,256]{3,2,1,0:T(8,128)(2,1)S(1)}, bf16[2,4,64,128]{3,2,1,0:T(8,128)(2,1)S(1)}, bf16[2,64,384]{2,1,0:T(8,128)(2,1)S(1)}) custom-call(s32[3]{0:T(128)S(1)} %pad_add_fusion.place, bf16[528,256]{1,0:T(8,128)(2,1)S(1)} %collective-permute-done.odd_ref, bf16[2,4,64,256]{3,2,1,0:T(8,128)(2,1)S(1)} %collective-permute-done.1.even_ref), custom_call_target="tpu_custom_call" | custom-call | bytes 1024012 | tf_op jit(solution)/shard_map/pallas_call | solution.py:21
  18.6 0.1 collective-permute-start.5
  18.7 0.9 %collective-permute-done.4 = f32[2,8,128]{2,1,0:T(8,128)S(1)} collective-permute-done((f32[2,8,128]{2,1,0:T(8,128)S(1)}, f32[2,8,128]{2,1,0:T(8,128)S(1)}, u32[]{:S(2)}, u32[]{:S(2)}) %collective-permute-start.4) | collective-permute-done | bytes 8224 | tf_op jit(solution)/shard_map/ppermute | solution.py:373
  19.7 0.3 collective-permute-done.5.edge_next.prev_edge
  20.0 0.2 collective-permute-start.6
  20.2 0.0 copy-done.2
  20.2 0.0 copy-done.3
  20.2 1.0 %collective-permute-done.6 = f32[4,8,128]{2,1,0:T(8,128)S(1)} collective-permute-done((f32[4,8,128]{2,1,0:T(8,128)S(1)}, f32[4,8,128]{2,1,0:T(8,128)S(1)}, u32[]{:S(2)}, u32[]{:S(2)}) %collective-permute-start.6) | collective-permute-done | bytes 16416 | tf_op jit(solution)/shard_map/ppermute | solution.py:373
  21.2 2.9 %shard_map.87 = (f32[3456,128]{1,0:T(8,128)S(1)}, bf16[3456,128]{1,0:T(8,128)(2,1)S(1)}) custom-call(s32[3]{0:T(128)S(1)} %pad_add_fusion.place, f32[5,8,128]{2,1,0:T(8,128)S(1)} %pad_maximum_fusion.stats_ref, bf16[2,4,64,256]{3,2,1,0:T(8,128)(2,1)S(1)} %get-tuple-element.91.next_ref, bf16[4,64,256]{2,1,0:T(8,128)(2,1)S(1)} %collective-permute-done.2.edge_ref, ...), custom_call_target="tpu_custom_call" | custom-call | bytes 3952652 | tf_op jit(solution)/shard_map/pallas_call | solution.py:21
  24.1 0.2 collective-permute-start.7
  24.3 0.0 copy-done.1
  24.3 1.8 %shard_map.88 = f32[2,128]{1,0:T(2,128)S(1)} custom-call(s32[3]{0:T(128)S(1)} %pad_add_fusion.place, f32[5,8,128]{2,1,0:T(8,128)S(1)} %pad_maximum_fusion.stats_ref, bf16[4,256,128]{2,1,0:T(8,128)(2,1)S(1)} %bitcast.17, f32[4,4,64,384]{3,2,1,0:T(8,128)S(1)} %shard_map.85.own_ref, bf16[2,4,64,256]{3,2,1,0:T(8,128)(2,1)S(1)} %get-tuple-element.91.next_ref, ...), custom_call_target="tpu_custom_call" | custom-call | bytes 4117516 | tf_op jit(solution)/shard_map/pallas_call | solution.py:21
  26.2 0.4 collective-permute-done.7.recv_ref
  26.6 0.2 collective-permute-start.8
  26.8 0.7 %shard_map.89 = (f32[1152,128]{1,0:T(8,128)S(1)}, bf16[1152,128]{1,0:T(8,128)(2,1)S(1)}, f32[288,128]{1,0:T(8,128)S(1)}, bf16[288,128]{1,0:T(8,128)(2,1)S(1)}, b...) custom-call(s32[3]{0:T(128)S(1)} %pad_add_fusion.place, f32[3456,128]{1,0:T(8,128)S(1)} %get-tuple-element.95.keep_ref, ...), custom_call_target="tpu_custom_call" | custom-call | bytes 3907596 | tf_op jit(solution)/shard_map/pallas_call | solution.py:21
  27.5 0.2 collective-permute-done.8
  27.7 1.5 %collective-permute-start.9 = (bf16[1152,128]{1,0:T(8,128)(2,1)S(1)}, bf16[1152,128]{1,0:T(8,128)(2,1)S(1)}, u32[]{:S(2)}, u32[]{:S(2)}) collective-permute-start(bf16[1152,128]{1,0:T(8,128)(2,1)S(1)} %get-tuple-element.107), channel_id=1, source_target_pairs={{0,2},{2,0},{1,3},{3,1},{4,6},{6,4},{5,7},{7,5},{8,10},{10,8},{9,1... | collective-permute-start | bytes 884744 | tf_op jit(solution)/shard_map/ppermute | solution.py:373
  29.2 2.6 %collective-permute-start.11 = (bf16[288,128]{1,0:T(8,128)(2,1)S(1)}, bf16[288,128]{1,0:T(8,128)(2,1)S(1)}, u32[]{:S(2)}, u32[]{:S(2)}) collective-permute-start(bf16[288,128]{1,0:T(8,128)(2,1)S(1)} %get-tuple-element.112), channel_id=1, source_target_pairs={{0,8},{4,12},{8,0},{12,4},{1,9},{5,13},{9,1},{13,5},{2,10},{6,14},... | collective-permute-start | bytes 221192 | tf_op jit(solution)/shard_map/ppermute | solution.py:373
  31.8 1.2 %collective-permute-start.12 = (bf16[288,128]{1,0:T(8,128)(2,1)S(1)}, bf16[288,128]{1,0:T(8,128)(2,1)S(1)}, u32[]{:S(2)}, u32[]{:S(2)}) collective-permute-start(bf16[288,128]{1,0:T(8,128)(2,1)S(1)} %get-tuple-element.113), channel_id=1, source_target_pairs={{0,12},{4,8},{8,4},{12,0},{1,13},{5,9},{9,5},{13,1},{2,14},{6,10},... | collective-permute-start | bytes 221192 | tf_op jit(solution)/shard_map/ppermute | solution.py:373
  33.0 0.0 collective-permute-start.13
  33.0 0.5 %collective-permute-start.10 = (f32[2,128]{1,0:T(2,128)S(1)}, f32[2,128]{1,0:T(2,128)S(1)}, u32[]{:S(2)}, u32[]{:S(2)}) collective-permute-start(f32[2,128]{1,0:T(2,128)S(1)} %add.17.rider_ref), channel_id=1, source_target_pairs={{0,2},{2,0},{1,3},{3,1},{4,6},{6,4},{5,7},{7,5},{8,10},{10,8},{9,1... | collective-permute-start | bytes 3080 | tf_op jit(solution)/shard_map/ppermute | solution.py:373
  33.5 1.1 %shard_map.90.h_ref = bf16[6,6,64,384]{3,2,1,0:T(8,128)(2,1)S(1)} custom-call(s32[3]{0:T(128)S(1)} %pad_add_fusion.place, f32[5,8,128]{2,1,0:T(8,128)S(1)} %pad_maximum_fusion.stats_ref, bf16[4,4,64,128]{3,2,1,0:T(8,128)(2,1)S(1)} %get-tuple-element.94.x_ref, bf16[2,4,64,128]{3,2,1,0:T(8,128)(2,1)S(1)} %get-tuple-element.110.prev_ref, ...), custom_call_target="tpu_custom_call" | custom-call | bytes 2347020 | tf_op jit(solution)/shard_map/pallas_call | solution.py:21
  34.7 2.2 %collective-permute-done.10.got_ref = f32[2,128]{1,0:T(2,128)S(1)} collective-permute-done((f32[2,128]{1,0:T(2,128)S(1)}, f32[2,128]{1,0:T(2,128)S(1)}, u32[]{:S(2)}, u32[]{:S(2)}) %collective-permute-start.10) | collective-permute-done | bytes 1056 | tf_op jit(solution)/shard_map/ppermute | solution.py:373
  36.9 0.7 %collective-permute-done.11.b_ref = bf16[288,128]{1,0:T(8,128)(2,1)S(1)} collective-permute-done((bf16[288,128]{1,0:T(8,128)(2,1)S(1)}, bf16[288,128]{1,0:T(8,128)(2,1)S(1)}, u32[]{:S(2)}, u32[]{:S(2)}) %collective-permute-start.11) | collective-permute-done | bytes 73760 | tf_op jit(solution)/shard_map/ppermute | solution.py:373
  37.6 0.8 %collective-permute-done.12.c_ref = bf16[288,128]{1,0:T(8,128)(2,1)S(1)} collective-permute-done((bf16[288,128]{1,0:T(8,128)(2,1)S(1)}, bf16[288,128]{1,0:T(8,128)(2,1)S(1)}, u32[]{:S(2)}, u32[]{:S(2)}) %collective-permute-start.12) | collective-permute-done | bytes 73760 | tf_op jit(solution)/shard_map/ppermute | solution.py:373
  38.4 0.5 collective-permute-done.13.a_ref
  38.8 0.0 collective-permute-done.9.recv1_ref
  38.8 0.6 %shard_map.91 = (f32[288,128]{1,0:T(8,128)S(1)}, bf16[304,128]{1,0:T(8,128)(2,1)S(1)}, bf16[304,128]{1,0:T(8,128)(2,1)S(1)}, bf16[304,128]{1,0:T(8,128)(2,1)S(1)...) custom-call(s32[3]{0:T(128)S(1)} %pad_add_fusion.place, ...), custom_call_target="tpu_custom_call" | custom-call | bytes 1747980 | tf_op jit(solution)/shard_map/pallas_call | solution.py:21
  39.5 1.0 %collective-permute-start.15 = (bf16[304,128]{1,0:T(8,128)(2,1)S(1)}, bf16[304,128]{1,0:T(8,128)(2,1)S(1)}, u32[]{:S(2)}, u32[]{:S(2)}) collective-permute-start(bf16[304,128]{1,0:T(8,128)(2,1)S(1)} %get-tuple-element.128), channel_id=1, source_target_pairs={{0,8},{4,12},{8,0},{12,4},{1,9},{5,13},{9,1},{13,5},{2,10},{6,14},... | collective-permute-start | bytes 233480 | tf_op jit(solution)/shard_map/ppermute | solution.py:373
  40.5 2.1 %collective-permute-start.16 = (bf16[304,128]{1,0:T(8,128)(2,1)S(1)}, bf16[304,128]{1,0:T(8,128)(2,1)S(1)}, u32[]{:S(2)}, u32[]{:S(2)}) collective-permute-start(bf16[304,128]{1,0:T(8,128)(2,1)S(1)} %get-tuple-element.129), channel_id=1, source_target_pairs={{0,12},{4,8},{8,4},{12,0},{1,13},{5,9},{9,5},{13,1},{2,14},{6,10},... | collective-permute-start | bytes 233480 | tf_op jit(solution)/shard_map/ppermute | solution.py:373
  42.6 0.4 collective-permute-start.17
  43.0 0.5 %collective-permute-start.14 = (bf16[144,128]{1,0:T(8,128)(2,1)S(1)}, bf16[144,128]{1,0:T(8,128)(2,1)S(1)}, u32[]{:S(2)}, u32[]{:S(2)}) collective-permute-start(bf16[144,128]{1,0:T(8,128)(2,1)S(1)} %get-tuple-element.126), channel_id=1, source_target_pairs={{0,2},{2,0},{1,3},{3,1},{4,6},{6,4},{5,7},{7,5},{8,10},{10,8},{9,1... | collective-permute-start | bytes 110600 | tf_op jit(solution)/shard_map/ppermute | solution.py:373
  43.6 3.4 %shard_map.92 = bf16[1024,256]{1,0:T(8,128)(2,1)} custom-call(bf16[6,6,64,384]{3,2,1,0:T(8,128)(2,1)S(1)} %shard_map.90.h_ref, bf16[3456,256]{1,0:T(8,128)(2,1)S(1)} %copy-done.1), custom_call_target="tpu_custom_call" | custom-call | bytes 4063232 | tf_op jit(solution)/shard_map/pallas_call | solution.py:21
  47.0 0.0 collective-permute-done.14.recv2_ref
  47.0 0.2 collective-permute-done.15.b_ref
  47.2 0.0 collective-permute-done.16.c_ref
  47.2 0.8 %collective-permute-done.17.a_ref = bf16[304,128]{1,0:T(8,128)(2,1)S(1)} collective-permute-done((bf16[304,128]{1,0:T(8,128)(2,1)S(1)}, bf16[304,128]{1,0:T(8,128)(2,1)S(1)}, u32[]{:S(2)}, u32[]{:S(2)}) %collective-permute-start.17) | collective-permute-done | bytes 77856 | tf_op jit(solution)/shard_map/ppermute | solution.py:373
  47.9 0.7 %shard_map.93 = (f32[432,128]{1,0:T(8,128)}, f32[1,128]{1,0:T(1,128)}, f32[1,128]{1,0:T(1,128)}) custom-call(f32[288,128]{1,0:T(8,128)S(1)} %get-tuple-element.132.stay1_ref, bf16[304,128]{1,0:T(8,128)(2,1)S(1)} %collective-permute-done.15.b_ref, bf16[304,128]{1,0:T(8,128)(2,1)S(1)} %collective-permute-done.16.c_ref, ...), custom_call_target="tpu_custom_call" | custom-call | bytes 714752 | tf_op jit(solution)/shard_map/pallas_call | solution.py:21
  (8 shorter events, 0.0 us)
Async XLA Ops:
  2.6 9.6 %collective-permute-start = (bf16[528,256]{1,0:T(8,128)(2,1)S(1)}, bf16[528,256]{1,0:T(8,128)(2,1)S(1)}, u32[]{:S(2)}, u32[]{:S(2)}) collective-permute-start(bf16[528,256]{1,0:T(8,128)(2,1)S(1)} %get-tuple-element.79), channel_id=1, source_target_pairs={{0,4},{4,0},{8,12},{12,8},{1,5},{5,1},{9,13},{13,9},{2,6},{6,2},{1... | collective-permute-start | bytes 811016 | tf_op jit(solution)/shard_map/ppermute | solution.py:428
  5.7 4.8 %collective-permute-start.1 = (bf16[2,4,64,256]{3,2,1,0:T(8,128)(2,1)S(1)}, bf16[2,4,64,256]{3,2,1,0:T(8,128)(2,1)S(1)}, u32[]{:S(2)}, u32[]{:S(2)}) collective-permute-start(bf16[2,4,64,256]{3,2,1,0:T(8,128)(2,1)S(1)} %get-tuple-element.80), channel_id=1, source_target_pairs={{4,8},{8,4},{5,9},{9,5},{6,10},{10,6},{7,11},{11,7},{20,24},{24,20... | collective-permute-start | bytes 786440 | tf_op jit(solution)/shard_map/ppermute | solution.py:429
  6.4 4.1 %collective-permute-start.2 = (bf16[4,64,256]{2,1,0:T(8,128)(2,1)S(1)}, bf16[4,64,256]{2,1,0:T(8,128)(2,1)S(1)}, u32[]{:S(2)}, u32[]{:S(2)}) collective-permute-start(bf16[4,64,256]{2,1,0:T(8,128)(2,1)S(1)} %get-tuple-element.81), channel_id=1, source_target_pairs={{0,1},{1,0},{2,3},{3,2},{4,5},{5,4},{6,7},{7,6},{8,9},{9,8},{10,11... | collective-permute-start | bytes 393224 | tf_op jit(solution)/shard_map/ppermute | solution.py:373
  6.5 4.0 %collective-permute-start.3 = (bf16[4,64,128]{2,1,0:T(8,128)(2,1)S(1)}, bf16[4,64,128]{2,1,0:T(8,128)(2,1)S(1)}, u32[]{:S(2)}, u32[]{:S(2)}) collective-permute-start(bf16[4,64,128]{2,1,0:T(8,128)(2,1)S(1)} %get-tuple-element.82), channel_id=1, source_target_pairs={{0,1},{1,0},{2,3},{3,2},{4,5},{5,4},{6,7},{7,6},{8,9},{9,8},{10,11... | collective-permute-start | bytes 196616 | tf_op jit(solution)/shard_map/ppermute | solution.py:373
  7.0 1.5 %copy-start = (bf16[3456,256]{1,0:T(8,128)(2,1)S(1)}, bf16[3456,256]{1,0:T(8,128)(2,1)}, u32[]{:S(2)}) copy-start(bf16[3456,256]{1,0:T(8,128)(2,1)} %w_ref.5) | copy-start | bytes 5308420
  8.4 11.7 %copy-start.2 = (f32[128]{0:T(128)S(1)}, f32[128]{0:T(128)}, u32[]{:S(2)}) copy-start(f32[128]{0:T(128)} %param.7) | copy-start | bytes 1540
  8.4 11.7 %copy-start.3 = (f32[128]{0:T(128)S(1)}, f32[128]{0:T(128)}, u32[]{:S(2)}) copy-start(f32[128]{0:T(128)} %param.6) | copy-start | bytes 1540
  10.5 13.9 %copy-start.1 = (bf16[3456,256]{1,0:T(8,128)(2,1)S(1)}, bf16[3456,256]{1,0:T(8,128)(2,1)}, u32[]{:S(2)}) copy-start(bf16[3456,256]{1,0:T(8,128)(2,1)} %w_ref.5) | copy-start | bytes 5308420
  12.2 7.5 %collective-permute-start.4 = (f32[2,8,128]{2,1,0:T(8,128)S(1)}, f32[2,8,128]{2,1,0:T(8,128)S(1)}, u32[]{:S(2)}, u32[]{:S(2)}) collective-permute-start(f32[2,8,128]{2,1,0:T(8,128)S(1)} %pad_maximum_fusion.2), channel_id=1, source_target_pairs={{0,8},{4,12},{8,0},{12,4},{1,9},{5,13},{9,1},{13,5},{2,10},{6,14},... | collective-permute-start | bytes 24584 | tf_op jit(solution)/shard_map/ppermute | solution.py:373
  18.6 1.4 %collective-permute-start.5 = (bf16[2,64,384]{2,1,0:T(8,128)(2,1)S(1)}, bf16[2,64,384]{2,1,0:T(8,128)(2,1)S(1)}, u32[]{:S(2)}, u32[]{:S(2)}) collective-permute-start(bf16[2,64,384]{2,1,0:T(8,128)(2,1)S(1)} %get-tuple-element.87), channel_id=1, source_target_pairs={{0,1},{1,0},{2,3},{3,2},{4,5},{5,4},{6,7},{7,6},{8,9},{9,8},{10,11... | collective-permute-start | bytes 294920 | tf_op jit(solution)/shard_map/ppermute | solution.py:373
  20.0 1.2 %collective-permute-start.6 = (f32[4,8,128]{2,1,0:T(8,128)S(1)}, f32[4,8,128]{2,1,0:T(8,128)S(1)}, u32[]{:S(2)}, u32[]{:S(2)}) collective-permute-start(f32[4,8,128]{2,1,0:T(8,128)S(1)} %pad_maximum_fusion.1), channel_id=1, source_target_pairs={{0,1},{1,0},{2,3},{3,2},{4,5},{5,4},{6,7},{7,6},{8,9},{9,8},{10,11... | collective-permute-start | bytes 49160 | tf_op jit(solution)/shard_map/ppermute | solution.py:373
  24.1 2.5 %collective-permute-start.7 = (bf16[3456,128]{1,0:T(8,128)(2,1)S(1)}, bf16[3456,128]{1,0:T(8,128)(2,1)S(1)}, u32[]{:S(2)}, u32[]{:S(2)}) collective-permute-start(bf16[3456,128]{1,0:T(8,128)(2,1)S(1)} %get-tuple-element.97), channel_id=1, source_target_pairs={{0,1},{1,0},{2,3},{3,2},{4,5},{5,4},{6,7},{7,6},{8,9},{9,8},{10,11... | collective-permute-start | bytes 2654216 | tf_op jit(solution)/shard_map/ppermute | solution.py:373
  26.6 1.1 %collective-permute-start.8 = (f32[2,128]{1,0:T(2,128)S(1)}, f32[2,128]{1,0:T(2,128)S(1)}, u32[]{:S(2)}, u32[]{:S(2)}) collective-permute-start(f32[2,128]{1,0:T(2,128)S(1)} %shard_map.88), channel_id=1, source_target_pairs={{0,1},{1,0},{2,3},{3,2},{4,5},{5,4},{6,7},{7,6},{8,9},{9,8},{10,11... | collective-permute-start | bytes 3080 | tf_op jit(solution)/shard_map/ppermute | solution.py:373
  27.7 11.1 %collective-permute-start.9 = (bf16[1152,128]{1,0:T(8,128)(2,1)S(1)}, bf16[1152,128]{1,0:T(8,128)(2,1)S(1)}, u32[]{:S(2)}, u32[]{:S(2)}) collective-permute-start(bf16[1152,128]{1,0:T(8,128)(2,1)S(1)} %get-tuple-element.107), channel_id=1, source_target_pairs={{0,2},{2,0},{1,3},{3,1},{4,6},{6,4},{5,7},{7,5},{8,10},{10,8},{9,1... | collective-permute-start | bytes 884744 | tf_op jit(solution)/shard_map/ppermute | solution.py:373
  29.2 8.3 %collective-permute-start.11 = (bf16[288,128]{1,0:T(8,128)(2,1)S(1)}, bf16[288,128]{1,0:T(8,128)(2,1)S(1)}, u32[]{:S(2)}, u32[]{:S(2)}) collective-permute-start(bf16[288,128]{1,0:T(8,128)(2,1)S(1)} %get-tuple-element.112), channel_id=1, source_target_pairs={{0,8},{4,12},{8,0},{12,4},{1,9},{5,13},{9,1},{13,5},{2,10},{6,14},... | collective-permute-start | bytes 221192 | tf_op jit(solution)/shard_map/ppermute | solution.py:373
  31.8 6.6 %collective-permute-start.12 = (bf16[288,128]{1,0:T(8,128)(2,1)S(1)}, bf16[288,128]{1,0:T(8,128)(2,1)S(1)}, u32[]{:S(2)}, u32[]{:S(2)}) collective-permute-start(bf16[288,128]{1,0:T(8,128)(2,1)S(1)} %get-tuple-element.113), channel_id=1, source_target_pairs={{0,12},{4,8},{8,4},{12,0},{1,13},{5,9},{9,5},{13,1},{2,14},{6,10},... | collective-permute-start | bytes 221192 | tf_op jit(solution)/shard_map/ppermute | solution.py:373
  33.0 5.8 %collective-permute-start.13 = (bf16[288,128]{1,0:T(8,128)(2,1)S(1)}, bf16[288,128]{1,0:T(8,128)(2,1)S(1)}, u32[]{:S(2)}, u32[]{:S(2)}) collective-permute-start(bf16[288,128]{1,0:T(8,128)(2,1)S(1)} %get-tuple-element.114), channel_id=1, source_target_pairs={{0,4},{4,0},{8,12},{12,8},{1,5},{5,1},{9,13},{13,9},{2,6},{6,2},{1... | collective-permute-start | bytes 221192 | tf_op jit(solution)/shard_map/ppermute | solution.py:373
  33.0 3.9 %collective-permute-start.10 = (f32[2,128]{1,0:T(2,128)S(1)}, f32[2,128]{1,0:T(2,128)S(1)}, u32[]{:S(2)}, u32[]{:S(2)}) collective-permute-start(f32[2,128]{1,0:T(2,128)S(1)} %add.17.rider_ref), channel_id=1, source_target_pairs={{0,2},{2,0},{1,3},{3,1},{4,6},{6,4},{5,7},{7,5},{8,10},{10,8},{9,1... | collective-permute-start | bytes 3080 | tf_op jit(solution)/shard_map/ppermute | solution.py:373
  39.5 7.7 %collective-permute-start.15 = (bf16[304,128]{1,0:T(8,128)(2,1)S(1)}, bf16[304,128]{1,0:T(8,128)(2,1)S(1)}, u32[]{:S(2)}, u32[]{:S(2)}) collective-permute-start(bf16[304,128]{1,0:T(8,128)(2,1)S(1)} %get-tuple-element.128), channel_id=1, source_target_pairs={{0,8},{4,12},{8,0},{12,4},{1,9},{5,13},{9,1},{13,5},{2,10},{6,14},... | collective-permute-start | bytes 233480 | tf_op jit(solution)/shard_map/ppermute | solution.py:373
  40.5 6.7 %collective-permute-start.16 = (bf16[304,128]{1,0:T(8,128)(2,1)S(1)}, bf16[304,128]{1,0:T(8,128)(2,1)S(1)}, u32[]{:S(2)}, u32[]{:S(2)}) collective-permute-start(bf16[304,128]{1,0:T(8,128)(2,1)S(1)} %get-tuple-element.129), channel_id=1, source_target_pairs={{0,12},{4,8},{8,4},{12,0},{1,13},{5,9},{9,5},{13,1},{2,14},{6,10},... | collective-permute-start | bytes 233480 | tf_op jit(solution)/shard_map/ppermute | solution.py:373
  42.6 5.3 %collective-permute-start.17 = (bf16[304,128]{1,0:T(8,128)(2,1)S(1)}, bf16[304,128]{1,0:T(8,128)(2,1)S(1)}, u32[]{:S(2)}, u32[]{:S(2)}) collective-permute-start(bf16[304,128]{1,0:T(8,128)(2,1)S(1)} %get-tuple-element.130), channel_id=1, source_target_pairs={{0,4},{4,0},{8,12},{12,8},{1,5},{5,1},{9,13},{13,9},{2,6},{6,2},{1... | collective-permute-start | bytes 233480 | tf_op jit(solution)/shard_map/ppermute | solution.py:373
  43.0 4.0 %collective-permute-start.14 = (bf16[144,128]{1,0:T(8,128)(2,1)S(1)}, bf16[144,128]{1,0:T(8,128)(2,1)S(1)}, u32[]{:S(2)}, u32[]{:S(2)}) collective-permute-start(bf16[144,128]{1,0:T(8,128)(2,1)S(1)} %get-tuple-element.126), channel_id=1, source_target_pairs={{0,2},{2,0},{1,3},{3,1},{4,6},{6,4},{5,7},{7,5},{8,10},{10,8},{9,1... | collective-permute-start | bytes 110600 | tf_op jit(solution)/shard_map/ppermute | solution.py:373

commit v7 on v6

--- a/solution.py
+++ b/solution.py
@@ -438,7 +438,7 @@
         [g, weight],
         [pltpu.VMEM((frames, rows + 2, cols, chan_out), BF16)],
     )
-    sums, from_odd, from_even, g_edge, x_edge, own_grad = together(sums, from_odd, from_even, g_edge, x_edge, own_grad)
+    sums, from_odd, g_edge, x_edge, own_grad = together(sums, from_odd, g_edge, x_edge, own_grad)
 
     g_next, x_prev, next_edge = call(
         arrived_kernel,

time: 48.9 us -> 47.3 us (0.967)
  starting transfers between devices: 20.6 us -> 18.5 us
  waiting for transfers between devices: 9.79 us -> 10.4 us
    ppermute x16, starting transfers between devices: 16.9 us -> 14.7 us  [swap(): lax.ppermute(value, axis, [(i, i ^ step) for i in range(lax.axis_size(axi...]
    ppermute x16, waiting for transfers between devices: 8.09 us -> 8.64 us  [swap(): lax.ppermute(value, axis, [(i, i ^ step) for i in range(lax.axis_size(axi...]
  transfers between devices with their start and end apart: 18 -> 18, of which waited for: 12 -> 11; matrix products, arithmetic and copies ran while one was open for 0% -> 0% of each run, Pallas kernels for 20% -> 21%
where the time goes in v7:
time: 47.3 us; the launch traced here: 47.1 us
  starting transfers between devices  18.5 us (39%)
  Pallas kernels  15.9 us (34%)
  waiting for transfers between devices  10.4 us (22%)
  local copies, waits for them, and re-layouts  1.49 us (3%)
  between operations  0.77 us (2%)
    pallas_call x10, Pallas kernels, call(): pl.pallas_call(kernel, out_shape=out_shape, in_specs=[SMEM] * scalars + [...  15.9 us
    ppermute x16, starting transfers between devices, swap(): lax.ppermute(value, axis, [(i, i ^ step) for i in range(lax.axis_size(axi...  14.7 us
    ppermute x16, waiting for transfers between devices, swap(): lax.ppermute(value, axis, [(i, i ^ step) for i in range(lax.axis_size(axi...  8.64 us
    ppermute x1, starting transfers between devices, body(): from_odd = lax.ppermute(to_odd, 'tm', odd_pairs)  3.09 us
    ppermute x1, waiting for transfers between devices, body(): from_odd = lax.ppermute(to_odd, 'tm', odd_pairs)  1.76 us
    unnamed x8, local copies, waits for them, and re-layouts  1.49 us
  transfers between devices with their start and end apart: 18, of which 11 were waited for; matrix products, arithmetic and copies ran while one was open for 0% of the time, Pallas kernels for 21%

profile of v7, /device:TPU:0, one launch (start us, length us, event | category | flops | bytes accessed | tf_op | source)
XLA Modules:
  0.0 47.1 jit_solution(9975215085784848557)
XLA Ops:
  0.6 0.1 pad_add_fusion.place
  0.7 1.9 %shard_map.84 = (f32[8,128]{1,0:T(8,128)S(1)}, bf16[528,256]{1,0:T(8,128)(2,1)S(1)}, bf16[2,4,64,256]{3,2,1,0:T(8,128)(2,1)S(1)}, bf16[4,64,256]{2,1,0:T(8,128)(...) custom-call(s32[3]{0:T(128)S(1)} %pad_add_fusion.place, ...), custom_call_target="tpu_custom_call" | custom-call | bytes 2306060 | tf_op jit(solution)/shard_map/pallas_call | solution.py:21
  2.6 3.1 %collective-permute-start = (bf16[528,256]{1,0:T(8,128)(2,1)S(1)}, bf16[528,256]{1,0:T(8,128)(2,1)S(1)}, u32[]{:S(2)}, u32[]{:S(2)}) collective-permute-start(bf16[528,256]{1,0:T(8,128)(2,1)S(1)} %get-tuple-element.78), channel_id=1, source_target_pairs={{0,4},{4,0},{8,12},{12,8},{1,5},{5,1},{9,13},{13,9},{2,6},{6,2},{1... | collective-permute-start | bytes 811016 | tf_op jit(solution)/shard_map/ppermute | solution.py:428
  5.7 0.0 collective-permute-start.1
  5.7 0.5 %collective-permute-start.2 = (bf16[4,64,128]{2,1,0:T(8,128)(2,1)S(1)}, bf16[4,64,128]{2,1,0:T(8,128)(2,1)S(1)}, u32[]{:S(2)}, u32[]{:S(2)}) collective-permute-start(bf16[4,64,128]{2,1,0:T(8,128)(2,1)S(1)} %get-tuple-element.80), channel_id=1, source_target_pairs={{0,1},{1,0},{2,3},{3,2},{4,5},{5,4},{6,7},{7,6},{8,9},{9,8},{10,11... | collective-permute-start | bytes 196616 | tf_op jit(solution)/shard_map/ppermute | solution.py:373
  6.2 0.7 %collective-permute-start.4 = (bf16[2,4,64,256]{3,2,1,0:T(8,128)(2,1)S(1)}, bf16[2,4,64,256]{3,2,1,0:T(8,128)(2,1)S(1)}, u32[]{:S(2)}, u32[]{:S(2)}) collective-permute-start(bf16[2,4,64,256]{3,2,1,0:T(8,128)(2,1)S(1)} %get-tuple-element.84), channel_id=1, source_target_pairs={{4,8},{8,4},{5,9},{9,5},{6,10},{10,6},{7,11},{11,7},{20,24},{24,20... | collective-permute-start | bytes 786440 | tf_op jit(solution)/shard_map/ppermute | solution.py:429
  6.9 0.0 copy-start
  6.9 1.5 %copy-done = bf16[3456,256]{1,0:T(8,128)(2,1)S(1)} copy-done((bf16[3456,256]{1,0:T(8,128)(2,1)S(1)}, bf16[3456,256]{1,0:T(8,128)(2,1)}, u32[]{:S(2)}) %copy-start) | copy-done | bytes 1769496
  8.4 0.0 copy-start.2
  8.4 0.0 copy-start.3
  8.4 2.0 %shard_map.85.own_ref = f32[4,4,64,384]{3,2,1,0:T(8,128)S(1)} custom-call(bf16[4,4,64,256]{3,2,1,0:T(8,128)(2,1)S(1)} %get-tuple-element.81.g_ref, bf16[3456,256]{1,0:T(8,128)(2,1)S(1)} %copy-done), custom_call_target="tpu_custom_call" | custom-call | bytes 3866624 | tf_op jit(solution)/shard_map/pallas_call | solution.py:21
  10.4 0.0 copy-start.1
  10.4 0.0 collective-permute-done.2.edge_ref
  10.4 0.0 collective-permute-done.1.edge_ref
  10.4 1.8 %collective-permute-done.odd_ref = bf16[528,256]{1,0:T(8,128)(2,1)S(1)} collective-permute-done((bf16[528,256]{1,0:T(8,128)(2,1)S(1)}, bf16[528,256]{1,0:T(8,128)(2,1)S(1)}, u32[]{:S(2)}, u32[]{:S(2)}) %collective-permute-start) | collective-permute-done | bytes 270368 | tf_op jit(solution)/shard_map/ppermute | solution.py:428
  12.2 2.8 %collective-permute-start.3 = (f32[2,8,128]{2,1,0:T(8,128)S(1)}, f32[2,8,128]{2,1,0:T(8,128)S(1)}, u32[]{:S(2)}, u32[]{:S(2)}) collective-permute-start(f32[2,8,128]{2,1,0:T(8,128)S(1)} %pad_maximum_fusion.2), channel_id=1, source_target_pairs={{0,8},{4,12},{8,0},{12,4},{1,9},{5,13},{9,1},{13,5},{2,10},{6,14},... | collective-permute-start | bytes 24584 | tf_op jit(solution)/shard_map/ppermute | solution.py:373
  15.0 0.0 collective-permute-done.4.even_ref
  15.0 0.6 %shard_map.86 = (bf16[2,4,64,256]{3,2,1,0:T(8,128)(2,1)S(1)}, bf16[2,4,64,128]{3,2,1,0:T(8,128)(2,1)S(1)}, bf16[2,64,384]{2,1,0:T(8,128)(2,1)S(1)}) custom-call(s32[3]{0:T(128)S(1)} %pad_add_fusion.place, bf16[528,256]{1,0:T(8,128)(2,1)S(1)} %collective-permute-done.odd_ref, bf16[2,4,64,256]{3,2,1,0:T(8,128)(2,1)S(1)} %collective-permute-done.4.even_ref), custom_call_target="tpu_custom_call" | custom-call | bytes 1024012 | tf_op jit(solution)/shard_map/pallas_call | solution.py:21
  15.6 0.1 collective-permute-start.5
  15.7 1.6 %collective-permute-done.3 = f32[2,8,128]{2,1,0:T(8,128)S(1)} collective-permute-done((f32[2,8,128]{2,1,0:T(8,128)S(1)}, f32[2,8,128]{2,1,0:T(8,128)S(1)}, u32[]{:S(2)}, u32[]{:S(2)}) %collective-permute-start.3) | collective-permute-done | bytes 8224 | tf_op jit(solution)/shard_map/ppermute | solution.py:373
  17.4 0.0 collective-permute-done.5.edge_next.prev_edge
  17.4 0.0 collective-permute-start.6
  17.4 0.0 copy-done.2
  17.4 0.0 copy-done.3
  17.4 1.1 %collective-permute-done.6 = f32[4,8,128]{2,1,0:T(8,128)S(1)} collective-permute-done((f32[4,8,128]{2,1,0:T(8,128)S(1)}, f32[4,8,128]{2,1,0:T(8,128)S(1)}, u32[]{:S(2)}, u32[]{:S(2)}) %collective-permute-start.6) | collective-permute-done | bytes 16416 | tf_op jit(solution)/shard_map/ppermute | solution.py:373
  18.6 2.9 %shard_map.87 = (f32[3456,128]{1,0:T(8,128)S(1)}, bf16[3456,128]{1,0:T(8,128)(2,1)S(1)}) custom-call(s32[3]{0:T(128)S(1)} %pad_add_fusion.place, f32[5,8,128]{2,1,0:T(8,128)S(1)} %pad_maximum_fusion.stats_ref, bf16[2,4,64,256]{3,2,1,0:T(8,128)(2,1)S(1)} %get-tuple-element.89.next_ref, bf16[4,64,256]{2,1,0:T(8,128)(2,1)S(1)} %collective-permute-done.1.edge_ref, ...), custom_call_target="tpu_custom_call" | custom-call | bytes 3952652 | tf_op jit(solution)/shard_map/pallas_call | solution.py:21
  21.4 0.2 collective-permute-start.7
  21.7 0.0 copy-done.1
  21.7 1.8 %shard_map.88 = f32[2,128]{1,0:T(2,128)S(1)} custom-call(s32[3]{0:T(128)S(1)} %pad_add_fusion.place, f32[5,8,128]{2,1,0:T(8,128)S(1)} %pad_maximum_fusion.stats_ref, bf16[4,256,128]{2,1,0:T(8,128)(2,1)S(1)} %bitcast.17, f32[4,4,64,384]{3,2,1,0:T(8,128)S(1)} %shard_map.85.own_ref, bf16[2,4,64,256]{3,2,1,0:T(8,128)(2,1)S(1)} %get-tuple-element.89.next_ref, ...), custom_call_target="tpu_custom_call" | custom-call | bytes 4117516 | tf_op jit(solution)/shard_map/pallas_call | solution.py:21
  23.5 0.4 collective-permute-done.7.recv_ref
  23.9 0.2 collective-permute-start.8
  24.1 0.7 %shard_map.89 = (f32[1152,128]{1,0:T(8,128)S(1)}, bf16[1152,128]{1,0:T(8,128)(2,1)S(1)}, f32[288,128]{1,0:T(8,128)S(1)}, bf16[288,128]{1,0:T(8,128)(2,1)S(1)}, b...) custom-call(s32[3]{0:T(128)S(1)} %pad_add_fusion.place, f32[3456,128]{1,0:T(8,128)S(1)} %get-tuple-element.93.keep_ref, ...), custom_call_target="tpu_custom_call" | custom-call | bytes 3907596 | tf_op jit(solution)/shard_map/pallas_call | solution.py:21
  24.8 0.3 collective-permute-done.8
  25.1 1.5 %collective-permute-start.9 = (bf16[1152,128]{1,0:T(8,128)(2,1)S(1)}, bf16[1152,128]{1,0:T(8,128)(2,1)S(1)}, u32[]{:S(2)}, u32[]{:S(2)}) collective-permute-start(bf16[1152,128]{1,0:T(8,128)(2,1)S(1)} %get-tuple-element.105), channel_id=1, source_target_pairs={{0,2},{2,0},{1,3},{3,1},{4,6},{6,4},{5,7},{7,5},{8,10},{10,8},{9,1... | collective-permute-start | bytes 884744 | tf_op jit(solution)/shard_map/ppermute | solution.py:373
  26.6 3.7 %collective-permute-start.11 = (bf16[288,128]{1,0:T(8,128)(2,1)S(1)}, bf16[288,128]{1,0:T(8,128)(2,1)S(1)}, u32[]{:S(2)}, u32[]{:S(2)}) collective-permute-start(bf16[288,128]{1,0:T(8,128)(2,1)S(1)} %get-tuple-element.110), channel_id=1, source_target_pairs={{0,8},{4,12},{8,0},{12,4},{1,9},{5,13},{9,1},{13,5},{2,10},{6,14},... | collective-permute-start | bytes 221192 | tf_op jit(solution)/shard_map/ppermute | solution.py:373
  30.3 1.1 %collective-permute-start.12 = (bf16[288,128]{1,0:T(8,128)(2,1)S(1)}, bf16[288,128]{1,0:T(8,128)(2,1)S(1)}, u32[]{:S(2)}, u32[]{:S(2)}) collective-permute-start(bf16[288,128]{1,0:T(8,128)(2,1)S(1)} %get-tuple-element.111), channel_id=1, source_target_pairs={{0,12},{4,8},{8,4},{12,0},{1,13},{5,9},{9,5},{13,1},{2,14},{6,10},... | collective-permute-start | bytes 221192 | tf_op jit(solution)/shard_map/ppermute | solution.py:373
  31.4 0.0 collective-permute-start.13
  31.4 0.5 %collective-permute-start.10 = (f32[2,128]{1,0:T(2,128)S(1)}, f32[2,128]{1,0:T(2,128)S(1)}, u32[]{:S(2)}, u32[]{:S(2)}) collective-permute-start(f32[2,128]{1,0:T(2,128)S(1)} %add.17.rider_ref), channel_id=1, source_target_pairs={{0,2},{2,0},{1,3},{3,1},{4,6},{6,4},{5,7},{7,5},{8,10},{10,8},{9,1... | collective-permute-start | bytes 3080 | tf_op jit(solution)/shard_map/ppermute | solution.py:373
  31.9 1.1 %shard_map.90.h_ref = bf16[6,6,64,384]{3,2,1,0:T(8,128)(2,1)S(1)} custom-call(s32[3]{0:T(128)S(1)} %pad_add_fusion.place, f32[5,8,128]{2,1,0:T(8,128)S(1)} %pad_maximum_fusion.stats_ref, bf16[4,4,64,128]{3,2,1,0:T(8,128)(2,1)S(1)} %get-tuple-element.92.x_ref, bf16[2,4,64,128]{3,2,1,0:T(8,128)(2,1)S(1)} %get-tuple-element.108.prev_ref, ...), custom_call_target="tpu_custom_call" | custom-call | bytes 2347020 | tf_op jit(solution)/shard_map/pallas_call | solution.py:21
  33.1 1.9 %collective-permute-done.10.got_ref = f32[2,128]{1,0:T(2,128)S(1)} collective-permute-done((f32[2,128]{1,0:T(2,128)S(1)}, f32[2,128]{1,0:T(2,128)S(1)}, u32[]{:S(2)}, u32[]{:S(2)}) %collective-permute-start.10) | collective-permute-done | bytes 1056 | tf_op jit(solution)/shard_map/ppermute | solution.py:373
  34.9 0.7 %collective-permute-done.11.b_ref = bf16[288,128]{1,0:T(8,128)(2,1)S(1)} collective-permute-done((bf16[288,128]{1,0:T(8,128)(2,1)S(1)}, bf16[288,128]{1,0:T(8,128)(2,1)S(1)}, u32[]{:S(2)}, u32[]{:S(2)}) %collective-permute-start.11) | collective-permute-done | bytes 73760 | tf_op jit(solution)/shard_map/ppermute | solution.py:373
  35.6 1.2 %collective-permute-done.12.c_ref = bf16[288,128]{1,0:T(8,128)(2,1)S(1)} collective-permute-done((bf16[288,128]{1,0:T(8,128)(2,1)S(1)}, bf16[288,128]{1,0:T(8,128)(2,1)S(1)}, u32[]{:S(2)}, u32[]{:S(2)}) %collective-permute-start.12) | collective-permute-done | bytes 73760 | tf_op jit(solution)/shard_map/ppermute | solution.py:373
  36.8 0.2 collective-permute-done.13.a_ref
  37.1 0.0 collective-permute-done.9.recv1_ref
  37.1 0.6 %shard_map.91 = (f32[288,128]{1,0:T(8,128)S(1)}, bf16[304,128]{1,0:T(8,128)(2,1)S(1)}, bf16[304,128]{1,0:T(8,128)(2,1)S(1)}, bf16[304,128]{1,0:T(8,128)(2,1)S(1)...) custom-call(s32[3]{0:T(128)S(1)} %pad_add_fusion.place, ...), custom_call_target="tpu_custom_call" | custom-call | bytes 1747980 | tf_op jit(solution)/shard_map/pallas_call | solution.py:21
  37.7 1.6 %collective-permute-start.15 = (bf16[304,128]{1,0:T(8,128)(2,1)S(1)}, bf16[304,128]{1,0:T(8,128)(2,1)S(1)}, u32[]{:S(2)}, u32[]{:S(2)}) collective-permute-start(bf16[304,128]{1,0:T(8,128)(2,1)S(1)} %get-tuple-element.126), channel_id=1, source_target_pairs={{0,8},{4,12},{8,0},{12,4},{1,9},{5,13},{9,1},{13,5},{2,10},{6,14},... | collective-permute-start | bytes 233480 | tf_op jit(solution)/shard_map/ppermute | solution.py:373
  39.4 1.6 %collective-permute-start.16 = (bf16[304,128]{1,0:T(8,128)(2,1)S(1)}, bf16[304,128]{1,0:T(8,128)(2,1)S(1)}, u32[]{:S(2)}, u32[]{:S(2)}) collective-permute-start(bf16[304,128]{1,0:T(8,128)(2,1)S(1)} %get-tuple-element.127), channel_id=1, source_target_pairs={{0,12},{4,8},{8,4},{12,0},{1,13},{5,9},{9,5},{13,1},{2,14},{6,10},... | collective-permute-start | bytes 233480 | tf_op jit(solution)/shard_map/ppermute | solution.py:373
  41.0 0.3 collective-permute-start.17
  41.3 0.5 %collective-permute-start.14 = (bf16[144,128]{1,0:T(8,128)(2,1)S(1)}, bf16[144,128]{1,0:T(8,128)(2,1)S(1)}, u32[]{:S(2)}, u32[]{:S(2)}) collective-permute-start(bf16[144,128]{1,0:T(8,128)(2,1)S(1)} %get-tuple-element.124), channel_id=1, source_target_pairs={{0,2},{2,0},{1,3},{3,1},{4,6},{6,4},{5,7},{7,5},{8,10},{10,8},{9,1... | collective-permute-start | bytes 110600 | tf_op jit(solution)/shard_map/ppermute | solution.py:373
  41.8 3.4 %shard_map.92 = bf16[1024,256]{1,0:T(8,128)(2,1)} custom-call(bf16[6,6,64,384]{3,2,1,0:T(8,128)(2,1)S(1)} %shard_map.90.h_ref, bf16[3456,256]{1,0:T(8,128)(2,1)S(1)} %copy-done.1), custom_call_target="tpu_custom_call" | custom-call | bytes 4063232 | tf_op jit(solution)/shard_map/pallas_call | solution.py:21
  45.2 0.0 collective-permute-done.14.recv2_ref
  45.2 0.0 collective-permute-done.15.b_ref
  45.2 0.5 %collective-permute-done.16.c_ref = bf16[304,128]{1,0:T(8,128)(2,1)S(1)} collective-permute-done((bf16[304,128]{1,0:T(8,128)(2,1)S(1)}, bf16[304,128]{1,0:T(8,128)(2,1)S(1)}, u32[]{:S(2)}, u32[]{:S(2)}) %collective-permute-start.16) | collective-permute-done | bytes 77856 | tf_op jit(solution)/shard_map/ppermute | solution.py:373
  45.7 0.7 %collective-permute-done.17.a_ref = bf16[304,128]{1,0:T(8,128)(2,1)S(1)} collective-permute-done((bf16[304,128]{1,0:T(8,128)(2,1)S(1)}, bf16[304,128]{1,0:T(8,128)(2,1)S(1)}, u32[]{:S(2)}, u32[]{:S(2)}) %collective-permute-start.17) | collective-permute-done | bytes 77856 | tf_op jit(solution)/shard_map/ppermute | solution.py:373
  46.4 0.7 %shard_map.93 = (f32[432,128]{1,0:T(8,128)}, f32[1,128]{1,0:T(1,128)}, f32[1,128]{1,0:T(1,128)}) custom-call(f32[288,128]{1,0:T(8,128)S(1)} %get-tuple-element.130.stay1_ref, bf16[304,128]{1,0:T(8,128)(2,1)S(1)} %collective-permute-done.15.b_ref, bf16[304,128]{1,0:T(8,128)(2,1)S(1)} %collective-permute-done.16.c_ref, ...), custom_call_target="tpu_custom_call" | custom-call | bytes 714752 | tf_op jit(solution)/shard_map/pallas_call | solution.py:21
  (8 shorter events, 0.0 us)
Async XLA Ops:
  2.6 9.6 %collective-permute-start = (bf16[528,256]{1,0:T(8,128)(2,1)S(1)}, bf16[528,256]{1,0:T(8,128)(2,1)S(1)}, u32[]{:S(2)}, u32[]{:S(2)}) collective-permute-start(bf16[528,256]{1,0:T(8,128)(2,1)S(1)} %get-tuple-element.78), channel_id=1, source_target_pairs={{0,4},{4,0},{8,12},{12,8},{1,5},{5,1},{9,13},{13,9},{2,6},{6,2},{1... | collective-permute-start | bytes 811016 | tf_op jit(solution)/shard_map/ppermute | solution.py:428
  5.7 4.7 %collective-permute-start.1 = (bf16[4,64,256]{2,1,0:T(8,128)(2,1)S(1)}, bf16[4,64,256]{2,1,0:T(8,128)(2,1)S(1)}, u32[]{:S(2)}, u32[]{:S(2)}) collective-permute-start(bf16[4,64,256]{2,1,0:T(8,128)(2,1)S(1)} %get-tuple-element.79), channel_id=1, source_target_pairs={{0,1},{1,0},{2,3},{3,2},{4,5},{5,4},{6,7},{7,6},{8,9},{9,8},{10,11... | collective-permute-start | bytes 393224 | tf_op jit(solution)/shard_map/ppermute | solution.py:373
  5.7 4.7 %collective-permute-start.2 = (bf16[4,64,128]{2,1,0:T(8,128)(2,1)S(1)}, bf16[4,64,128]{2,1,0:T(8,128)(2,1)S(1)}, u32[]{:S(2)}, u32[]{:S(2)}) collective-permute-start(bf16[4,64,128]{2,1,0:T(8,128)(2,1)S(1)} %get-tuple-element.80), channel_id=1, source_target_pairs={{0,1},{1,0},{2,3},{3,2},{4,5},{5,4},{6,7},{7,6},{8,9},{9,8},{10,11... | collective-permute-start | bytes 196616 | tf_op jit(solution)/shard_map/ppermute | solution.py:373
  6.2 8.8 %collective-permute-start.4 = (bf16[2,4,64,256]{3,2,1,0:T(8,128)(2,1)S(1)}, bf16[2,4,64,256]{3,2,1,0:T(8,128)(2,1)S(1)}, u32[]{:S(2)}, u32[]{:S(2)}) collective-permute-start(bf16[2,4,64,256]{3,2,1,0:T(8,128)(2,1)S(1)} %get-tuple-element.84), channel_id=1, source_target_pairs={{4,8},{8,4},{5,9},{9,5},{6,10},{10,6},{7,11},{11,7},{20,24},{24,20... | collective-permute-start | bytes 786440 | tf_op jit(solution)/shard_map/ppermute | solution.py:429
  6.9 1.5 %copy-start = (bf16[3456,256]{1,0:T(8,128)(2,1)S(1)}, bf16[3456,256]{1,0:T(8,128)(2,1)}, u32[]{:S(2)}) copy-start(bf16[3456,256]{1,0:T(8,128)(2,1)} %w_ref.5) | copy-start | bytes 5308420
  8.4 9.0 %copy-start.2 = (f32[128]{0:T(128)S(1)}, f32[128]{0:T(128)}, u32[]{:S(2)}) copy-start(f32[128]{0:T(128)} %param.7) | copy-start | bytes 1540
  8.4 9.0 %copy-start.3 = (f32[128]{0:T(128)S(1)}, f32[128]{0:T(128)}, u32[]{:S(2)}) copy-start(f32[128]{0:T(128)} %param.6) | copy-start | bytes 1540
  10.4 11.3 %copy-start.1 = (bf16[3456,256]{1,0:T(8,128)(2,1)S(1)}, bf16[3456,256]{1,0:T(8,128)(2,1)}, u32[]{:S(2)}) copy-start(bf16[3456,256]{1,0:T(8,128)(2,1)} %w_ref.5) | copy-start | bytes 5308420
  12.2 5.1 %collective-permute-start.3 = (f32[2,8,128]{2,1,0:T(8,128)S(1)}, f32[2,8,128]{2,1,0:T(8,128)S(1)}, u32[]{:S(2)}, u32[]{:S(2)}) collective-permute-start(f32[2,8,128]{2,1,0:T(8,128)S(1)} %pad_maximum_fusion.2), channel_id=1, source_target_pairs={{0,8},{4,12},{8,0},{12,4},{1,9},{5,13},{9,1},{13,5},{2,10},{6,14},... | collective-permute-start | bytes 24584 | tf_op jit(solution)/shard_map/ppermute | solution.py:373
  15.6 1.7 %collective-permute-start.5 = (bf16[2,64,384]{2,1,0:T(8,128)(2,1)S(1)}, bf16[2,64,384]{2,1,0:T(8,128)(2,1)S(1)}, u32[]{:S(2)}, u32[]{:S(2)}) collective-permute-start(bf16[2,64,384]{2,1,0:T(8,128)(2,1)S(1)} %get-tuple-element.85), channel_id=1, source_target_pairs={{0,1},{1,0},{2,3},{3,2},{4,5},{5,4},{6,7},{7,6},{8,9},{9,8},{10,11... | collective-permute-start | bytes 294920 | tf_op jit(solution)/shard_map/ppermute | solution.py:373
  17.4 1.2 %collective-permute-start.6 = (f32[4,8,128]{2,1,0:T(8,128)S(1)}, f32[4,8,128]{2,1,0:T(8,128)S(1)}, u32[]{:S(2)}, u32[]{:S(2)}) collective-permute-start(f32[4,8,128]{2,1,0:T(8,128)S(1)} %pad_maximum_fusion.1), channel_id=1, source_target_pairs={{0,1},{1,0},{2,3},{3,2},{4,5},{5,4},{6,7},{7,6},{8,9},{9,8},{10,11... | collective-permute-start | bytes 49160 | tf_op jit(solution)/shard_map/ppermute | solution.py:373
  21.4 2.5 %collective-permute-start.7 = (bf16[3456,128]{1,0:T(8,128)(2,1)S(1)}, bf16[3456,128]{1,0:T(8,128)(2,1)S(1)}, u32[]{:S(2)}, u32[]{:S(2)}) collective-permute-start(bf16[3456,128]{1,0:T(8,128)(2,1)S(1)} %get-tuple-element.95), channel_id=1, source_target_pairs={{0,1},{1,0},{2,3},{3,2},{4,5},{5,4},{6,7},{7,6},{8,9},{9,8},{10,11... | collective-permute-start | bytes 2654216 | tf_op jit(solution)/shard_map/ppermute | solution.py:373
  23.9 1.1 %collective-permute-start.8 = (f32[2,128]{1,0:T(2,128)S(1)}, f32[2,128]{1,0:T(2,128)S(1)}, u32[]{:S(2)}, u32[]{:S(2)}) collective-permute-start(f32[2,128]{1,0:T(2,128)S(1)} %shard_map.88), channel_id=1, source_target_pairs={{0,1},{1,0},{2,3},{3,2},{4,5},{5,4},{6,7},{7,6},{8,9},{9,8},{10,11... | collective-permute-start | bytes 3080 | tf_op jit(solution)/shard_map/ppermute | solution.py:373
  25.1 12.0 %collective-permute-start.9 = (bf16[1152,128]{1,0:T(8,128)(2,1)S(1)}, bf16[1152,128]{1,0:T(8,128)(2,1)S(1)}, u32[]{:S(2)}, u32[]{:S(2)}) collective-permute-start(bf16[1152,128]{1,0:T(8,128)(2,1)S(1)} %get-tuple-element.105), channel_id=1, source_target_pairs={{0,2},{2,0},{1,3},{3,1},{4,6},{6,4},{5,7},{7,5},{8,10},{10,8},{9,1... | collective-permute-start | bytes 884744 | tf_op jit(solution)/shard_map/ppermute | solution.py:373
  26.6 9.1 %collective-permute-start.11 = (bf16[288,128]{1,0:T(8,128)(2,1)S(1)}, bf16[288,128]{1,0:T(8,128)(2,1)S(1)}, u32[]{:S(2)}, u32[]{:S(2)}) collective-permute-start(bf16[288,128]{1,0:T(8,128)(2,1)S(1)} %get-tuple-element.110), channel_id=1, source_target_pairs={{0,8},{4,12},{8,0},{12,4},{1,9},{5,13},{9,1},{13,5},{2,10},{6,14},... | collective-permute-start | bytes 221192 | tf_op jit(solution)/shard_map/ppermute | solution.py:373
  30.3 6.6 %collective-permute-start.12 = (bf16[288,128]{1,0:T(8,128)(2,1)S(1)}, bf16[288,128]{1,0:T(8,128)(2,1)S(1)}, u32[]{:S(2)}, u32[]{:S(2)}) collective-permute-start(bf16[288,128]{1,0:T(8,128)(2,1)S(1)} %get-tuple-element.111), channel_id=1, source_target_pairs={{0,12},{4,8},{8,4},{12,0},{1,13},{5,9},{9,5},{13,1},{2,14},{6,10},... | collective-permute-start | bytes 221192 | tf_op jit(solution)/shard_map/ppermute | solution.py:373
  31.4 5.7 %collective-permute-start.13 = (bf16[288,128]{1,0:T(8,128)(2,1)S(1)}, bf16[288,128]{1,0:T(8,128)(2,1)S(1)}, u32[]{:S(2)}, u32[]{:S(2)}) collective-permute-start(bf16[288,128]{1,0:T(8,128)(2,1)S(1)} %get-tuple-element.112), channel_id=1, source_target_pairs={{0,4},{4,0},{8,12},{12,8},{1,5},{5,1},{9,13},{13,9},{2,6},{6,2},{1... | collective-permute-start | bytes 221192 | tf_op jit(solution)/shard_map/ppermute | solution.py:373
  31.4 3.6 %collective-permute-start.10 = (f32[2,128]{1,0:T(2,128)S(1)}, f32[2,128]{1,0:T(2,128)S(1)}, u32[]{:S(2)}, u32[]{:S(2)}) collective-permute-start(f32[2,128]{1,0:T(2,128)S(1)} %add.17.rider_ref), channel_id=1, source_target_pairs={{0,2},{2,0},{1,3},{3,1},{4,6},{6,4},{5,7},{7,5},{8,10},{10,8},{9,1... | collective-permute-start | bytes 3080 | tf_op jit(solution)/shard_map/ppermute | solution.py:373
  37.7 7.5 %collective-permute-start.15 = (bf16[304,128]{1,0:T(8,128)(2,1)S(1)}, bf16[304,128]{1,0:T(8,128)(2,1)S(1)}, u32[]{:S(2)}, u32[]{:S(2)}) collective-permute-start(bf16[304,128]{1,0:T(8,128)(2,1)S(1)} %get-tuple-element.126), channel_id=1, source_target_pairs={{0,8},{4,12},{8,0},{12,4},{1,9},{5,13},{9,1},{13,5},{2,10},{6,14},... | collective-permute-start | bytes 233480 | tf_op jit(solution)/shard_map/ppermute | solution.py:373
  39.4 6.4 %collective-permute-start.16 = (bf16[304,128]{1,0:T(8,128)(2,1)S(1)}, bf16[304,128]{1,0:T(8,128)(2,1)S(1)}, u32[]{:S(2)}, u32[]{:S(2)}) collective-permute-start(bf16[304,128]{1,0:T(8,128)(2,1)S(1)} %get-tuple-element.127), channel_id=1, source_target_pairs={{0,12},{4,8},{8,4},{12,0},{1,13},{5,9},{9,5},{13,1},{2,14},{6,10},... | collective-permute-start | bytes 233480 | tf_op jit(solution)/shard_map/ppermute | solution.py:373
  41.0 5.4 %collective-permute-start.17 = (bf16[304,128]{1,0:T(8,128)(2,1)S(1)}, bf16[304,128]{1,0:T(8,128)(2,1)S(1)}, u32[]{:S(2)}, u32[]{:S(2)}) collective-permute-start(bf16[304,128]{1,0:T(8,128)(2,1)S(1)} %get-tuple-element.128), channel_id=1, source_target_pairs={{0,4},{4,0},{8,12},{12,8},{1,5},{5,1},{9,13},{13,9},{2,6},{6,2},{1... | collective-permute-start | bytes 233480 | tf_op jit(solution)/shard_map/ppermute | solution.py:373
  41.3 4.0 %collective-permute-start.14 = (bf16[144,128]{1,0:T(8,128)(2,1)S(1)}, bf16[144,128]{1,0:T(8,128)(2,1)S(1)}, u32[]{:S(2)}, u32[]{:S(2)}) collective-permute-start(bf16[144,128]{1,0:T(8,128)(2,1)S(1)} %get-tuple-element.124), channel_id=1, source_target_pairs={{0,2},{2,0},{1,3},{3,1},{4,6},{6,4},{5,7},{7,5},{8,10},{10,8},{9,1... | collective-permute-start | bytes 110600 | tf_op jit(solution)/shard_map/ppermute | solution.py:373

commit v8 on v7

--- a/solution.py
+++ b/solution.py
@@ -318,12 +318,12 @@
         part = rider.astype(BF16)
         rider = rider - part.astype(F32)
         parts.append(part.astype(F32))
-    parts.append(jnp.zeros((16 - 3 * rider.shape[0], rider.shape[1]), F32))
-    dst[at : at + 16] = jnp.concatenate(parts, axis=0).astype(BF16)
+    parts.append(jnp.zeros((8 - 3 * rider.shape[0], rider.shape[1]), F32))
+    dst[at : at + 8] = jnp.concatenate(parts, axis=0).astype(BF16)
 
 
 def get_rider(src, at, n):
-    rows = src[at : at + 16].astype(F32)
+    rows = src[at : at + 8].astype(F32)
     return (rows[:n] + rows[n : 2 * n]) + rows[2 * n : 3 * n]
 
 
@@ -546,7 +546,7 @@
         stay1, *send1, stay2, send2, rider = call(
             middle_kernel,
             [piece(cut, F32)]
-            + [piece(cut + 16, BF16)] * (tm - 1)
+            + [piece(cut + 8, BF16)] * (tm - 1)
             + [piece(rest, F32), piece(rest, BF16), shape(rider.shape, F32)],
             [place, stay1, recv1, stay2, *recv2, rider, got],
             scalars=1,

time: 47.3 us -> 47.2 us (level)
  no operation moved by 1% of the time
where the time goes in v8:
time: 47.2 us; the launch traced here: 47 us
  starting transfers between devices  18.5 us (39%)
  Pallas kernels  15.9 us (34%)
  waiting for transfers between devices  10.3 us (22%)
  local copies, waits for them, and re-layouts  1.49 us (3%)
  between operations  0.77 us (2%)
    pallas_call x10, Pallas kernels, call(): pl.pallas_call(kernel, out_shape=out_shape, in_specs=[SMEM] * scalars + [...  15.9 us
    ppermute x16, starting transfers between devices, swap(): lax.ppermute(value, axis, [(i, i ^ step) for i in range(lax.axis_size(axi...  14.7 us
    ppermute x16, waiting for transfers between devices, swap(): lax.ppermute(value, axis, [(i, i ^ step) for i in range(lax.axis_size(axi...  8.53 us
    ppermute x1, starting transfers between devices, body(): from_odd = lax.ppermute(to_odd, 'tm', odd_pairs)  3.09 us
    ppermute x1, waiting for transfers between devices, body(): from_odd = lax.ppermute(to_odd, 'tm', odd_pairs)  1.76 us
    unnamed x8, local copies, waits for them, and re-layouts  1.49 us
  transfers between devices with their start and end apart: 18, of which 11 were waited for; matrix products, arithmetic and copies ran while one was open for 0% of the time, Pallas kernels for 21%

profile of v8, /device:TPU:0, one launch (start us, length us, event | category | flops | bytes accessed | tf_op | source)
XLA Modules:
  0.0 47.0 jit_solution(2508553502690058351)
XLA Ops:
  0.6 0.1 pad_add_fusion.place
  0.7 1.9 %shard_map.84 = (f32[8,128]{1,0:T(8,128)S(1)}, bf16[528,256]{1,0:T(8,128)(2,1)S(1)}, bf16[2,4,64,256]{3,2,1,0:T(8,128)(2,1)S(1)}, bf16[4,64,256]{2,1,0:T(8,128)(...) custom-call(s32[3]{0:T(128)S(1)} %pad_add_fusion.place, ...), custom_call_target="tpu_custom_call" | custom-call | bytes 2306060 | tf_op jit(solution)/shard_map/pallas_call | solution.py:21
  2.6 3.1 %collective-permute-start = (bf16[528,256]{1,0:T(8,128)(2,1)S(1)}, bf16[528,256]{1,0:T(8,128)(2,1)S(1)}, u32[]{:S(2)}, u32[]{:S(2)}) collective-permute-start(bf16[528,256]{1,0:T(8,128)(2,1)S(1)} %get-tuple-element.78), channel_id=1, source_target_pairs={{0,4},{4,0},{8,12},{12,8},{1,5},{5,1},{9,13},{13,9},{2,6},{6,2},{1... | collective-permute-start | bytes 811016 | tf_op jit(solution)/shard_map/ppermute | solution.py:428
  5.7 0.0 collective-permute-start.1
  5.7 0.5 %collective-permute-start.2 = (bf16[4,64,128]{2,1,0:T(8,128)(2,1)S(1)}, bf16[4,64,128]{2,1,0:T(8,128)(2,1)S(1)}, u32[]{:S(2)}, u32[]{:S(2)}) collective-permute-start(bf16[4,64,128]{2,1,0:T(8,128)(2,1)S(1)} %get-tuple-element.80), channel_id=1, source_target_pairs={{0,1},{1,0},{2,3},{3,2},{4,5},{5,4},{6,7},{7,6},{8,9},{9,8},{10,11... | collective-permute-start | bytes 196616 | tf_op jit(solution)/shard_map/ppermute | solution.py:373
  6.2 0.7 %collective-permute-start.4 = (bf16[2,4,64,256]{3,2,1,0:T(8,128)(2,1)S(1)}, bf16[2,4,64,256]{3,2,1,0:T(8,128)(2,1)S(1)}, u32[]{:S(2)}, u32[]{:S(2)}) collective-permute-start(bf16[2,4,64,256]{3,2,1,0:T(8,128)(2,1)S(1)} %get-tuple-element.84), channel_id=1, source_target_pairs={{4,8},{8,4},{5,9},{9,5},{6,10},{10,6},{7,11},{11,7},{20,24},{24,20... | collective-permute-start | bytes 786440 | tf_op jit(solution)/shard_map/ppermute | solution.py:429
  6.9 0.0 copy-start
  6.9 1.5 %copy-done = bf16[3456,256]{1,0:T(8,128)(2,1)S(1)} copy-done((bf16[3456,256]{1,0:T(8,128)(2,1)S(1)}, bf16[3456,256]{1,0:T(8,128)(2,1)}, u32[]{:S(2)}) %copy-start) | copy-done | bytes 1769496
  8.4 0.0 copy-start.2
  8.4 0.0 copy-start.3
  8.4 2.0 %shard_map.85.own_ref = f32[4,4,64,384]{3,2,1,0:T(8,128)S(1)} custom-call(bf16[4,4,64,256]{3,2,1,0:T(8,128)(2,1)S(1)} %get-tuple-element.81.g_ref, bf16[3456,256]{1,0:T(8,128)(2,1)S(1)} %copy-done), custom_call_target="tpu_custom_call" | custom-call | bytes 3866624 | tf_op jit(solution)/shard_map/pallas_call | solution.py:21
  10.4 0.0 copy-start.1
  10.4 0.0 collective-permute-done.2.edge_ref
  10.4 0.0 collective-permute-done.1.edge_ref
  10.4 1.8 %collective-permute-done.odd_ref = bf16[528,256]{1,0:T(8,128)(2,1)S(1)} collective-permute-done((bf16[528,256]{1,0:T(8,128)(2,1)S(1)}, bf16[528,256]{1,0:T(8,128)(2,1)S(1)}, u32[]{:S(2)}, u32[]{:S(2)}) %collective-permute-start) | collective-permute-done | bytes 270368 | tf_op jit(solution)/shard_map/ppermute | solution.py:428
  12.2 2.8 %collective-permute-start.3 = (f32[2,8,128]{2,1,0:T(8,128)S(1)}, f32[2,8,128]{2,1,0:T(8,128)S(1)}, u32[]{:S(2)}, u32[]{:S(2)}) collective-permute-start(f32[2,8,128]{2,1,0:T(8,128)S(1)} %pad_maximum_fusion.2), channel_id=1, source_target_pairs={{0,8},{4,12},{8,0},{12,4},{1,9},{5,13},{9,1},{13,5},{2,10},{6,14},... | collective-permute-start | bytes 24584 | tf_op jit(solution)/shard_map/ppermute | solution.py:373
  15.0 0.0 collective-permute-done.4.even_ref
  15.0 0.6 %shard_map.86 = (bf16[2,4,64,256]{3,2,1,0:T(8,128)(2,1)S(1)}, bf16[2,4,64,128]{3,2,1,0:T(8,128)(2,1)S(1)}, bf16[2,64,384]{2,1,0:T(8,128)(2,1)S(1)}) custom-call(s32[3]{0:T(128)S(1)} %pad_add_fusion.place, bf16[528,256]{1,0:T(8,128)(2,1)S(1)} %collective-permute-done.odd_ref, bf16[2,4,64,256]{3,2,1,0:T(8,128)(2,1)S(1)} %collective-permute-done.4.even_ref), custom_call_target="tpu_custom_call" | custom-call | bytes 1024012 | tf_op jit(solution)/shard_map/pallas_call | solution.py:21
  15.6 0.1 collective-permute-start.5
  15.7 1.6 %collective-permute-done.3 = f32[2,8,128]{2,1,0:T(8,128)S(1)} collective-permute-done((f32[2,8,128]{2,1,0:T(8,128)S(1)}, f32[2,8,128]{2,1,0:T(8,128)S(1)}, u32[]{:S(2)}, u32[]{:S(2)}) %collective-permute-start.3) | collective-permute-done | bytes 8224 | tf_op jit(solution)/shard_map/ppermute | solution.py:373
  17.4 0.0 collective-permute-done.5.edge_next.prev_edge
  17.4 0.0 collective-permute-start.6
  17.4 0.0 copy-done.2
  17.4 0.0 copy-done.3
  17.4 1.1 %collective-permute-done.6 = f32[4,8,128]{2,1,0:T(8,128)S(1)} collective-permute-done((f32[4,8,128]{2,1,0:T(8,128)S(1)}, f32[4,8,128]{2,1,0:T(8,128)S(1)}, u32[]{:S(2)}, u32[]{:S(2)}) %collective-permute-start.6) | collective-permute-done | bytes 16416 | tf_op jit(solution)/shard_map/ppermute | solution.py:373
  18.6 2.9 %shard_map.87 = (f32[3456,128]{1,0:T(8,128)S(1)}, bf16[3456,128]{1,0:T(8,128)(2,1)S(1)}) custom-call(s32[3]{0:T(128)S(1)} %pad_add_fusion.place, f32[5,8,128]{2,1,0:T(8,128)S(1)} %pad_maximum_fusion.stats_ref, bf16[2,4,64,256]{3,2,1,0:T(8,128)(2,1)S(1)} %get-tuple-element.89.next_ref, bf16[4,64,256]{2,1,0:T(8,128)(2,1)S(1)} %collective-permute-done.1.edge_ref, ...), custom_call_target="tpu_custom_call" | custom-call | bytes 3952652 | tf_op jit(solution)/shard_map/pallas_call | solution.py:21
  21.4 0.2 collective-permute-start.7
  21.7 0.0 copy-done.1
  21.7 1.8 %shard_map.88 = f32[2,128]{1,0:T(2,128)S(1)} custom-call(s32[3]{0:T(128)S(1)} %pad_add_fusion.place, f32[5,8,128]{2,1,0:T(8,128)S(1)} %pad_maximum_fusion.stats_ref, bf16[4,256,128]{2,1,0:T(8,128)(2,1)S(1)} %bitcast.17, f32[4,4,64,384]{3,2,1,0:T(8,128)S(1)} %shard_map.85.own_ref, bf16[2,4,64,256]{3,2,1,0:T(8,128)(2,1)S(1)} %get-tuple-element.89.next_ref, ...), custom_call_target="tpu_custom_call" | custom-call | bytes 4117516 | tf_op jit(solution)/shard_map/pallas_call | solution.py:21
  23.5 0.4 collective-permute-done.7.recv_ref
  23.9 0.2 collective-permute-start.8
  24.1 0.7 %shard_map.89 = (f32[1152,128]{1,0:T(8,128)S(1)}, bf16[1152,128]{1,0:T(8,128)(2,1)S(1)}, f32[288,128]{1,0:T(8,128)S(1)}, bf16[288,128]{1,0:T(8,128)(2,1)S(1)}, b...) custom-call(s32[3]{0:T(128)S(1)} %pad_add_fusion.place, f32[3456,128]{1,0:T(8,128)S(1)} %get-tuple-element.93.keep_ref, ...), custom_call_target="tpu_custom_call" | custom-call | bytes 3907596 | tf_op jit(solution)/shard_map/pallas_call | solution.py:21
  24.8 0.3 collective-permute-done.8
  25.1 1.5 %collective-permute-start.9 = (bf16[1152,128]{1,0:T(8,128)(2,1)S(1)}, bf16[1152,128]{1,0:T(8,128)(2,1)S(1)}, u32[]{:S(2)}, u32[]{:S(2)}) collective-permute-start(bf16[1152,128]{1,0:T(8,128)(2,1)S(1)} %get-tuple-element.105), channel_id=1, source_target_pairs={{0,2},{2,0},{1,3},{3,1},{4,6},{6,4},{5,7},{7,5},{8,10},{10,8},{9,1... | collective-permute-start | bytes 884744 | tf_op jit(solution)/shard_map/ppermute | solution.py:373
  26.6 3.7 %collective-permute-start.11 = (bf16[288,128]{1,0:T(8,128)(2,1)S(1)}, bf16[288,128]{1,0:T(8,128)(2,1)S(1)}, u32[]{:S(2)}, u32[]{:S(2)}) collective-permute-start(bf16[288,128]{1,0:T(8,128)(2,1)S(1)} %get-tuple-element.110), channel_id=1, source_target_pairs={{0,8},{4,12},{8,0},{12,4},{1,9},{5,13},{9,1},{13,5},{2,10},{6,14},... | collective-permute-start | bytes 221192 | tf_op jit(solution)/shard_map/ppermute | solution.py:373
  30.3 1.1 %collective-permute-start.12 = (bf16[288,128]{1,0:T(8,128)(2,1)S(1)}, bf16[288,128]{1,0:T(8,128)(2,1)S(1)}, u32[]{:S(2)}, u32[]{:S(2)}) collective-permute-start(bf16[288,128]{1,0:T(8,128)(2,1)S(1)} %get-tuple-element.111), channel_id=1, source_target_pairs={{0,12},{4,8},{8,4},{12,0},{1,13},{5,9},{9,5},{13,1},{2,14},{6,10},... | collective-permute-start | bytes 221192 | tf_op jit(solution)/shard_map/ppermute | solution.py:373
  31.4 0.0 collective-permute-start.13
  31.4 0.5 %collective-permute-start.10 = (f32[2,128]{1,0:T(2,128)S(1)}, f32[2,128]{1,0:T(2,128)S(1)}, u32[]{:S(2)}, u32[]{:S(2)}) collective-permute-start(f32[2,128]{1,0:T(2,128)S(1)} %add.17.rider_ref), channel_id=1, source_target_pairs={{0,2},{2,0},{1,3},{3,1},{4,6},{6,4},{5,7},{7,5},{8,10},{10,8},{9,1... | collective-permute-start | bytes 3080 | tf_op jit(solution)/shard_map/ppermute | solution.py:373
  31.9 1.1 %shard_map.90.h_ref = bf16[6,6,64,384]{3,2,1,0:T(8,128)(2,1)S(1)} custom-call(s32[3]{0:T(128)S(1)} %pad_add_fusion.place, f32[5,8,128]{2,1,0:T(8,128)S(1)} %pad_maximum_fusion.stats_ref, bf16[4,4,64,128]{3,2,1,0:T(8,128)(2,1)S(1)} %get-tuple-element.92.x_ref, bf16[2,4,64,128]{3,2,1,0:T(8,128)(2,1)S(1)} %get-tuple-element.108.prev_ref, ...), custom_call_target="tpu_custom_call" | custom-call | bytes 2347020 | tf_op jit(solution)/shard_map/pallas_call | solution.py:21
  33.1 1.9 %collective-permute-done.10.got_ref = f32[2,128]{1,0:T(2,128)S(1)} collective-permute-done((f32[2,128]{1,0:T(2,128)S(1)}, f32[2,128]{1,0:T(2,128)S(1)}, u32[]{:S(2)}, u32[]{:S(2)}) %collective-permute-start.10) | collective-permute-done | bytes 1056 | tf_op jit(solution)/shard_map/ppermute | solution.py:373
  34.9 0.7 %collective-permute-done.11.b_ref = bf16[288,128]{1,0:T(8,128)(2,1)S(1)} collective-permute-done((bf16[288,128]{1,0:T(8,128)(2,1)S(1)}, bf16[288,128]{1,0:T(8,128)(2,1)S(1)}, u32[]{:S(2)}, u32[]{:S(2)}) %collective-permute-start.11) | collective-permute-done | bytes 73760 | tf_op jit(solution)/shard_map/ppermute | solution.py:373
  35.6 1.2 %collective-permute-done.12.c_ref = bf16[288,128]{1,0:T(8,128)(2,1)S(1)} collective-permute-done((bf16[288,128]{1,0:T(8,128)(2,1)S(1)}, bf16[288,128]{1,0:T(8,128)(2,1)S(1)}, u32[]{:S(2)}, u32[]{:S(2)}) %collective-permute-start.12) | collective-permute-done | bytes 73760 | tf_op jit(solution)/shard_map/ppermute | solution.py:373
  36.8 0.2 collective-permute-done.13.a_ref
  37.1 0.0 collective-permute-done.9.recv1_ref
  37.1 0.6 %shard_map.91 = (f32[288,128]{1,0:T(8,128)S(1)}, bf16[296,128]{1,0:T(8,128)(2,1)S(1)}, bf16[296,128]{1,0:T(8,128)(2,1)S(1)}, bf16[296,128]{1,0:T(8,128)(2,1)S(1)...) custom-call(s32[3]{0:T(128)S(1)} %pad_add_fusion.place, ...), custom_call_target="tpu_custom_call" | custom-call | bytes 1741836 | tf_op jit(solution)/shard_map/pallas_call | solution.py:21
  37.7 1.6 %collective-permute-start.15 = (bf16[296,128]{1,0:T(8,128)(2,1)S(1)}, bf16[296,128]{1,0:T(8,128)(2,1)S(1)}, u32[]{:S(2)}, u32[]{:S(2)}) collective-permute-start(bf16[296,128]{1,0:T(8,128)(2,1)S(1)} %get-tuple-element.126), channel_id=1, source_target_pairs={{0,8},{4,12},{8,0},{12,4},{1,9},{5,13},{9,1},{13,5},{2,10},{6,14},... | collective-permute-start | bytes 227336 | tf_op jit(solution)/shard_map/ppermute | solution.py:373
  39.4 1.7 %collective-permute-start.16 = (bf16[296,128]{1,0:T(8,128)(2,1)S(1)}, bf16[296,128]{1,0:T(8,128)(2,1)S(1)}, u32[]{:S(2)}, u32[]{:S(2)}) collective-permute-start(bf16[296,128]{1,0:T(8,128)(2,1)S(1)} %get-tuple-element.127), channel_id=1, source_target_pairs={{0,12},{4,8},{8,4},{12,0},{1,13},{5,9},{9,5},{13,1},{2,14},{6,10},... | collective-permute-start | bytes 227336 | tf_op jit(solution)/shard_map/ppermute | solution.py:373
  41.0 0.3 collective-permute-start.17
  41.3 0.5 %collective-permute-start.14 = (bf16[144,128]{1,0:T(8,128)(2,1)S(1)}, bf16[144,128]{1,0:T(8,128)(2,1)S(1)}, u32[]{:S(2)}, u32[]{:S(2)}) collective-permute-start(bf16[144,128]{1,0:T(8,128)(2,1)S(1)} %get-tuple-element.124), channel_id=1, source_target_pairs={{0,2},{2,0},{1,3},{3,1},{4,6},{6,4},{5,7},{7,5},{8,10},{10,8},{9,1... | collective-permute-start | bytes 110600 | tf_op jit(solution)/shard_map/ppermute | solution.py:373
  41.8 3.4 %shard_map.92 = bf16[1024,256]{1,0:T(8,128)(2,1)} custom-call(bf16[6,6,64,384]{3,2,1,0:T(8,128)(2,1)S(1)} %shard_map.90.h_ref, bf16[3456,256]{1,0:T(8,128)(2,1)S(1)} %copy-done.1), custom_call_target="tpu_custom_call" | custom-call | bytes 4063232 | tf_op jit(solution)/shard_map/pallas_call | solution.py:21
  45.2 0.0 collective-permute-done.14.recv2_ref
  45.2 0.0 collective-permute-done.15.b_ref
  45.2 0.5 collective-permute-done.16.c_ref
  45.7 0.6 %collective-permute-done.17.a_ref = bf16[296,128]{1,0:T(8,128)(2,1)S(1)} collective-permute-done((bf16[296,128]{1,0:T(8,128)(2,1)S(1)}, bf16[296,128]{1,0:T(8,128)(2,1)S(1)}, u32[]{:S(2)}, u32[]{:S(2)}) %collective-permute-start.17) | collective-permute-done | bytes 75808 | tf_op jit(solution)/shard_map/ppermute | solution.py:373
  46.3 0.7 %shard_map.93 = (f32[432,128]{1,0:T(8,128)}, f32[1,128]{1,0:T(1,128)}, f32[1,128]{1,0:T(1,128)}) custom-call(f32[288,128]{1,0:T(8,128)S(1)} %get-tuple-element.130.stay1_ref, bf16[296,128]{1,0:T(8,128)(2,1)S(1)} %collective-permute-done.15.b_ref, bf16[296,128]{1,0:T(8,128)(2,1)S(1)} %collective-permute-done.16.c_ref, ...), custom_call_target="tpu_custom_call" | custom-call | bytes 708608 | tf_op jit(solution)/shard_map/pallas_call | solution.py:21
  (8 shorter events, 0.0 us)
Async XLA Ops:
  2.6 9.6 %collective-permute-start = (bf16[528,256]{1,0:T(8,128)(2,1)S(1)}, bf16[528,256]{1,0:T(8,128)(2,1)S(1)}, u32[]{:S(2)}, u32[]{:S(2)}) collective-permute-start(bf16[528,256]{1,0:T(8,128)(2,1)S(1)} %get-tuple-element.78), channel_id=1, source_target_pairs={{0,4},{4,0},{8,12},{12,8},{1,5},{5,1},{9,13},{13,9},{2,6},{6,2},{1... | collective-permute-start | bytes 811016 | tf_op jit(solution)/shard_map/ppermute | solution.py:428
  5.7 4.7 %collective-permute-start.1 = (bf16[4,64,256]{2,1,0:T(8,128)(2,1)S(1)}, bf16[4,64,256]{2,1,0:T(8,128)(2,1)S(1)}, u32[]{:S(2)}, u32[]{:S(2)}) collective-permute-start(bf16[4,64,256]{2,1,0:T(8,128)(2,1)S(1)} %get-tuple-element.79), channel_id=1, source_target_pairs={{0,1},{1,0},{2,3},{3,2},{4,5},{5,4},{6,7},{7,6},{8,9},{9,8},{10,11... | collective-permute-start | bytes 393224 | tf_op jit(solution)/shard_map/ppermute | solution.py:373
  5.7 4.7 %collective-permute-start.2 = (bf16[4,64,128]{2,1,0:T(8,128)(2,1)S(1)}, bf16[4,64,128]{2,1,0:T(8,128)(2,1)S(1)}, u32[]{:S(2)}, u32[]{:S(2)}) collective-permute-start(bf16[4,64,128]{2,1,0:T(8,128)(2,1)S(1)} %get-tuple-element.80), channel_id=1, source_target_pairs={{0,1},{1,0},{2,3},{3,2},{4,5},{5,4},{6,7},{7,6},{8,9},{9,8},{10,11... | collective-permute-start | bytes 196616 | tf_op jit(solution)/shard_map/ppermute | solution.py:373
  6.2 8.8 %collective-permute-start.4 = (bf16[2,4,64,256]{3,2,1,0:T(8,128)(2,1)S(1)}, bf16[2,4,64,256]{3,2,1,0:T(8,128)(2,1)S(1)}, u32[]{:S(2)}, u32[]{:S(2)}) collective-permute-start(bf16[2,4,64,256]{3,2,1,0:T(8,128)(2,1)S(1)} %get-tuple-element.84), channel_id=1, source_target_pairs={{4,8},{8,4},{5,9},{9,5},{6,10},{10,6},{7,11},{11,7},{20,24},{24,20... | collective-permute-start | bytes 786440 | tf_op jit(solution)/shard_map/ppermute | solution.py:429
  6.9 1.5 %copy-start = (bf16[3456,256]{1,0:T(8,128)(2,1)S(1)}, bf16[3456,256]{1,0:T(8,128)(2,1)}, u32[]{:S(2)}) copy-start(bf16[3456,256]{1,0:T(8,128)(2,1)} %w_ref.5) | copy-start | bytes 5308420
  8.4 9.0 %copy-start.2 = (f32[128]{0:T(128)S(1)}, f32[128]{0:T(128)}, u32[]{:S(2)}) copy-start(f32[128]{0:T(128)} %param.7) | copy-start | bytes 1540
  8.4 9.0 %copy-start.3 = (f32[128]{0:T(128)S(1)}, f32[128]{0:T(128)}, u32[]{:S(2)}) copy-start(f32[128]{0:T(128)} %param.6) | copy-start | bytes 1540
  10.4 11.3 %copy-start.1 = (bf16[3456,256]{1,0:T(8,128)(2,1)S(1)}, bf16[3456,256]{1,0:T(8,128)(2,1)}, u32[]{:S(2)}) copy-start(bf16[3456,256]{1,0:T(8,128)(2,1)} %w_ref.5) | copy-start | bytes 5308420
  12.2 5.1 %collective-permute-start.3 = (f32[2,8,128]{2,1,0:T(8,128)S(1)}, f32[2,8,128]{2,1,0:T(8,128)S(1)}, u32[]{:S(2)}, u32[]{:S(2)}) collective-permute-start(f32[2,8,128]{2,1,0:T(8,128)S(1)} %pad_maximum_fusion.2), channel_id=1, source_target_pairs={{0,8},{4,12},{8,0},{12,4},{1,9},{5,13},{9,1},{13,5},{2,10},{6,14},... | collective-permute-start | bytes 24584 | tf_op jit(solution)/shard_map/ppermute | solution.py:373
  15.6 1.7 %collective-permute-start.5 = (bf16[2,64,384]{2,1,0:T(8,128)(2,1)S(1)}, bf16[2,64,384]{2,1,0:T(8,128)(2,1)S(1)}, u32[]{:S(2)}, u32[]{:S(2)}) collective-permute-start(bf16[2,64,384]{2,1,0:T(8,128)(2,1)S(1)} %get-tuple-element.85), channel_id=1, source_target_pairs={{0,1},{1,0},{2,3},{3,2},{4,5},{5,4},{6,7},{7,6},{8,9},{9,8},{10,11... | collective-permute-start | bytes 294920 | tf_op jit(solution)/shard_map/ppermute | solution.py:373
  17.4 1.2 %collective-permute-start.6 = (f32[4,8,128]{2,1,0:T(8,128)S(1)}, f32[4,8,128]{2,1,0:T(8,128)S(1)}, u32[]{:S(2)}, u32[]{:S(2)}) collective-permute-start(f32[4,8,128]{2,1,0:T(8,128)S(1)} %pad_maximum_fusion.1), channel_id=1, source_target_pairs={{0,1},{1,0},{2,3},{3,2},{4,5},{5,4},{6,7},{7,6},{8,9},{9,8},{10,11... | collective-permute-start | bytes 49160 | tf_op jit(solution)/shard_map/ppermute | solution.py:373
  21.4 2.5 %collective-permute-start.7 = (bf16[3456,128]{1,0:T(8,128)(2,1)S(1)}, bf16[3456,128]{1,0:T(8,128)(2,1)S(1)}, u32[]{:S(2)}, u32[]{:S(2)}) collective-permute-start(bf16[3456,128]{1,0:T(8,128)(2,1)S(1)} %get-tuple-element.95), channel_id=1, source_target_pairs={{0,1},{1,0},{2,3},{3,2},{4,5},{5,4},{6,7},{7,6},{8,9},{9,8},{10,11... | collective-permute-start | bytes 2654216 | tf_op jit(solution)/shard_map/ppermute | solution.py:373
  23.9 1.1 %collective-permute-start.8 = (f32[2,128]{1,0:T(2,128)S(1)}, f32[2,128]{1,0:T(2,128)S(1)}, u32[]{:S(2)}, u32[]{:S(2)}) collective-permute-start(f32[2,128]{1,0:T(2,128)S(1)} %shard_map.88), channel_id=1, source_target_pairs={{0,1},{1,0},{2,3},{3,2},{4,5},{5,4},{6,7},{7,6},{8,9},{9,8},{10,11... | collective-permute-start | bytes 3080 | tf_op jit(solution)/shard_map/ppermute | solution.py:373
  25.1 12.0 %collective-permute-start.9 = (bf16[1152,128]{1,0:T(8,128)(2,1)S(1)}, bf16[1152,128]{1,0:T(8,128)(2,1)S(1)}, u32[]{:S(2)}, u32[]{:S(2)}) collective-permute-start(bf16[1152,128]{1,0:T(8,128)(2,1)S(1)} %get-tuple-element.105), channel_id=1, source_target_pairs={{0,2},{2,0},{1,3},{3,1},{4,6},{6,4},{5,7},{7,5},{8,10},{10,8},{9,1... | collective-permute-start | bytes 884744 | tf_op jit(solution)/shard_map/ppermute | solution.py:373
  26.6 9.1 %collective-permute-start.11 = (bf16[288,128]{1,0:T(8,128)(2,1)S(1)}, bf16[288,128]{1,0:T(8,128)(2,1)S(1)}, u32[]{:S(2)}, u32[]{:S(2)}) collective-permute-start(bf16[288,128]{1,0:T(8,128)(2,1)S(1)} %get-tuple-element.110), channel_id=1, source_target_pairs={{0,8},{4,12},{8,0},{12,4},{1,9},{5,13},{9,1},{13,5},{2,10},{6,14},... | collective-permute-start | bytes 221192 | tf_op jit(solution)/shard_map/ppermute | solution.py:373
  30.3 6.6 %collective-permute-start.12 = (bf16[288,128]{1,0:T(8,128)(2,1)S(1)}, bf16[288,128]{1,0:T(8,128)(2,1)S(1)}, u32[]{:S(2)}, u32[]{:S(2)}) collective-permute-start(bf16[288,128]{1,0:T(8,128)(2,1)S(1)} %get-tuple-element.111), channel_id=1, source_target_pairs={{0,12},{4,8},{8,4},{12,0},{1,13},{5,9},{9,5},{13,1},{2,14},{6,10},... | collective-permute-start | bytes 221192 | tf_op jit(solution)/shard_map/ppermute | solution.py:373
  31.4 5.7 %collective-permute-start.13 = (bf16[288,128]{1,0:T(8,128)(2,1)S(1)}, bf16[288,128]{1,0:T(8,128)(2,1)S(1)}, u32[]{:S(2)}, u32[]{:S(2)}) collective-permute-start(bf16[288,128]{1,0:T(8,128)(2,1)S(1)} %get-tuple-element.112), channel_id=1, source_target_pairs={{0,4},{4,0},{8,12},{12,8},{1,5},{5,1},{9,13},{13,9},{2,6},{6,2},{1... | collective-permute-start | bytes 221192 | tf_op jit(solution)/shard_map/ppermute | solution.py:373
  31.4 3.6 %collective-permute-start.10 = (f32[2,128]{1,0:T(2,128)S(1)}, f32[2,128]{1,0:T(2,128)S(1)}, u32[]{:S(2)}, u32[]{:S(2)}) collective-permute-start(f32[2,128]{1,0:T(2,128)S(1)} %add.17.rider_ref), channel_id=1, source_target_pairs={{0,2},{2,0},{1,3},{3,1},{4,6},{6,4},{5,7},{7,5},{8,10},{10,8},{9,1... | collective-permute-start | bytes 3080 | tf_op jit(solution)/shard_map/ppermute | solution.py:373
  37.7 7.5 %collective-permute-start.15 = (bf16[296,128]{1,0:T(8,128)(2,1)S(1)}, bf16[296,128]{1,0:T(8,128)(2,1)S(1)}, u32[]{:S(2)}, u32[]{:S(2)}) collective-permute-start(bf16[296,128]{1,0:T(8,128)(2,1)S(1)} %get-tuple-element.126), channel_id=1, source_target_pairs={{0,8},{4,12},{8,0},{12,4},{1,9},{5,13},{9,1},{13,5},{2,10},{6,14},... | collective-permute-start | bytes 227336 | tf_op jit(solution)/shard_map/ppermute | solution.py:373
  39.4 6.3 %collective-permute-start.16 = (bf16[296,128]{1,0:T(8,128)(2,1)S(1)}, bf16[296,128]{1,0:T(8,128)(2,1)S(1)}, u32[]{:S(2)}, u32[]{:S(2)}) collective-permute-start(bf16[296,128]{1,0:T(8,128)(2,1)S(1)} %get-tuple-element.127), channel_id=1, source_target_pairs={{0,12},{4,8},{8,4},{12,0},{1,13},{5,9},{9,5},{13,1},{2,14},{6,10},... | collective-permute-start | bytes 227336 | tf_op jit(solution)/shard_map/ppermute | solution.py:373
  41.0 5.3 %collective-permute-start.17 = (bf16[296,128]{1,0:T(8,128)(2,1)S(1)}, bf16[296,128]{1,0:T(8,128)(2,1)S(1)}, u32[]{:S(2)}, u32[]{:S(2)}) collective-permute-start(bf16[296,128]{1,0:T(8,128)(2,1)S(1)} %get-tuple-element.128), channel_id=1, source_target_pairs={{0,4},{4,0},{8,12},{12,8},{1,5},{5,1},{9,13},{13,9},{2,6},{6,2},{1... | collective-permute-start | bytes 227336 | tf_op jit(solution)/shard_map/ppermute | solution.py:373
  41.3 4.0 %collective-permute-start.14 = (bf16[144,128]{1,0:T(8,128)(2,1)S(1)}, bf16[144,128]{1,0:T(8,128)(2,1)S(1)}, u32[]{:S(2)}, u32[]{:S(2)}) collective-permute-start(bf16[144,128]{1,0:T(8,128)(2,1)S(1)} %get-tuple-element.124), channel_id=1, source_target_pairs={{0,2},{2,0},{1,3},{3,1},{4,6},{6,4},{5,7},{7,5},{8,10},{10,8},{9,1... | collective-permute-start | bytes 110600 | tf_op jit(solution)/shard_map/ppermute | solution.py:373
